TPU v7x, 32 devices: a whole 2x2x4 slice. The times are simulated.
32 devices in a mesh: frames: 8 (over y, x, core), heads: 4 (over z).
Axes of the slice: x: 2, y: 2, z: 4, core: 2. Of those that a mesh axis runs over, the one named last changes fastest.
Arguments:
- frames_in: bfloat16 [64, 197, 768], P('frames', None, 'heads'), may hold values from -6 to 6
- upstream: bfloat16 [64, 197, 768], P('frames', None, 'heads'), may hold values from -6 to 6
- video_of_frame: int32 [64], replicated, may hold values from 0 to 11, never falling along the last dimension, each value on 1 to 8 neighbouring positions
- group_ids: int32 [12], replicated, may hold values from 0 to 3
- msg_fc_weight: bfloat16 [768, 768], P('heads'), may hold values from -0.21875 to 0.21875
- msg_fc_bias: bfloat16 [768], P('heads'), may hold values from -1.75 to 1.75
- msg_gain: bfloat16 [768], P('heads'), may hold values from 0.5 to 1.5
- msg_shift: bfloat16 [768], P('heads'), may hold values from -1.75 to 1.75
- msg_qkv_weight: bfloat16 [768, 3, 768], P(None, None, 'heads'), may hold values from -0.21875 to 0.21875
- msg_qv_bias: bfloat16 [2, 768], P(None, 'heads'), may hold values from -1.75 to 1.75
- courier_result_kernel: bfloat16 [768, 768], P('heads'), may hold values from -0.4375 to 0.4375
- msg_out_bias: bfloat16 [768], P('heads'), may hold values from -1.75 to 1.75
- ln1_gain: bfloat16 [768], P('heads'), may hold values from 0.5 to 1.5
- ln1_shift: bfloat16 [768], P('heads'), may hold values from -1.75 to 1.75
- qkv_weight: bfloat16 [768, 3, 768], P(None, None, 'heads'), may hold values from -0.21875 to 0.21875
- qv_bias: bfloat16 [2, 768], P(None, 'heads'), may hold values from -1.75 to 1.75
- picture_result_kernel: bfloat16 [768, 768], P('heads'), may hold values from -0.875 to 0.875
- out_bias: bfloat16 [768], P('heads'), may hold values from -1.75 to 1.75
- ln2_gain: bfloat16 [768], P('heads'), may hold values from 0.5 to 1.5
- ln2_shift: bfloat16 [768], P('heads'), may hold values from -1.75 to 1.75
- fc_weight: bfloat16 [768, 3072], P(None, 'heads'), may hold values from -0.21875 to 0.21875
- fc_bias: bfloat16 [3072], P('heads'), may hold values from -1.75 to 1.75
- proj_weight: bfloat16 [3072, 768], P('heads'), may hold values from -0.15625 to 0.15625
- proj_bias: bfloat16 [768], P('heads'), may hold values from -1.75 to 1.75
Outputs:
- output: bfloat16 [64, 197, 768], P('frames', None, 'heads')
- loss: float32 [], replicated
- grad_input: float32 [64, 197, 768], P('frames', None, 'heads')
- grad_msg_fc_weight: float32 [768, 768], P('heads')
- grad_msg_fc_bias: float32 [768], P('heads')
- grad_msg_gain: float32 [768], P('heads')
- grad_msg_shift: float32 [768], P('heads')
- grad_msg_qkv_weight: float32 [768, 3, 768], P(None, None, 'heads')
- grad_msg_qv_bias: float32 [2, 768], P(None, 'heads')
- grad_msg_out_weight: float32 [768, 768], P('heads')
- grad_msg_out_bias: float32 [768], P('heads')
- first_norm_gain_gradient: float32 [768], P('heads')
- grad_ln1_shift: float32 [768], P('heads')
- grad_qkv_weight: float32 [768, 3, 768], P(None, None, 'heads')
- grad_qv_bias: float32 [2, 768], P(None, 'heads')
- grad_out_weight: float32 [768, 768], P('heads')
- grad_out_bias: float32 [768], P('heads')
- grad_ln2_gain: float32 [768], P('heads')
- grad_ln2_shift: float32 [768], P('heads')
- grad_fc_weight: float32 [768, 3072], P(None, 'heads')
- grad_fc_bias: float32 [3072], P('heads')
- grad_proj_weight: float32 [3072, 768], P('heads')
- grad_proj_bias: float32 [768], P('heads')
Inputs may be any that keep to these rules, and one draw needn't show every extreme that they name: `video_of_frame`: video ids never fall along the frames; every video has 1 to 8 frames, and some video has exactly 8.
All inputs are finite; a program needn't handle non-finite values.
Results may differ from a plain program's by a relative error of at most 0.025.
Values may be sent and summed in bfloat16 or wider, within the bound.
No kernel may reach another device: no remote copies, remote signals or barrier semaphores. Data moves between devices by JAX's collectives and lax.ppermute only.
A program may use at most 128 MiB of HBM per device.

v0:
```python
import jax
import jax.numpy as jnp
from jax import lax
from jax.sharding import PartitionSpec as P

D = 768
HS = 64


norm_eps = 1e-05
score_scale = 0.125
gelu_rate = 1.702
contrast_sharpness = 0.02
masked_score = -1000000000.0
largest_cosine_score = lax.Precision.HIGHEST


def passed_along(value, axis, steps):
    count = lax.axis_size(axis)
    initial, last = (max(0, -steps), min(count, count - steps))
    return lax.ppermute(value, axis, [(source, source + steps) for source in range(initial, last)])


def extended(array, sides, width):
    for axis, dim in sides:
        size, length = (lax.axis_size(axis), array.shape[dim])
        up = [(i, (i + 1) % size) for i in range(size - 1)]
        down = [(j, i) for i, j in up]
        last = lax.slice_in_dim(array, length - width, length, axis=dim)
        initial = lax.slice_in_dim(array, 0, width, axis=dim)
        before = lax.ppermute(last, axis, up)
        after = lax.ppermute(initial, axis, down)
        array = jnp.concatenate([before, array, after], axis=dim)
    return array


def matrix_multiply(left, right):
    return jnp.dot(left, right, preferred_element_type=jnp.float32)


def matmul_nt(left, right):
    return lax.dot_general(
        left, right, (((1,), (1,)), ((), ())), preferred_element_type=jnp.float32
    )


def matmul_tn(left, right):
    return lax.dot_general(
        left, right, (((0,), (0,)), ((), ())), preferred_element_type=jnp.float32
    )


def gather_rows(value):
    return lax.all_gather(value, "heads", axis=1, tiled=True)


def sum_rows(partial_value):
    return lax.psum_scatter(partial_value, "heads", scatter_dimension=1, tiled=True)


def row_totals(first, second):
    return lax.psum((first, second), "heads")


def pass_back(value, offset):
    return passed_along(value, "frames", offset)


def norm_forward(rows, gain, shift):
    running_totals, squares = row_totals(jnp.sum(rows, axis=1), jnp.sum(rows * rows, axis=1))
    center = running_totals / D
    spread = squares / D - center * center
    factor = lax.rsqrt(spread + norm_eps)
    normed = (rows - center[:, None]) * factor[:, None]
    return (normed * gain + shift, normed, factor)


def norm_backward(grad_out, normed, factor, gain):
    scaled = grad_out * gain
    first, second = row_totals(jnp.sum(scaled, axis=1), jnp.sum(scaled * normed, axis=1))
    grad_in = factor[:, None] * (scaled - first[:, None] / D - normed * second[:, None] / D)
    return (grad_in, jnp.sum(grad_out * normed, axis=0), jnp.sum(grad_out, axis=0))


def contrast_loss(pooled_sum, frame_counts, group_ids):
    video_count = group_ids.shape[0]
    pooled = pooled_sum / frame_counts[:, None]
    direction_embeddings = pooled * lax.rsqrt(
        jnp.sum(pooled * pooled, axis=1, keepdims=True) + 1e-06
    )
    cosine_score_table = (
        jnp.matmul(direction_embeddings, direction_embeddings.T, precision=largest_cosine_score)
        / contrast_sharpness
    )
    video_list = jnp.arange(video_count, dtype=jnp.int32)
    itself = video_list[:, None] == video_list[None, :]
    cosine_score_table = jnp.where(itself, masked_score, cosine_score_table)
    log_total = jax.nn.logsumexp(cosine_score_table, axis=1)
    positive = jnp.logical_and(
        group_ids[:, None] == group_ids[None, :], jnp.logical_not(itself)
    ).astype(jnp.float32)
    pos_count = jnp.maximum(jnp.sum(positive, axis=1), 1.0)
    per_anchor = jnp.sum(positive * (log_total[:, None] - cosine_score_table), axis=1) / pos_count
    return jnp.sum(per_anchor)


def on_device(
    frames_in,
    upstream,
    video_of_frame,
    group_ids,
    msg_fc_weight,
    msg_fc_bias,
    msg_gain,
    msg_shift,
    msg_qkv_weight,
    msg_qv_bias,
    courier_result_kernel,
    msg_out_bias,
    ln1_gain,
    ln1_shift,
    qkv_weight,
    qv_bias,
    picture_result_kernel,
    out_bias,
    ln2_gain,
    ln2_shift,
    fc_weight,
    fc_bias,
    proj_weight,
    proj_bias,
):
    frame_count, patch_count, slice_width = frames_in.shape
    width = msg_qkv_weight.shape[0]
    head_local = slice_width // HS
    tokens = patch_count + 1
    row_count = frame_count * tokens
    mlp_count = frame_count * patch_count
    frame_index = lax.axis_index("frames")
    head_index = lax.axis_index("heads")
    f32 = jnp.float32
    bf16 = jnp.bfloat16
    cls_rows = frames_in[:, 0, :]
    msg_start = sum_rows(matrix_multiply(cls_rows, msg_fc_weight)) + msg_fc_bias.astype(f32)
    msg_ln_out, msg_normed, msg_factor = norm_forward(
        msg_start, msg_gain.astype(f32), msg_shift.astype(f32)
    )
    msg_rows = gather_rows(msg_ln_out.astype(bf16))
    msg_flat = msg_qkv_weight.reshape(width, 3 * slice_width)
    msg_bias = jnp.concatenate(
        [msg_qv_bias[0], jnp.zeros_like(msg_qv_bias[0]), msg_qv_bias[1]]
    ).astype(f32)
    msg_query = (
        matrix_multiply(msg_rows, msg_flat[:, :slice_width]) + msg_bias[:slice_width]
    ).astype(bf16)
    near_rows = extended(msg_rows, (("frames", 0),), frame_count)
    near_pairs = (
        matrix_multiply(near_rows, msg_flat[:, slice_width:]) + msg_bias[slice_width:]
    ).astype(bf16)
    near_count = 3 * frame_count
    near_keys = near_pairs[:, :slice_width].reshape(near_count, head_local, HS)
    near_values = near_pairs[:, slice_width:].reshape(near_count, head_local, HS)
    padded_ids = jnp.pad(video_of_frame, (frame_count, frame_count), constant_values=-1)
    near_ids = lax.dynamic_slice_in_dim(padded_ids, frame_index * frame_count, near_count)
    own_ids = near_ids[frame_count : 2 * frame_count]
    msg_mask = (own_ids[:, None] == near_ids[None, :])[None]
    query_heads = msg_query.reshape(frame_count, head_local, HS)
    msg_scores = (
        jnp.einsum("qhd,khd->hqk", query_heads, near_keys, preferred_element_type=f32) * score_scale
    )
    msg_scores = jnp.where(msg_mask, msg_scores, masked_score)
    msg_lse = jax.nn.logsumexp(msg_scores, axis=-1)
    msg_probs = jnp.exp(msg_scores - msg_lse[..., None]).astype(bf16)
    msg_context = jnp.einsum("hqk,khd->qhd", msg_probs, near_values, preferred_element_type=f32)
    msg_context = msg_context.astype(bf16).reshape(frame_count, slice_width)
    msg_final = (
        msg_start
        + sum_rows(matrix_multiply(msg_context, courier_result_kernel))
        + msg_out_bias.astype(f32)
    )
    stream_one = jnp.concatenate([frames_in.astype(f32), msg_final[:, None, :]], axis=1)
    flat_one = stream_one.reshape(row_count, slice_width)
    ln1_out, ln1_normed, ln1_factor = norm_forward(
        flat_one, ln1_gain.astype(f32), ln1_shift.astype(f32)
    )
    attn_rows = gather_rows(ln1_out.astype(bf16))
    qkv_flat = qkv_weight.reshape(width, 3 * slice_width)
    frame_bias = jnp.concatenate([qv_bias[0], jnp.zeros_like(qv_bias[0]), qv_bias[1]]).astype(f32)
    projected = (matrix_multiply(attn_rows, qkv_flat) + frame_bias).astype(bf16)
    split_proj = projected.reshape(frame_count, tokens, 3, head_local, HS)
    queries = split_proj[:, :, 0]
    keys_in = split_proj[:, :, 1]
    values_in = split_proj[:, :, 2]
    scores = (
        jnp.einsum("fqhd,fkhd->fhqk", queries, keys_in, preferred_element_type=f32) * score_scale
    )
    frame_lse = jax.nn.logsumexp(scores, axis=-1)
    probs_low = jnp.exp(scores - frame_lse[..., None]).astype(bf16)
    context = jnp.einsum("fhqk,fkhd->fqhd", probs_low, values_in, preferred_element_type=f32)
    context = context.astype(bf16).reshape(row_count, slice_width)
    attn_out = sum_rows(matrix_multiply(context, picture_result_kernel)) + out_bias.astype(f32)
    stream_two = (flat_one + attn_out).reshape(frame_count, tokens, slice_width)[:, :patch_count]
    flat_two = stream_two.reshape(mlp_count, slice_width)
    ln2_out, ln2_normed, ln2_factor = norm_forward(
        flat_two, ln2_gain.astype(f32), ln2_shift.astype(f32)
    )
    mlp_rows = gather_rows(ln2_out.astype(bf16))
    hidden_pre = matrix_multiply(mlp_rows, fc_weight) + fc_bias.astype(f32)
    gate = jax.nn.sigmoid(gelu_rate * hidden_pre)
    hidden = (hidden_pre * gate).astype(bf16)
    flat_three = flat_two + sum_rows(matrix_multiply(hidden, proj_weight)) + proj_bias.astype(f32)
    stream_three = flat_three.reshape(frame_count, patch_count, slice_width)
    output = stream_three.astype(bf16)
    video_count = group_ids.shape[0]
    video_list = jnp.arange(video_count, dtype=jnp.int32)
    own_onehot = (own_ids[None, :] == video_list[:, None]).astype(f32)
    frame_counts = jnp.sum((video_of_frame[None, :] == video_list[:, None]).astype(f32), axis=1)
    partial_pool = jnp.dot(own_onehot, stream_three[:, 0, :], precision=largest_cosine_score)
    placed = lax.dynamic_update_slice_in_dim(
        jnp.zeros((video_count, width), f32), partial_pool, head_index * slice_width, 1
    )
    pooled_sum = lax.psum(placed, ("frames", "heads"))

    def loss_of(total):
        return contrast_loss(total, frame_counts, group_ids)

    loss_value, loss_pull = jax.vjp(loss_of, pooled_sum)
    (pool_grad,) = loss_pull(jnp.ones((), f32))
    own_pool_grad = lax.dynamic_slice_in_dim(pool_grad, head_index * slice_width, slice_width, 1)
    cls_grad = jnp.dot(own_onehot.T, own_pool_grad, precision=largest_cosine_score)
    grad_three = upstream.astype(f32).at[:, 0, :].add(cls_grad)
    flat_grad_three = grad_three.reshape(mlp_count, slice_width)
    mlp_grad = flat_grad_three.astype(bf16)
    grad_proj_bias = jnp.sum(mlp_grad.astype(f32), axis=0)
    mlp_grad_rows = gather_rows(mlp_grad)
    grad_proj_weight = matmul_tn(hidden, mlp_grad_rows)
    hidden_grad = matmul_nt(mlp_grad_rows, proj_weight)
    pre_grad = (hidden_grad * (gate + gelu_rate * hidden_pre * gate * (1.0 - gate))).astype(bf16)
    grad_fc_bias = jnp.sum(pre_grad.astype(f32), axis=0)
    grad_fc_weight = matmul_tn(mlp_rows, pre_grad)
    ln2_back = sum_rows(matmul_nt(pre_grad, fc_weight))
    ln2_grad_in, grad_ln2_gain, grad_ln2_shift = norm_backward(
        ln2_back, ln2_normed, ln2_factor, ln2_gain.astype(f32)
    )
    grad_two = (flat_grad_three + ln2_grad_in).reshape(frame_count, patch_count, slice_width)
    message_zero = jnp.zeros((frame_count, 1, slice_width), f32)
    attn_grad = (
        jnp.concatenate([grad_two, message_zero], axis=1)
        .reshape(row_count, slice_width)
        .astype(bf16)
    )
    grad_out_bias = jnp.sum(attn_grad.astype(f32), axis=0)
    attn_grad_rows = gather_rows(attn_grad)
    grad_out_weight = matmul_tn(context, attn_grad_rows)
    context_grad = (
        matmul_nt(attn_grad_rows, picture_result_kernel)
        .astype(bf16)
        .reshape(frame_count, tokens, head_local, HS)
    )
    scores_again = (
        jnp.einsum("fqhd,fkhd->fhqk", queries, keys_in, preferred_element_type=f32) * score_scale
    )
    probs_again = jnp.exp(scores_again - frame_lse[..., None])
    probs_again_low = probs_again.astype(bf16)
    prob_grad = jnp.einsum("fqhd,fkhd->fhqk", context_grad, values_in, preferred_element_type=f32)
    score_grad = probs_again * (
        prob_grad - jnp.sum(probs_again * prob_grad, axis=-1, keepdims=True)
    )
    score_grad = score_grad.astype(bf16)
    query_grad = (
        jnp.einsum("fhqk,fkhd->fqhd", score_grad, keys_in, preferred_element_type=f32) * score_scale
    ).astype(bf16)
    key_grad = (
        jnp.einsum("fhqk,fqhd->fkhd", score_grad, queries, preferred_element_type=f32) * score_scale
    ).astype(bf16)
    value_grad = jnp.einsum(
        "fhqk,fqhd->fkhd", probs_again_low, context_grad, preferred_element_type=f32
    ).astype(bf16)
    proj_grads = jnp.stack([query_grad, key_grad, value_grad], axis=2).reshape(
        row_count, 3 * slice_width
    )
    grad_qkv_weight = matmul_tn(attn_rows, proj_grads).reshape(width, 3, slice_width)
    proj_totals = jnp.sum(proj_grads.astype(f32), axis=0).reshape(3, slice_width)
    grad_qv_bias = jnp.stack([proj_totals[0], proj_totals[2]])
    ln1_back = sum_rows(matmul_nt(proj_grads, qkv_flat))
    ln1_grad_in, first_norm_gain_gradient, grad_ln1_shift = norm_backward(
        ln1_back, ln1_normed, ln1_factor, ln1_gain.astype(f32)
    )
    grad_one = ln1_grad_in.reshape(frame_count, tokens, slice_width)
    grad_patches = grad_one[:, :patch_count] + grad_two
    grad_message = grad_one[:, patch_count]
    msg_attn_grad = grad_message.astype(bf16)
    grad_msg_out_bias = jnp.sum(msg_attn_grad.astype(f32), axis=0)
    msg_attn_rows = gather_rows(msg_attn_grad)
    grad_msg_out_weight = matmul_tn(msg_context, msg_attn_rows)
    msg_context_grad = (
        matmul_nt(msg_attn_rows, courier_result_kernel)
        .astype(bf16)
        .reshape(frame_count, head_local, HS)
    )
    msg_probs_full = jnp.exp(msg_scores - msg_lse[..., None])
    msg_prob_grad = jnp.einsum(
        "qhd,khd->hqk", msg_context_grad, near_values, preferred_element_type=f32
    )
    msg_score_grad = msg_probs_full * (
        msg_prob_grad - jnp.sum(msg_probs_full * msg_prob_grad, axis=-1, keepdims=True)
    )
    msg_score_grad = msg_score_grad.astype(bf16)
    msg_query_grad = (
        jnp.einsum("hqk,khd->qhd", msg_score_grad, near_keys, preferred_element_type=f32)
        * score_scale
    ).astype(bf16)
    near_key_grad = (
        jnp.einsum("hqk,qhd->khd", msg_score_grad, query_heads, preferred_element_type=f32)
        * score_scale
    )
    near_value_grad = jnp.einsum(
        "hqk,qhd->khd", msg_probs, msg_context_grad, preferred_element_type=f32
    )
    near_pair_grad = jnp.concatenate(
        [
            near_key_grad.reshape(near_count, slice_width),
            near_value_grad.reshape(near_count, slice_width),
        ],
        axis=1,
    )
    from_right = pass_back(near_pair_grad[:frame_count], -1)
    from_left = pass_back(near_pair_grad[2 * frame_count :], 1)
    pair_grad = (near_pair_grad[frame_count : 2 * frame_count] + from_right + from_left).astype(
        bf16
    )
    msg_proj_grads = jnp.concatenate(
        [msg_query_grad.reshape(frame_count, slice_width), pair_grad], axis=1
    )
    grad_msg_qkv_weight = matmul_tn(msg_rows, msg_proj_grads).reshape(width, 3, slice_width)
    msg_totals = jnp.sum(msg_proj_grads.astype(f32), axis=0).reshape(3, slice_width)
    grad_msg_qv_bias = jnp.stack([msg_totals[0], msg_totals[2]])
    msg_ln_back = sum_rows(matmul_nt(msg_proj_grads, msg_flat))
    msg_norm_in, grad_msg_gain, grad_msg_shift = norm_backward(
        msg_ln_back, msg_normed, msg_factor, msg_gain.astype(f32)
    )
    start_grad = (grad_message + msg_norm_in).astype(bf16)
    grad_msg_fc_bias = jnp.sum(start_grad.astype(f32), axis=0)
    leading_line_entries = gather_rows(start_grad)
    grad_msg_fc_weight = matmul_tn(cls_rows, leading_line_entries)
    cls_back = matmul_nt(leading_line_entries, msg_fc_weight)
    grad_input = grad_patches.at[:, 0, :].add(cls_back)
    (
        grad_msg_fc_weight,
        grad_msg_fc_bias,
        grad_msg_gain,
        grad_msg_shift,
        grad_msg_qkv_weight,
        grad_msg_qv_bias,
        grad_msg_out_weight,
        grad_msg_out_bias,
        first_norm_gain_gradient,
        grad_ln1_shift,
        grad_qkv_weight,
        grad_qv_bias,
        grad_out_weight,
        grad_out_bias,
        grad_ln2_gain,
        grad_ln2_shift,
        grad_fc_weight,
        grad_fc_bias,
        grad_proj_weight,
        grad_proj_bias,
    ) = lax.psum(
        (
            grad_msg_fc_weight,
            grad_msg_fc_bias,
            grad_msg_gain,
            grad_msg_shift,
            grad_msg_qkv_weight,
            grad_msg_qv_bias,
            grad_msg_out_weight,
            grad_msg_out_bias,
            first_norm_gain_gradient,
            grad_ln1_shift,
            grad_qkv_weight,
            grad_qv_bias,
            grad_out_weight,
            grad_out_bias,
            grad_ln2_gain,
            grad_ln2_shift,
            grad_fc_weight,
            grad_fc_bias,
            grad_proj_weight,
            grad_proj_bias,
        ),
        "frames",
    )
    return (
        output,
        loss_value,
        grad_input,
        grad_msg_fc_weight,
        grad_msg_fc_bias,
        grad_msg_gain,
        grad_msg_shift,
        grad_msg_qkv_weight,
        grad_msg_qv_bias,
        grad_msg_out_weight,
        grad_msg_out_bias,
        first_norm_gain_gradient,
        grad_ln1_shift,
        grad_qkv_weight,
        grad_qv_bias,
        grad_out_weight,
        grad_out_bias,
        grad_ln2_gain,
        grad_ln2_shift,
        grad_fc_weight,
        grad_fc_bias,
        grad_proj_weight,
        grad_proj_bias,
    )


def solution(mesh):
    placed = (
        P("frames", None, "heads"),
        P("frames", None, "heads"),
        P(),
        P(),
        P("heads", None),
        P("heads"),
        P("heads"),
        P("heads"),
        P(None, None, "heads"),
        P(None, "heads"),
        P("heads", None),
        P("heads"),
        P("heads"),
        P("heads"),
        P(None, None, "heads"),
        P(None, "heads"),
        P("heads", None),
        P("heads"),
        P("heads"),
        P("heads"),
        P(None, "heads"),
        P("heads"),
        P("heads", None),
        P("heads"),
    )
    return jax.shard_map(
        on_device,
        mesh=mesh,
        in_specs=placed,
        out_specs=(
            P("frames", None, "heads"),
            P(),
            P("frames", None, "heads"),
            P("heads", None),
            P("heads"),
            P("heads"),
            P("heads"),
            P(None, None, "heads"),
            P(None, "heads"),
            P("heads", None),
            P("heads"),
            P("heads"),
            P("heads"),
            P(None, None, "heads"),
            P(None, "heads"),
            P("heads", None),
            P("heads"),
            P("heads"),
            P("heads"),
            P(None, "heads"),
            P("heads"),
            P("heads", None),
            P("heads"),
        ),
        check_vma=False,
    )
```

profile of v0, /device:TPU:0, one launch (start us, length us, event | category | flops | bytes accessed | tf_op | source)
XLA Modules:
  0.0 1149.1 jit_solution(17513186176723951204)
XLA Ops:
  14.3 20.2 %reduce-scatter.22.cloned.1.call-done = f32[192,8]{1,0:T(8,128)} async-done(((f32[768,8]{1,0:T(8,128)}), f32[192,8]{1,0:T(8,128)}) %reduce-scatter.22.cloned.1.call-update) | async-done | bytes 6160
  35.6 8.5 all-reduce.9
  44.8 13.2 %all-gather = bf16[4,192,8]{1,2,0:T(8,128)(2,1)S(1)} all-gather(bf16[1,192,8]{1,2,0:T(8,128)(2,1)S(1)} %fusion.68), channel_id=1, replica_groups=mesh['frames'=8,'heads'=4] {'heads'}, dimensions={0}, use_global_device_ids=true | all-gather | bytes 15360 | tf_op jit(solution)/shard_map/all_gather | solution.py:54
  67.6 20.0 %reduce-scatter.24.cloned.1.call-done = f32[192,8]{1,0:T(8,128)} async-done(((f32[768,8]{1,0:T(8,128)}), f32[192,8]{1,0:T(8,128)}) %reduce-scatter.24.cloned.1.call-update) | async-done | bytes 6160
  98.2 15.7 %all-reduce.8 = (f32[1584]{0:T(1024)S(1)}, f32[1584]{0:T(1024)S(1)}) all-reduce(f32[1584]{0:T(1024)S(1)} %reduce_sum.355, f32[1584]{0:T(1024)S(1)} %reduce_sum.353), channel_id=1, replica_groups=mesh['frames'=8,'heads'=4] {'heads'}, use_global_device_ids=true, to_apply=%region_11.12 | all-reduce | flops 3168 | bytes 25344 | tf_op jit(solution)/shard_map/psum | solution.py:62
  115.4 52.0 %all-gather.8.cloned.1.call-done = bf16[1584,768]{0,1:T(8,128)(2,1)} async-done(((bf16[1584,192]{0,1:T(8,128)(2,1)}), bf16[1584,768]{0,1:T(8,128)(2,1)}) %all-gather.8.cloned.1.call-update) | async-done | bytes 2433040 | tf_op jit(solution)/shard_map/all_gather | solution.py:54
  167.3 4.8 add_convert_fusion
  172.1 5.8 reshape.330
  191.4 89.9 %reduce-scatter.14.cloned.1.call-done = f32[1584,192]{0,1:T(8,128)} async-done(((f32[1584,768]{0,1:T(8,128)}), f32[1584,192]{0,1:T(8,128)}) %reduce-scatter.14.cloned.1.call-update) | async-done | bytes 1216528 | tf_op jit(solution)/shard_map/reduce_scatter | solution.py:58
  292.8 18.1 %all-reduce.7 = (f32[1576]{0:T(1024)S(1)}, f32[1576]{0:T(1024)S(1)}) all-reduce(f32[1576]{0:T(1024)S(1)} %reduce_sum.360, f32[1576]{0:T(1024)S(1)} %reduce_sum.358), channel_id=1, replica_groups=mesh['frames'=8,'heads'=4] {'heads'}, use_global_device_ids=true, to_apply=%region_18.19 | all-reduce | flops 3152 | bytes 25216 | tf_op jit(solution)/shard_map/psum | solution.py:62
  313.8 51.9 %all-gather.10.cloned.1.call-done = bf16[1576,768]{0,1:T(8,128)(2,1)} async-done(((bf16[1576,192]{0,1:T(8,128)(2,1)}), bf16[1576,768]{0,1:T(8,128)(2,1)}) %all-gather.10.cloned.1.call-update) | async-done | bytes 2420752 | tf_op jit(solution)/shard_map/all_gather | solution.py:54
  365.7 6.6 multiply_convert_fusion.2
  373.7 4.7 fusion.104
  382.5 86.5 %reduce-scatter.16.cloned.1.call-done = f32[1576,192]{0,1:T(8,128)} async-done(((f32[1576,768]{0,1:T(8,128)}), f32[1576,192]{0,1:T(8,128)}) %reduce-scatter.16.cloned.1.call-update) | async-done | bytes 1210384 | tf_op jit(solution)/shard_map/reduce_scatter | solution.py:58
  477.2 41.1 %psum.237 = f32[12,768]{1,0:T(8,128)S(1)} all-reduce(f32[12,768]{1,0:T(8,128)S(1)} %dynamic_update_slice.3), channel_id=1, replica_groups=mesh['frames'=8,'heads'=4] {'frames','heads'}, use_global_device_ids=true, to_apply=%region_20.21 | all-reduce | flops 9216 | bytes 73728 | tf_op jit(solution)/shard_map/psum | solution.py:222
  529.7 53.2 %all-gather.12.cloned.1.call-done = bf16[1576,768]{0,1:T(8,128)(2,1)} async-done(((bf16[1576,192]{0,1:T(8,128)(2,1)}), bf16[1576,768]{0,1:T(8,128)(2,1)}) %all-gather.12.cloned.1.call-update) | async-done | bytes 2420752 | tf_op jit(solution)/shard_map/all_gather | solution.py:54
  582.8 7.2 convert_reduce_fusion
  591.5 4.7 fusion.105
  596.2 90.5 %reduce-scatter.18.cloned.1.call-done = f32[1576,192]{0,1:T(8,128)} async-done(((f32[1576,768]{0,1:T(8,128)}), f32[1576,192]{0,1:T(8,128)}) %reduce-scatter.18.cloned.1.call-update) | async-done | bytes 1210384 | tf_op jit(solution)/shard_map/reduce_scatter | solution.py:58
  689.0 18.0 %all-reduce.6 = (f32[1576]{0:T(1024)S(1)}, f32[1576]{0:T(1024)S(1)}) all-reduce(f32[1576]{0:T(1024)S(1)} %get-tuple-element.163, f32[1576]{0:T(1024)S(1)} %get-tuple-element.171), channel_id=1, replica_groups=mesh['frames'=8,'heads'=4] {'heads'}, use_global_device_ids=true, to_apply=%region_34.35 | all-reduce | flops 3152 | bytes 25216 | tf_op jit(solution)/shard_map/psum | solution.py:62
  718.2 51.9 %all-gather.14.cloned.1.call-done = bf16[1584,768]{0,1:T(8,128)(2,1)} async-done(((bf16[1584,192]{0,1:T(8,128)(2,1)}), bf16[1584,768]{0,1:T(8,128)(2,1)}) %all-gather.14.cloned.1.call-update) | async-done | bytes 2433040 | tf_op jit(solution)/shard_map/all_gather | solution.py:54
  787.8 5.1 reshape.339
  792.9 6.2 fusion.106
  799.4 6.4 fusion.110
  814.3 75.4 %reduce-scatter.20.cloned.1.call-done = f32[1584,192]{0,1:T(8,128)} async-done(((f32[1584,768]{0,1:T(8,128)}), f32[1584,192]{0,1:T(8,128)}) %reduce-scatter.20.cloned.1.call-update) | async-done | bytes 1216528 | tf_op jit(solution)/shard_map/reduce_scatter | solution.py:58
  891.5 18.0 %all-reduce.5 = (f32[1584]{0:T(1024)S(1)}, f32[1584]{0:T(1024)S(1)}) all-reduce(f32[1584]{0:T(1024)S(1)} %get-tuple-element.165, f32[1584]{0:T(1024)S(1)} %get-tuple-element.170), channel_id=1, replica_groups=mesh['frames'=8,'heads'=4] {'heads'}, use_global_device_ids=true, to_apply=%region_40.41 | all-reduce | flops 3168 | bytes 25344 | tf_op jit(solution)/shard_map/psum | solution.py:62
  915.4 13.3 %all-gather.1 = bf16[4,192,8]{1,2,0:T(8,128)(2,1)S(1)} all-gather(bf16[1,192,8]{1,2,0:T(8,128)(2,1)S(1)} %fusion.78), channel_id=1, replica_groups=mesh['frames'=8,'heads'=4] {'heads'}, dimensions={0}, use_global_device_ids=true | all-gather | bytes 15360 | tf_op jit(solution)/shard_map/all_gather | solution.py:54
  940.8 19.3 %reduce-scatter.26.cloned.1.call-done = f32[192,8]{1,0:T(8,128)} async-done(((f32[768,8]{1,0:T(8,128)}), f32[192,8]{1,0:T(8,128)}) %reduce-scatter.26.cloned.1.call-update) | async-done | bytes 6160
  961.3 8.5 all-reduce.4
  970.0 13.5 %all-gather.2 = bf16[4,192,8]{1,2,0:T(8,128)(2,1)S(1)} all-gather(bf16[1,192,8]{1,2,0:T(8,128)(2,1)S(1)} %bitcast.196), channel_id=1, replica_groups=mesh['frames'=8,'heads'=4] {'heads'}, dimensions={0}, use_global_device_ids=true | all-gather | bytes 15360 | tf_op jit(solution)/shard_map/all_gather | solution.py:54
  997.8 24.6 %all-reduce.2 = (f32[192]{0:T(256)}, f32[192]{0:T(256)}, f32[192]{0:T(256)}, f32[2,192]{1,0:T(2,128)}, f32[192]{0:T(256)}, /*index=5*/f32[192]{0:T(256)}, f32[19...) all-reduce(f32[192]{0:T(256)S(1)} %get-tuple-element.221, ...), channel_id=1, replica_groups=mesh['frames'=8,'heads'=4] {'frames'}, use_global_device_ids=true, to_apply=%region_49.50 | all-reduce | flops 3456 | bytes 27648 | tf_op jit(solution)/shard_map/psum | solution.py:369
  1022.4 107.3 %all-reduce.12.cloned.1.call-done = (f32[192,768]{1,0:T(8,128)}, f32[768,3,192]{0,2,1:T(8,128)}, f32[192,768]{1,0:T(8,128)}, f32[768,3,192]{0,2,1:T(8,128)}, f32...) async-done(((f32[192,768]{1,0:T(8,128)}, f32[768,3,192]{0,2,1:T(8,128)}, f32[192,768]{1,0:T(8,128)}, f32[768,3,192]{0,2,1:T(8,128)}, f32[192,768]{1,0:T(8,128)}, ...) | async-done | bytes 10027024 | tf_op jit(solution)/shard_map/psum | solution.py:369
  (398 shorter events, 171.0 us)
Async XLA Ops:
  7.2 358.5 %copy-start = (bf16[768,768]{1,0:T(8,128)(2,1)S(1)}, bf16[768,768]{1,0:T(8,128)(2,1)}, u32[]{:S(2)}) copy-start(bf16[768,768]{1,0:T(8,128)(2,1)} %param.48) | copy-start | bytes 3538948
  7.3 57.2 %copy-start.21 = (bf16[192,768]{1,0:T(8,128)(2,1)S(1)}, bf16[192,768]{1,0:T(8,128)(2,1)}, u32[]{:S(2)}) copy-start(bf16[192,768]{1,0:T(8,128)(2,1)} %param.38) | copy-start | bytes 884740
  7.3 27.3 %reduce-scatter.22.cloned.1.call-start = ((), (), s32[]{:S(2)}) async-start(), calls=%async_computation.15 | async-start | bytes 491520
  8.7 57.0 %copy-start.19 = (bf16[8,197,192]{1,2,0:T(8,128)(2,1)S(1)}, bf16[8,197,192]{1,2,0:T(8,128)(2,1)}, u32[]{:S(2)}) copy-start(bf16[8,197,192]{1,2,0:T(8,128)(2,1)} %param.28) | copy-start | bytes 1815556
  10.8 76.9 %reduce-scatter.24.cloned.1.call-start = ((), (), s32[]{:S(2)}) async-start(), calls=%async_computation.16 | async-start | bytes 491520
  58.1 4.6 collective-permute-start.1
  59.4 3.9 collective-permute-start
  65.6 101.7 %all-gather.8.cloned.1.call-start = ((), (), s32[]{:S(2)}) async-start(), calls=%async_computation.7 | async-start | bytes 3194880 | tf_op jit(solution)/shard_map/all_gather | solution.py:54
  98.1 69.2 %copy-start.71 = (f32[576]{0:T(1024)S(1)}, f32[576]{0:T(1024)}, u32[]{:S(2)}) copy-start(f32[576]{0:T(1024)} %get-tuple-element.243) | copy-start | bytes 6916
  98.2 69.2 %copy-start.79 = (bf16[768,3,192]{0,2,1:T(8,128)(2,1)S(1)}, bf16[768,3,192]{0,2,1:T(8,128)(2,1)}, u32[]{:S(2)}) copy-start(bf16[768,3,192]{0,2,1:T(8,128)(2,1)} %param.42) | copy-start | bytes 2654212
  113.9 58.2 %copy-start.33 = (f32[1584]{0:T(1024)}, f32[1584]{0:T(1024)S(1)}, u32[]{:S(2)}) copy-start(f32[1584]{0:T(1024)S(1)} %get-tuple-element.238) | copy-start | bytes 19012
  115.1 166.2 %reduce-scatter.14.cloned.1.call-start = ((), (), s32[]{:S(2)}) async-start(), calls=%async_computation.8 | async-start | bytes 6389760 | tf_op jit(solution)/shard_map/reduce_scatter | solution.py:58
  190.7 174.9 %all-gather.10.cloned.1.call-start = ((), (), s32[]{:S(2)}) async-start(), calls=%async_computation.9 | async-start | bytes 3194880 | tf_op jit(solution)/shard_map/all_gather | solution.py:54
  191.4 119.6 %copy-start.57 = (f32[192]{0:T(256)}, f32[192]{0:T(256)S(1)}, u32[]{:S(2)}) copy-start(f32[192]{0:T(256)S(1)} %convert_element_type.208) | copy-start | bytes 2308
  311.0 61.3 %copy-start.35 = (f32[1576]{0:T(1024)}, f32[1576]{0:T(1024)S(1)}, u32[]{:S(2)}) copy-start(f32[1576]{0:T(1024)S(1)} %get-tuple-element.235) | copy-start | bytes 18916
  311.0 61.3 %copy-start.37 = (f32[1576]{0:T(1024)}, f32[1576]{0:T(1024)S(1)}, u32[]{:S(2)}) copy-start(f32[1576]{0:T(1024)S(1)} %get-tuple-element.236) | copy-start | bytes 18916
  313.5 155.5 %reduce-scatter.16.cloned.1.call-start = ((), (), s32[]{:S(2)}) async-start(), calls=%async_computation.10 | async-start | bytes 6389760 | tf_op jit(solution)/shard_map/reduce_scatter | solution.py:58
  313.8 58.5 %copy-start.69 = (f32[768]{0:T(1024)}, f32[768]{0:T(1024)S(1)}, u32[]{:S(2)}) copy-start(f32[768]{0:T(1024)S(1)} %convert_element_type.211) | copy-start | bytes 9220
  378.4 204.4 %all-gather.12.cloned.1.call-start = ((), (), s32[]{:S(2)}) async-start(), calls=%async_computation.11 | async-start | bytes 3194880 | tf_op jit(solution)/shard_map/all_gather | solution.py:54
  382.5 89.4 %copy-start.89 = (f32[12]{0:T(128)}, f32[12]{0:T(128)S(1)}, u32[]{:S(2)}) copy-start(f32[12]{0:T(128)S(1)} %convert_reduce_fusion.7) | copy-start | bytes 148
  529.2 157.6 %reduce-scatter.18.cloned.1.call-start = ((), (), s32[]{:S(2)}) async-start(), calls=%async_computation.12 | async-start | bytes 6389760 | tf_op jit(solution)/shard_map/reduce_scatter | solution.py:58
  596.2 90.6 %copy-start.36 = (f32[1576]{0:T(1024)S(1)}, f32[1576]{0:T(1024)}, u32[]{:S(2)}) copy-start(f32[1576]{0:T(1024)} %copy-done.35) | copy-start | bytes 18916
  596.2 90.6 %copy-start.38 = (f32[1576]{0:T(1024)S(1)}, f32[1576]{0:T(1024)}, u32[]{:S(2)}) copy-start(f32[1576]{0:T(1024)} %copy-done.37) | copy-start | bytes 18916
  596.2 90.6 %copy-start.58 = (f32[192]{0:T(256)S(1)}, f32[192]{0:T(256)}, u32[]{:S(2)}) copy-start(f32[192]{0:T(256)} %copy-done.57) | copy-start | bytes 2308
  596.2 174.0 %all-gather.14.cloned.1.call-start = ((), (), s32[]{:S(2)}) async-start(), calls=%async_computation.13 | async-start | bytes 3194880 | tf_op jit(solution)/shard_map/all_gather | solution.py:54
  718.0 171.7 %reduce-scatter.20.cloned.1.call-start = ((), (), s32[]{:S(2)}) async-start(), calls=%async_computation.14 | async-start | bytes 6389760 | tf_op jit(solution)/shard_map/reduce_scatter | solution.py:58
  799.1 161.0 %reduce-scatter.26.cloned.1.call-start = ((), (), s32[]{:S(2)}) async-start(), calls=%async_computation.17 | async-start | bytes 491520
  811.2 78.5 %copy-start.34 = (f32[1584]{0:T(1024)S(1)}, f32[1584]{0:T(1024)}, u32[]{:S(2)}) copy-start(f32[1584]{0:T(1024)} %copy-done.33) | copy-start | bytes 19012
  811.2 78.5 %copy-start.54 = (f32[192]{0:T(256)S(1)}, f32[192]{0:T(256)}, u32[]{:S(2)}) copy-start(f32[192]{0:T(256)} %convert_element_type.199) | copy-start | bytes 2308
  931.3 4.6 collective-permute-start.2
  932.6 3.9 collective-permute-start.3
  939.0 190.7 %all-reduce.12.cloned.1.call-start = ((), (), s32[]{:S(2)}) async-start(), calls=%async_computation.18 | async-start | bytes 20054016 | tf_op jit(solution)/shard_map/psum | solution.py:369
  (81 other events, 891.1 us)
Sparse Core Ops, SparseCore 0:
  11.0 23.5 reduce-scatter.21
  65.7 21.9 reduce-scatter.23
  115.3 52.0 all-gather.7
  190.9 90.4 reduce-scatter.13
  313.6 52.0 all-gather.9
  378.5 90.4 reduce-scatter.15
  529.3 53.4 all-gather.11
  596.3 90.4 reduce-scatter.17
  718.1 52.0 all-gather.13
  799.2 90.4 reduce-scatter.19
  939.2 20.9 reduce-scatter.25
  984.8 144.8 all-reduce.11
where the time goes:
time: 1160 us; the launch traced here: 1150 us
  waiting for transfers between devices  720 us (62%)
  blocking collectives  193 us (17%)
  local copies, waits for them, and re-layouts  88.8 us (8%)
  matrix products  79.8 us (7%)
  other arithmetic  42.3 us (4%)
  between operations  15.6 us (1%)
    reduce_scatter x4, waiting for transfers between devices, sum_rows(): lax.psum_scatter(partial_value, 'heads', scatter_dimension=1, tiled=True)  342 us
    all_gather x4, waiting for transfers between devices, gather_rows(): return lax.all_gather(value, 'heads', axis=1, tiled=True)  209 us
    psum x1, waiting for transfers between devices, on_device(): lax.psum((grad_msg_fc_weight, grad_msg_fc_bias, grad_msg_gain, grad_msg_s...  107 us
    psum x6, blocking collectives, row_totals(): return lax.psum((first, second), 'heads')  87 us
    unnamed x15, waiting for transfers between devices  59.8 us
    psum x1, blocking collectives, on_device(): pooled_sum = lax.psum(placed, ('frames', 'heads'))  41.1 us
    all_gather x3, blocking collectives, gather_rows(): return lax.all_gather(value, 'heads', axis=1, tiled=True)  40 us
    unnamed x210, local copies, waits for them, and re-layouts  29.5 us
  transfers between devices with their start and end apart: 16, of which 14 were waited for; matrix products, arithmetic and copies ran while one was open for 3% of the time, Pallas kernels for 0%

commit v1 on v0

v1 whole, which is shorter than its diff:
```python
import functools

import jax
import jax.numpy as jnp
from jax import lax
from jax.experimental import pallas as pl
from jax.experimental.pallas import tpu as pltpu
from jax.sharding import PartitionSpec as P

HS = 64
GROUP = 8

norm_eps = 1e-05
score_scale = 0.125
gelu_rate = 1.702
contrast_sharpness = 0.02
masked_score = -1000000000.0
exact = lax.Precision.HIGHEST
f32 = jnp.float32
bf16 = jnp.bfloat16

PIECES = ((0, 2, 4, 6), (0, 4, 2, 6))


def nn(left, right):
    return lax.dot_general(left, right, (((1,), (0,)), ((), ())), preferred_element_type=f32)


def nt(left, right):
    return lax.dot_general(left, right, (((1,), (1,)), ((), ())), preferred_element_type=f32)


def tn(left, right):
    return lax.dot_general(left, right, (((0,), (0,)), ((), ())), preferred_element_type=f32)


def to_heads(value, step):
    count = lax.axis_size("heads")
    return lax.ppermute(value, "heads", [(i, (i + step) % count) for i in range(count)])


def swap_frames(value, bit):
    count = lax.axis_size("frames")
    return lax.ppermute(value, "frames", [(i, i ^ bit) for i in range(count)])


def frame_bits(start=1):
    count = lax.axis_size("frames")
    bits = []
    bit = start
    while bit < count:
        bits.append(bit)
        bit *= 2
    return bits


def in_order(slots, head_index):
    count = len(slots)
    return [
        lax.select_n(jnp.mod(head_index - block, count).astype(jnp.int32), *slots)
        for block in range(count)
    ]


def all_frames(value):
    for bit in frame_bits():
        value = jnp.concatenate([value, swap_frames(value, bit)], axis=0)
    return value


def norm_stats(rows):
    center = jnp.mean(rows, axis=-1, keepdims=True)
    offset = rows - center
    factor = lax.rsqrt(jnp.mean(offset * offset, axis=-1, keepdims=True) + norm_eps)
    return offset * factor, factor


def norm_back(grad_out, normed, factor, gain):
    scaled = grad_out * gain
    first = jnp.mean(scaled, axis=-1, keepdims=True)
    second = jnp.mean(scaled * normed, axis=-1, keepdims=True)
    grad_in = factor * (scaled - first - normed * second)
    return (
        grad_in,
        jnp.sum(grad_out * normed, axis=0, keepdims=True),
        jnp.sum(grad_out, axis=0, keepdims=True),
    )


def place_weight(target, own, near, far, place, slot):
    block = target.shape[0] // GROUP
    half = block // 2

    @pl.when(slot == 0)
    def _():
        target[...] = own[...]

    @pl.when(slot > 0)
    def _():
        for q in range(2):
            for j in range(4):
                here = (place ^ PIECES[q][j]) * block + q * half
                there = (place ^ PIECES[q][j] ^ 1) * block + q * half
                target[pl.ds(pl.multiple_of(here, 16), half), :] = near[q, j]
                target[pl.ds(pl.multiple_of(there, 16), half), :] = far[q, j]


def spread_grad(keep, send, value, place):
    block = value.shape[0] // GROUP
    for owner in range(GROUP):
        part = value[owner * block : (owner + 1) * block].astype(bf16)
        offset = place ^ owner
        rest = offset // 2
        mine = offset % 2 == 0

        @pl.when(mine)
        def _():
            keep[rest % 2, rest // 2] = part

        @pl.when(jnp.logical_not(mine))
        def _():
            send[rest % 2, rest // 2] = part


def attention_forward(
    scalars, x_ref, msg_ref, gain_ref, shift_ref, bias_ref, out_bias_ref, own, near, far,
    qkv_out, probs_out, ctx_out, s2_out, rows, normed, weight, total, *, patches, heads,
):
    slot = pl.program_id(0)
    place = scalars[1]
    frames, tokens, width = x_ref.shape
    local = heads * HS

    @pl.when(slot == 0)
    def _():
        token = lax.broadcasted_iota(jnp.int32, (tokens, 1), 0)
        for i in range(frames):
            value = x_ref[i].astype(f32)
            value = jnp.where(token == patches, msg_ref[i : i + 1, :], value)
            rows[pl.ds(i * tokens, tokens), :] = value
            base, _ = norm_stats(value)
            normed[pl.ds(i * tokens, tokens), :] = (
                base * gain_ref[...] + shift_ref[...]
            ).astype(bf16)
        total[...] = jnp.zeros_like(total)

    place_weight(weight, own, near, far, place, slot)
    projected = (nn(normed[...], weight[:, : 3 * local]) + bias_ref[...]).astype(bf16)
    qkv_out[...] = projected
    key_ok = lax.broadcasted_iota(jnp.int32, (tokens, tokens), 1) <= patches
    blank = jnp.zeros((tokens, width // 3 - local), bf16)
    for i in range(frames):
        block = projected[i * tokens : (i + 1) * tokens]
        pieces = [blank]
        for j in range(heads):
            q = block[:, j * HS : (j + 1) * HS]
            k = block[:, local + j * HS : local + (j + 1) * HS]
            v = block[:, 2 * local + j * HS : 2 * local + (j + 1) * HS]
            scores = jnp.where(key_ok, nt(q, k) * score_scale, masked_score)
            scores = jnp.exp(scores - jnp.max(scores, axis=-1, keepdims=True))
            probs = (scores / jnp.sum(scores, axis=-1, keepdims=True)).astype(bf16)
            probs_out[i * heads + j] = probs
            pieces.append(nn(probs, v).astype(bf16))
        context = jnp.concatenate(pieces, axis=1)
        ctx_out[pl.ds(i * tokens, tokens), :] = context
        total[pl.ds(i * tokens, tokens), :] += nt(context, weight[:, 2 * width // 3 :])

    @pl.when(slot == pl.num_programs(0) - 1)
    def _():
        s2_out[...] = rows[...] + total[...] + out_bias_ref[...]


def mlp_forward(
    scalars, s2_ref, gain_ref, shift_ref, fc_bias_ref, proj_bias_ref,
    fc_own, fc_near, fc_far, proj_own, proj_near, proj_far,
    pre_out, s3_out, cls_out, normed, fc, proj, total, *, tokens, patches,
):
    slot = pl.program_id(0)
    place = scalars[1]

    @pl.when(slot == 0)
    def _():
        base, _ = norm_stats(s2_ref[...])
        normed[...] = (base * gain_ref[...] + shift_ref[...]).astype(bf16)
        total[...] = jnp.zeros_like(total)

    place_weight(fc, fc_own, fc_near, fc_far, place, slot)
    place_weight(proj, proj_own, proj_near, proj_far, place, slot)
    pre = nn(normed[...], fc[...]) + fc_bias_ref[...]
    pre_out[...] = pre
    hidden = (pre * jax.nn.sigmoid(gelu_rate * pre)).astype(bf16)
    total[...] += nn(hidden, proj[...])

    @pl.when(slot == pl.num_programs(0) - 1)
    def _():
        final = s2_ref[...] + total[...] + proj_bias_ref[...]
        for i in range(s3_out.shape[0]):
            s3_out[i] = final[i * tokens : (i + 1) * tokens].astype(bf16)
            cls_out[i : i + 1, :] = final[i * tokens : i * tokens + 1]


def mlp_backward(
    scalars, up_ref, cls_ref, s2_ref, pre_ref, gain_ref, shift_ref,
    fc_own, fc_near, fc_far, proj_own, proj_near, proj_far,
    fc_keep, fc_send, proj_keep, proj_send, fc_bias_out, vec_out, g2_out,
    normed, grad3, fc, proj, total,
):
    slot = pl.program_id(0)
    place = scalars[1]
    frames, tokens, width = up_ref.shape

    @pl.when(slot == 0)
    def _():
        base, _ = norm_stats(s2_ref[...])
        normed[...] = (base * gain_ref[...] + shift_ref[...]).astype(bf16)
        token = lax.broadcasted_iota(jnp.int32, (tokens, 1), 0)
        for i in range(frames):
            value = up_ref[i].astype(f32)
            value = value + jnp.where(token == 0, cls_ref[i : i + 1, :], 0.0)
            grad3[pl.ds(i * tokens, tokens), :] = value
        total[...] = jnp.zeros_like(total)

    place_weight(fc, fc_own, fc_near, fc_far, place, slot)
    place_weight(proj, proj_own, proj_near, proj_far, place, slot)
    mlp_grad = grad3[...].astype(bf16)
    pre = pre_ref[...]
    gate = jax.nn.sigmoid(gelu_rate * pre)
    hidden = (pre * gate).astype(bf16)
    spread_grad(proj_keep, proj_send, tn(hidden, mlp_grad), place)
    hidden_grad = nt(mlp_grad, proj[...])
    pre_grad = (hidden_grad * (gate + gelu_rate * pre * gate * (1.0 - gate))).astype(bf16)
    fc_bias_out[...] = jnp.sum(pre_grad.astype(f32), axis=0, keepdims=True)
    spread_grad(fc_keep, fc_send, tn(normed[...], pre_grad), place)
    total[...] += nt(pre_grad, fc[...])

    @pl.when(slot == pl.num_programs(0) - 1)
    def _():
        base, factor = norm_stats(s2_ref[...])
        grad_in, gain_grad, shift_grad = norm_back(total[...], base, factor, gain_ref[...])
        g2_out[...] = grad3[...] + grad_in
        vec_out[0:1, :] = gain_grad
        vec_out[1:2, :] = shift_grad
        vec_out[2:3, :] = jnp.sum(grad3[...].astype(bf16).astype(f32), axis=0, keepdims=True)
        vec_out[3:8, :] = jnp.zeros((5, width), f32)


def attention_backward(
    scalars, g2_ref, x_ref, msg_ref, qkv_ref, probs_ref, ctx_ref, gain_ref, shift_ref,
    own, near, far,
    keep, send, bias_out, vec_out, g1_out,
    normed, grad, dproj, weight, total, *, patches, heads,
):
    slot = pl.program_id(0)
    place = scalars[1]
    frames, tokens, width = x_ref.shape
    local = heads * HS
    wide = width // 3
    token = lax.broadcasted_iota(jnp.int32, (tokens, 1), 0)

    def stream(i):
        return jnp.where(token == patches, msg_ref[i : i + 1, :], x_ref[i].astype(f32))

    @pl.when(slot == 0)
    def _():
        for i in range(frames):
            base, _ = norm_stats(stream(i))
            normed[pl.ds(i * tokens, tokens), :] = (
                base * gain_ref[...] + shift_ref[...]
            ).astype(bf16)
        grad[...] = g2_ref[...].astype(bf16)
        total[...] = jnp.zeros_like(total)

    place_weight(weight, own, near, far, place, slot)
    context_grad = nn(grad[...], weight[:, 2 * wide :]).astype(bf16)
    skip = wide - local
    for i in range(frames):
        span = slice(i * tokens, (i + 1) * tokens)
        dq, dk, dv = [], [], []
        for j in range(heads):
            q = qkv_ref[span, j * HS : (j + 1) * HS]
            k = qkv_ref[span, local + j * HS : local + (j + 1) * HS]
            v = qkv_ref[span, 2 * local + j * HS : 2 * local + (j + 1) * HS]
            cg = context_grad[span, skip + j * HS : skip + (j + 1) * HS]
            low = probs_ref[i * heads + j]
            probs = low.astype(f32)
            prob_grad = nt(cg, v)
            weighted = probs * prob_grad
            score_grad = (
                weighted - probs * jnp.sum(weighted, axis=-1, keepdims=True)
            ).astype(bf16)
            dq.append((nn(score_grad, k) * score_scale).astype(bf16))
            dk.append((tn(score_grad, q) * score_scale).astype(bf16))
            dv.append(tn(low, cg).astype(bf16))
        dproj[pl.ds(i * tokens, tokens), :] = jnp.concatenate(
            dq + dk + dv + [jnp.zeros((tokens, width - 3 * local), bf16)], axis=1
        )
    all_grads = dproj[...]
    bias_out[...] = jnp.sum(all_grads.astype(f32), axis=0, keepdims=True)
    low_part = tn(normed[...], all_grads[:, : 2 * wide])
    high_part = tn(normed[...], all_grads[:, 2 * wide :]) + tn(grad[...], ctx_ref[...])
    spread_grad(keep, send, jnp.concatenate([low_part, high_part], axis=1), place)
    total[...] += nt(all_grads[:, : 3 * local], weight[:, : 3 * local])

    @pl.when(slot == pl.num_programs(0) - 1)
    def _():
        gain_total = jnp.zeros((1, width), f32)
        shift_total = jnp.zeros((1, width), f32)
        for i in range(frames):
            span = pl.ds(i * tokens, tokens)
            base, factor = norm_stats(stream(i))
            grad_in, gain_grad, shift_grad = norm_back(
                total[span, :], base, factor, gain_ref[...]
            )
            g1_out[i] = grad_in + g2_ref[span, :]
            gain_total = gain_total + gain_grad
            shift_total = shift_total + shift_grad
        vec_out[0:1, :] = gain_total
        vec_out[1:2, :] = shift_total
        vec_out[2:3, :] = jnp.sum(grad[...].astype(f32), axis=0, keepdims=True)
        vec_out[3:8, :] = jnp.zeros((5, width), f32)


def whole(array):
    count = array.ndim
    return pl.BlockSpec(array.shape, lambda s, sc: (0,) * count)


def per_slot(array):
    count = array.ndim - 1
    return pl.BlockSpec((None,) + array.shape[1:], lambda s, sc: (s,) + (0,) * count)


def weight_specs(own, near, far, which):
    def pick(s, sc):
        return (0, 0, jnp.maximum(s - 1, 0), which, 0, 0)

    far_spec = pl.BlockSpec((2, 4, None, None) + near.shape[4:], pick)
    return [pl.BlockSpec(own.shape, lambda s, sc: (0, 0)), far_spec, far_spec]


def call(kernel, scalars, inputs, specs, outs, scratch, slots, flops):
    shapes, out_specs = zip(*outs)
    moved = sum(a.size * a.dtype.itemsize for a in inputs)
    return pl.pallas_call(
        kernel,
        grid_spec=pltpu.PrefetchScalarGridSpec(
            num_scalar_prefetch=1,
            grid=(slots,),
            in_specs=specs,
            out_specs=list(out_specs),
            scratch_shapes=scratch,
        ),
        out_shape=list(shapes),
        cost_estimate=pl.CostEstimate(flops=flops, bytes_accessed=moved, transcendentals=0),
    )(scalars, *inputs)


def shaped(shape, dtype):
    return jax.ShapeDtypeStruct(shape, dtype)


def slot_out(shape, dtype, slots):
    count = len(shape)
    return (
        shaped((slots,) + tuple(shape), dtype),
        pl.BlockSpec((None,) + tuple(shape), lambda s, sc: (s,) + (0,) * count),
    )


def full_out(shape, dtype):
    count = len(shape)
    return shaped(tuple(shape), dtype), pl.BlockSpec(tuple(shape), lambda s, sc: (0,) * count)


def gather_weights(matrices, place):
    block = matrices[0].shape[0] // GROUP
    half = block // 2
    mine = jnp.stack(
        [lax.dynamic_slice_in_dim(m, place * block, block, axis=0) for m in matrices]
    )
    count = lax.axis_size("heads")
    got = [to_heads(mine, step) for step in range(1, count)]
    first = jnp.stack([g[:, :half] for g in got])
    second = jnp.stack([g[:, half:] for g in got])
    first = jnp.stack([first, swap_frames(first, 2)])
    second = jnp.stack([second, swap_frames(second, 4)])
    first_far = swap_frames(first, 4)
    second_far = swap_frames(second, 2)
    near = jnp.stack(
        [
            jnp.concatenate([first, first_far], axis=0),
            jnp.concatenate([second, second_far], axis=0),
        ]
    )
    return near, swap_frames(near, 1)


def reduce_grads(keep, send):
    half = keep.shape[4] // 2
    got = swap_frames(send, 1)

    def summed(x, y, low):
        rows = slice(0, half) if low else slice(half, 2 * half)
        index = (slice(None), slice(None), x, y, rows)
        return keep[index].astype(f32) + got[index].astype(f32)

    both = slice(None)
    first_got = swap_frames(summed(1, both, True).astype(bf16), 2)
    second_got = swap_frames(summed(both, 1, False).astype(bf16), 4)

    def next_first(y):
        return summed(0, y, True) + first_got[:, :, y].astype(f32)

    def next_second(x):
        return summed(x, 0, False) + second_got[:, :, x].astype(f32)

    first_last = swap_frames(next_first(1).astype(bf16), 4)
    second_last = swap_frames(next_second(1).astype(bf16), 2)
    first = next_first(0) + first_last.astype(f32)
    second = next_second(0) + second_last.astype(f32)
    total = jnp.concatenate([first, second], axis=2).astype(bf16)
    for bit in frame_bits(GROUP):
        total = (total.astype(f32) + swap_frames(total, bit).astype(f32)).astype(bf16)
    own = total[0].astype(f32)
    for step in range(1, total.shape[0]):
        own = own + to_heads(total[step], -step).astype(f32)
    return own.astype(bf16)


def regather(rows, place):
    half = rows.shape[1] // 2
    first, second = rows[:, :half], rows[:, half:]
    first = jnp.stack([first, swap_frames(first, 2)])
    second = jnp.stack([second, swap_frames(second, 4)])
    first = jnp.concatenate([first, swap_frames(first, 4)], axis=0)
    second = jnp.concatenate([second, swap_frames(second, 2)], axis=0)
    second = jnp.stack([second[0], second[2], second[1], second[3]])
    near = jnp.concatenate([first, second], axis=2)
    both = jnp.stack([near, swap_frames(near, 1)], axis=1)
    both = both.reshape((GROUP,) + rows.shape)
    order = jnp.arange(GROUP) ^ place
    both = both[order]
    return jnp.moveaxis(both, 0, 1).reshape(rows.shape[0], GROUP * rows.shape[1], rows.shape[2])


def contrast_loss(pooled_sum, frame_counts, group_ids):
    video_count = group_ids.shape[0]
    pooled = pooled_sum / frame_counts[:, None]
    unit = pooled * lax.rsqrt(jnp.sum(pooled * pooled, axis=1, keepdims=True) + 1e-06)
    logits = jnp.matmul(unit, unit.T, precision=exact) / contrast_sharpness
    video_list = jnp.arange(video_count, dtype=jnp.int32)
    itself = video_list[:, None] == video_list[None, :]
    logits = jnp.where(itself, masked_score, logits)
    log_total = jax.nn.logsumexp(logits, axis=1)
    positive = jnp.logical_and(
        group_ids[:, None] == group_ids[None, :], jnp.logical_not(itself)
    ).astype(f32)
    pos_count = jnp.maximum(jnp.sum(positive, axis=1), 1.0)
    per_anchor = jnp.sum(positive * (log_total[:, None] - logits), axis=1) / pos_count
    return jnp.sum(per_anchor)


def on_device(
    frames_in,
    upstream,
    video_of_frame,
    group_ids,
    msg_fc_weight,
    msg_fc_bias,
    msg_gain,
    msg_shift,
    msg_qkv_weight,
    msg_qv_bias,
    courier_result_kernel,
    msg_out_bias,
    ln1_gain,
    ln1_shift,
    qkv_weight,
    qv_bias,
    picture_result_kernel,
    out_bias,
    ln2_gain,
    ln2_shift,
    fc_weight,
    fc_bias,
    proj_weight,
    proj_bias,
):
    block_frames, patches, local = frames_in.shape
    width = msg_qkv_weight.shape[0]
    slots = lax.axis_size("heads")
    own_frames = block_frames // slots
    heads = local // HS
    tokens = -(-(patches + 1) // 16) * 16
    rows = own_frames * tokens
    frame_index = lax.axis_index("frames")
    head_index = lax.axis_index("heads")
    place = frame_index % GROUP
    scalars = jnp.stack([head_index, place]).astype(jnp.int32)
    steps = range(1, slots)

    def frames_of(array, step):
        start = jnp.mod(head_index + step, slots) * own_frames
        return lax.dynamic_slice_in_dim(array, start, own_frames, axis=0)

    def to_rows(array):
        parts = [frames_of(array, 0)] + [to_heads(frames_of(array, s), s) for s in steps]
        value = jnp.concatenate(in_order(parts, head_index), axis=2)
        return jnp.pad(value, ((0, 0), (0, tokens - patches), (0, 0)))

    def features_of(array, step):
        start = jnp.mod(head_index + step, slots) * local
        return lax.dynamic_slice_in_dim(array, start, local, axis=array.ndim - 1)

    def to_features(array):
        parts = [features_of(array, 0)] + [to_heads(features_of(array, s), s) for s in steps]
        return jnp.concatenate(in_order(parts, head_index), axis=0)

    def heads_rows(value):
        parts = [value] + [to_heads(value, s) for s in steps]
        return jnp.concatenate(in_order(parts, head_index), axis=0)

    cls_own = frames_in[:, 0, :]
    vectors = jnp.stack(
        [
            msg_fc_bias, msg_gain, msg_shift, msg_out_bias, ln1_gain, ln1_shift,
            out_bias, ln2_gain, ln2_shift, proj_bias,
        ]
    )
    vectors = jnp.concatenate([vectors, qv_bias, fc_bias.reshape(slots, local)], axis=0)
    vectors = vectors.astype(f32)
    start_part = nn(cls_own, msg_fc_weight)
    small = jnp.concatenate([start_part, vectors.reshape(-1, width)], axis=0)
    small = [small] + [to_heads(small, s) for s in steps]
    vector_slots = [part[block_frames:].reshape(-1, local) for part in small]
    natural = jnp.concatenate(in_order([v[:10] for v in vector_slots], head_index), axis=1)
    (
        msg_fc_full, msg_gain_full, msg_shift_full, msg_out_full, ln1_gain_full, ln1_shift_full,
        out_full, ln2_gain_full, ln2_shift_full, proj_full,
    ) = [natural[i : i + 1] for i in range(10)]
    zero_bias = jnp.zeros((local,), f32)
    qkv_bias = jnp.stack(
        [jnp.concatenate([v[10], zero_bias, v[11]])[None] for v in vector_slots]
    )
    fc_bias_slots = jnp.stack([v[12:].reshape(1, -1) for v in vector_slots])
    start_block = sum(part[:block_frames] for part in small) + msg_fc_full

    x = to_rows(frames_in)

    out_turned = picture_result_kernel.T
    attn_own = jnp.concatenate([qkv_weight.reshape(width, 3 * local), out_turned], axis=1)
    attn_near, attn_far = gather_weights([attn_own], place)

    sent = jnp.concatenate(
        [start_block, cls_own.astype(f32), jnp.zeros((block_frames, 64), f32)], axis=1
    )
    sent = all_frames(sent)
    start = sent[:, :width]
    cls_all = sent[:, width : width + local].astype(bf16)
    frame_total = start.shape[0]
    places = frame_index ^ jnp.arange(lax.axis_size("frames"))
    near_ids = video_of_frame.reshape(-1, block_frames)[places].reshape(-1)
    msg_base, msg_factor = norm_stats(start)
    msg_rows = (msg_base * msg_gain_full + msg_shift_full).astype(bf16)
    msg_flat = msg_qkv_weight.reshape(width, 3 * local)
    msg_bias = jnp.concatenate([msg_qv_bias[0].astype(f32), zero_bias, msg_qv_bias[1].astype(f32)])
    msg_proj = (nn(msg_rows, msg_flat) + msg_bias).astype(bf16)
    msg_split = msg_proj.reshape(frame_total, 3, heads, HS)
    msg_q, msg_k, msg_v = msg_split[:, 0], msg_split[:, 1], msg_split[:, 2]
    same = (near_ids[:, None] == near_ids[None, :])[None]
    msg_scores = jnp.einsum("qhd,khd->hqk", msg_q, msg_k, preferred_element_type=f32) * score_scale
    msg_probs = jax.nn.softmax(jnp.where(same, msg_scores, masked_score), axis=-1)
    msg_low = msg_probs.astype(bf16)
    msg_context = jnp.einsum("hqk,khd->qhd", msg_low, msg_v, preferred_element_type=f32)
    msg_context = msg_context.astype(bf16).reshape(frame_total, local)
    msg_part = nn(msg_context[:block_frames], courier_result_kernel)
    msg_sum = frames_of(msg_part, 0) + sum(to_heads(frames_of(msg_part, s), s) for s in steps)
    message = frames_of(start_block, 0) + msg_sum + msg_out_full

    pad_tail = width // 3 - local
    outs = call(
        functools.partial(attention_forward, patches=patches, heads=heads),
        scalars,
        [x, message, ln1_gain_full, ln1_shift_full, qkv_bias, out_full, attn_own, attn_near, attn_far],
        [whole(x), whole(message), whole(ln1_gain_full), whole(ln1_shift_full), per_slot(qkv_bias),
         whole(out_full)] + weight_specs(attn_own, attn_near, attn_far, 0),
        [
            slot_out((rows, 3 * local), bf16, slots),
            slot_out((own_frames * heads, tokens, tokens), bf16, slots),
            slot_out((rows, local + pad_tail), bf16, slots),
            full_out((rows, width), f32),
        ],
        [
            pltpu.VMEM((rows, width), f32),
            pltpu.VMEM((rows, width), bf16),
            pltpu.VMEM((width, width), bf16),
            pltpu.VMEM((rows, width), f32),
        ],
        slots,
        2 * rows * width * width * slots,
    )
    qkv, probs, context, stream_two = outs

    mlp_near, mlp_far = gather_weights([fc_weight, proj_weight], place)
    up = to_rows(upstream)

    mlp_specs = weight_specs(fc_weight, mlp_near, mlp_far, 0) + weight_specs(
        proj_weight, mlp_near, mlp_far, 1
    )
    mlp_weights = [fc_weight, mlp_near, mlp_far, proj_weight, mlp_near, mlp_far]
    hidden_local = fc_weight.shape[1]
    pre, stream_three, cls_three = call(
        functools.partial(mlp_forward, tokens=tokens, patches=patches),
        scalars,
        [stream_two, ln2_gain_full, ln2_shift_full, fc_bias_slots, proj_full] + mlp_weights,
        [whole(stream_two), whole(ln2_gain_full), whole(ln2_shift_full), per_slot(fc_bias_slots),
         whole(proj_full)] + mlp_specs,
        [
            slot_out((rows, hidden_local), f32, slots),
            full_out((own_frames, tokens, width), bf16),
            full_out((own_frames, width), f32),
        ],
        [
            pltpu.VMEM((rows, width), bf16),
            pltpu.VMEM((width, hidden_local), bf16),
            pltpu.VMEM((hidden_local, width), bf16),
            pltpu.VMEM((rows, width), f32),
        ],
        slots,
        4 * rows * width * hidden_local * slots,
    )
    output = to_features(stream_three[:, :patches])

    cls_block = heads_rows(cls_three)
    cls_every = all_frames(cls_block)
    video_count = group_ids.shape[0]
    video_list = jnp.arange(video_count, dtype=jnp.int32)
    onehot = (near_ids[None, :] == video_list[:, None]).astype(f32)
    frame_counts = jnp.sum(onehot, axis=1)
    pooled_sum = jnp.dot(onehot, cls_every, precision=exact)
    loss_value, loss_pull = jax.vjp(
        lambda total: contrast_loss(total, frame_counts, group_ids), pooled_sum
    )
    (pool_grad,) = loss_pull(jnp.ones((), f32))
    own_onehot = frames_of(onehot[:, :block_frames].T, 0)
    cls_grad = jnp.dot(own_onehot, pool_grad, precision=exact)

    piece = (2, 2, width // GROUP, width)
    grads = call(
        mlp_backward,
        scalars,
        [up, cls_grad, stream_two, pre, ln2_gain_full, ln2_shift_full] + mlp_weights,
        [whole(up), whole(cls_grad), whole(stream_two), per_slot(pre), whole(ln2_gain_full),
         whole(ln2_shift_full)] + mlp_specs,
        [
            slot_out(piece, bf16, slots),
            slot_out(piece, bf16, slots),
            slot_out(piece, bf16, slots),
            slot_out(piece, bf16, slots),
            slot_out((1, hidden_local), f32, slots),
            full_out((8, width), f32),
            full_out((rows, width), f32),
        ],
        [
            pltpu.VMEM((rows, width), bf16),
            pltpu.VMEM((rows, width), f32),
            pltpu.VMEM((width, hidden_local), bf16),
            pltpu.VMEM((hidden_local, width), bf16),
            pltpu.VMEM((rows, width), f32),
        ],
        slots,
        8 * rows * width * hidden_local * slots,
    )
    fc_keep, fc_send, proj_keep, proj_send, fc_bias_grad, mlp_vec, grad_two = grads
    mlp_grads = regather(
        reduce_grads(
            jnp.stack([fc_keep, proj_keep], axis=1), jnp.stack([fc_send, proj_send], axis=1)
        ),
        place,
    )

    grads = call(
        functools.partial(attention_backward, patches=patches, heads=heads),
        scalars,
        [grad_two, x, message, qkv, probs, context, ln1_gain_full, ln1_shift_full, attn_own, attn_near,
         attn_far],
        [whole(grad_two), whole(x), whole(message), per_slot(qkv), per_slot(probs), per_slot(context),
         whole(ln1_gain_full), whole(ln1_shift_full)]
        + weight_specs(attn_own, attn_near, attn_far, 0),
        [
            slot_out(piece, bf16, slots),
            slot_out(piece, bf16, slots),
            slot_out((1, width), f32, slots),
            full_out((8, width), f32),
            full_out((own_frames, tokens, width), f32),
        ],
        [
            pltpu.VMEM((rows, width), bf16),
            pltpu.VMEM((rows, width), bf16),
            pltpu.VMEM((rows, width), bf16),
            pltpu.VMEM((width, width), bf16),
            pltpu.VMEM((rows, width), f32),
        ],
        slots,
        6 * rows * width * width * slots,
    )
    attn_keep, attn_send, proj_bias_grad, attn_vec, grad_one = grads
    attn_grads = regather(reduce_grads(attn_keep[:, None], attn_send[:, None]), place)
    grad_features = to_features(grad_one[:, :patches].astype(bf16)).astype(f32)

    grad_message = all_frames(heads_rows(grad_one[:, patches]))
    msg_attn_grad = grad_message.astype(bf16)
    msg_bias_sum = jnp.sum(msg_attn_grad.astype(f32), axis=0)
    grad_msg_out_bias = features_of(msg_bias_sum, 0)
    grad_msg_out_weight = tn(msg_context, msg_attn_grad)
    msg_context_grad = nt(msg_attn_grad, courier_result_kernel).astype(bf16)
    msg_context_grad = msg_context_grad.reshape(frame_total, heads, HS)
    msg_prob_grad = jnp.einsum("qhd,khd->hqk", msg_context_grad, msg_v, preferred_element_type=f32)
    msg_score_grad = msg_probs * (
        msg_prob_grad - jnp.sum(msg_probs * msg_prob_grad, axis=-1, keepdims=True)
    )
    msg_score_grad = msg_score_grad.astype(bf16)
    msg_dq = jnp.einsum("hqk,khd->qhd", msg_score_grad, msg_k, preferred_element_type=f32)
    msg_dk = jnp.einsum("hqk,qhd->khd", msg_score_grad, msg_q, preferred_element_type=f32)
    msg_dv = jnp.einsum("hqk,qhd->khd", msg_low, msg_context_grad, preferred_element_type=f32)
    msg_grads = jnp.stack([msg_dq * score_scale, msg_dk * score_scale, msg_dv], axis=1)
    msg_grads = msg_grads.astype(bf16).reshape(frame_total, 3 * local)
    grad_msg_qkv_weight = tn(msg_rows, msg_grads).reshape(width, 3, local)
    msg_totals = jnp.sum(msg_grads.astype(f32), axis=0).reshape(3, local)
    grad_msg_qv_bias = jnp.stack([msg_totals[0], msg_totals[2]])
    back_part = nt(msg_grads, msg_flat)
    back = back_part + sum(to_heads(back_part.astype(bf16), s).astype(f32) for s in steps)
    msg_norm_in, msg_gain_grad, msg_shift_grad = norm_back(
        back, msg_base, msg_factor, msg_gain_full
    )
    grad_msg_gain = features_of(msg_gain_grad[0], 0)
    grad_msg_shift = features_of(msg_shift_grad[0], 0)
    start_grad = (grad_message + msg_norm_in).astype(bf16)
    grad_msg_fc_bias = features_of(jnp.sum(start_grad.astype(f32), axis=0), 0)
    grad_msg_fc_weight = tn(cls_all, start_grad)
    cls_back = nt(start_grad[:block_frames], msg_fc_weight)
    grad_input = grad_features.at[:, 0, :].add(cls_back)

    feature_rows = jnp.concatenate([attn_vec[:3], mlp_vec[:3]], axis=0)
    per_head = [
        jnp.concatenate(
            [
                features_of(feature_rows, -s),
                proj_bias_grad[s, 0, :local][None],
                proj_bias_grad[s, 0, 2 * local : 3 * local][None],
                fc_bias_grad[s].reshape(slots, local),
            ],
            axis=0,
        ).reshape(-1, width)
        for s in range(slots)
    ]
    vec = per_head[0] + sum(to_heads(per_head[s], -s) for s in steps)
    for bit in frame_bits():
        vec = vec + swap_frames(vec, bit)
    vec = vec.reshape(-1, local)

    attn_final = attn_grads[0].astype(f32)
    return (
        output,
        loss_value,
        grad_input,
        grad_msg_fc_weight,
        grad_msg_fc_bias,
        grad_msg_gain,
        grad_msg_shift,
        grad_msg_qkv_weight,
        grad_msg_qv_bias,
        grad_msg_out_weight,
        grad_msg_out_bias,
        vec[0],
        vec[1],
        attn_final[:, : 3 * local].reshape(width, 3, local),
        vec[6:8],
        attn_final[:, 3 * local :].T,
        vec[2],
        vec[3],
        vec[4],
        mlp_grads[0].astype(f32),
        vec[8:].reshape(-1),
        mlp_grads[1].astype(f32),
        vec[5],
    )


def solution(mesh):
    placed = (
        P("frames", None, "heads"),
        P("frames", None, "heads"),
        P(),
        P(),
        P("heads", None),
        P("heads"),
        P("heads"),
        P("heads"),
        P(None, None, "heads"),
        P(None, "heads"),
        P("heads", None),
        P("heads"),
        P("heads"),
        P("heads"),
        P(None, None, "heads"),
        P(None, "heads"),
        P("heads", None),
        P("heads"),
        P("heads"),
        P("heads"),
        P(None, "heads"),
        P("heads"),
        P("heads", None),
        P("heads"),
    )
    return jax.shard_map(
        on_device,
        mesh=mesh,
        in_specs=placed,
        out_specs=(
            P("frames", None, "heads"),
            P(),
            P("frames", None, "heads"),
            P("heads", None),
            P("heads"),
            P("heads"),
            P("heads"),
            P(None, None, "heads"),
            P(None, "heads"),
            P("heads", None),
            P("heads"),
            P("heads"),
            P("heads"),
            P(None, None, "heads"),
            P(None, "heads"),
            P("heads", None),
            P("heads"),
            P("heads"),
            P("heads"),
            P(None, "heads"),
            P("heads"),
            P("heads", None),
            P("heads"),
        ),
        check_vma=False,
    )
```

time: 1160 us -> 501 us (0.43)
  waiting for transfers between devices: 720 us -> 134 us
  blocking collectives: 193 us -> 0 us
  starting transfers between devices: 10.3 us -> 94.2 us
  Pallas kernels: 0 us -> 83.2 us
  matrix products: 79.8 us -> 20.3 us
  other arithmetic: 42.3 us -> 69 us
  between operations: 15.6 us -> 2.28 us
    reduce_scatter x4 -> x0, waiting for transfers between devices: 342 us -> none  [sum_rows(): lax.psum_scatter(partial_value, 'heads', scatter_dimension=1, tiled=True)]
    all_gather x4 -> x0, waiting for transfers between devices: 209 us -> none  [gather_rows(): return lax.all_gather(value, 'heads', axis=1, tiled=True)]
    psum x8 -> x0, blocking collectives: 153 us -> none  [the longest x6 87 us: row_totals(): return lax.psum((first, second), 'heads')]
    ppermute x4 -> x84, waiting for transfers between devices: 1.13 us -> 134 us  [the longest x42 97.8 us: swap_frames(): return lax.ppermute(value, 'frames', [(i, i ^ bit) for i in range(count)])]
    psum x1 -> x0, waiting for transfers between devices: 107 us -> none  [on_device(): lax.psum((grad_msg_fc_weight, grad_msg_fc_bias, grad_msg_gain, grad_msg_s...]
    ppermute x4 -> x84, starting transfers between devices: 8.62 us -> 94.2 us  [the longest x42 60 us: to_heads(): lax.ppermute(value, 'heads', [(i, (i + step) % count) for i in range(coun...]
    pallas_call x0 -> x4, Pallas kernels: none -> 83.2 us  [call(): pl.pallas_call(kernel, grid_spec=pltpu.PrefetchScalarGridSpec(num_scalar_...]
    unnamed x15 -> x0, waiting for transfers between devices: 59.8 us -> none
  transfers between devices with their start and end apart: 16 -> 84, of which waited for: 14 -> 27; matrix products, arithmetic and copies ran while one was open for 3% -> 32% of each run, Pallas kernels for 0% -> 6%
where the time goes in v1:
time: 501 us; the launch traced here: 492 us
  waiting for transfers between devices  134 us (27%)
  starting transfers between devices  94.2 us (19%)
  local copies, waits for them, and re-layouts  88.8 us (18%)
  Pallas kernels  83.2 us (17%)
  other arithmetic  69 us (14%)
  matrix products  20.3 us (4%)
    ppermute x42, waiting for transfers between devices, swap_frames(): return lax.ppermute(value, 'frames', [(i, i ^ bit) for i in range(count)])  97.8 us
    pallas_call x4, Pallas kernels, call(): pl.pallas_call(kernel, grid_spec=pltpu.PrefetchScalarGridSpec(num_scalar_...  83.2 us
    ppermute x42, starting transfers between devices, to_heads(): lax.ppermute(value, 'heads', [(i, (i + step) % count) for i in range(coun...  60 us
    ppermute x42, waiting for transfers between devices, to_heads(): lax.ppermute(value, 'heads', [(i, (i + step) % count) for i in range(coun...  36.4 us
    ppermute x42, starting transfers between devices, swap_frames(): return lax.ppermute(value, 'frames', [(i, i ^ bit) for i in range(count)])  34.2 us
    unnamed x161, local copies, waits for them, and re-layouts  16.2 us
    concatenate x6, local copies, waits for them, and re-layouts, all_frames(): value = jnp.concatenate([value, swap_frames(value, bit)], axis=0)  10.3 us
  transfers between devices with their start and end apart: 84, of which 27 were waited for; matrix products, arithmetic and copies ran while one was open for 32% of the time, Pallas kernels for 6%

profile of v1, /device:TPU:0, one launch (start us, length us, event | category | flops | bytes accessed | tf_op | source)
XLA Modules:
  0.0 492.0 jit_solution(9072949909196081230)
XLA Ops:
  2.6 5.1 %collective-permute-start.22 = (bf16[2,96,768]{2,1,0:T(8,128)(2,1)}, bf16[2,96,768]{2,1,0:T(8,128)(2,1)}, u32[]{:S(2)}, u32[]{:S(2)}) collective-permute-start(bf16[2,96,768]{2,1,0:T(8,128)(2,1)} %pad_maximum_fusion.16), channel_id=1, source_target_pairs={{0,3},{1,0},{2,1},{3,2},{4,7},{5,4},{6,5},{7,6},{8,11},{9,8},{10,9... | collective-permute-start | bytes 884744 | tf_op jit(solution)/shard_map/ppermute | solution.py:39
  37.7 3.9 collective-permute-start.14
  55.6 9.5 %collective-permute-done.7 = f32[16,1024]{1,0:T(8,128)S(1)} collective-permute-done((f32[16,1024]{1,0:T(8,128)S(1)}, f32[16,1024]{1,0:T(8,128)S(1)}, u32[]{:S(2)}, u32[]{:S(2)}) %collective-permute-start.7) | collective-permute-done | bytes 65568 | tf_op jit(solution)/shard_map/ppermute | solution.py:44
  65.5 3.3 collective-permute-start
  75.7 13.9 %collective-permute-done.24 = bf16[2,3,2,48,768]{4,3,2,1,0:T(8,128)(2,1)S(1)} collective-permute-done((bf16[2,3,2,48,768]{4,3,2,1,0:T(8,128)(2,1)S(1)}, bf16[2,3,2,48,768]{4,3,2,1,0:T(8,128)(2,1)S(1)}, u32[]{:S(2)}, u32[]{:S(2)}) %collective-permute-start.24) | collective-permute-done | bytes 884768 | tf_op jit(solution)/shard_map/ppermute | solution.py:44
  98.5 3.6 collective-permute-done.17
  102.9 7.6 %collective-permute-done.16 = bf16[2,3,1,48,768]{4,3,1,2,0:T(8,128)(2,1)S(1)} collective-permute-done((bf16[2,3,1,48,768]{4,3,1,2,0:T(8,128)(2,1)S(1)}, bf16[2,3,1,48,768]{4,3,1,2,0:T(8,128)(2,1)S(1)}, u32[]{:S(2)}, u32[]{:S(2)}) %collective-permute-start.16) | collective-permute-done | bytes 442400 | tf_op jit(solution)/shard_map/ppermute | solution.py:44
  122.3 3.7 collective-permute-start.39
  126.6 16.4 %shard_map.407 = (bf16[4,416,576]{2,1,0:T(8,128)(2,1)}, bf16[4,6,208,208]{3,2,1,0:T(8,128)(2,1)}, bf16[4,416,256]{2,1,0:T(8,128)(2,1)}, f32[416,768]{1,0:T(8,128)}) custom-call(s32[2]{0:T(128)} %pad_add_fusion.scalars, bf16[2,208,768]{2,1,0:T(8,128)(2,1)} %fusion.30.x_ref, f32[2,768]{1,0:T(2,128)} %fusion.98.msg_ref, f32[1,768]{1,0:T(1,128)} %get-tuple-element.266.gain_ref, ...), custom_call_target="tpu_custom_call" | custom-call | flops 1962934272 | bytes 5382144 | tf_op jit(solution)/shard_map/pallas_call | solution.py:344
  143.0 12.0 %shard_map.408 = (f32[4,416,768]{2,1,0:T(8,128)}, bf16[2,208,768]{2,1,0:T(8,128)(2,1)}, f32[2,768]{1,0:T(2,128)}) custom-call(s32[2]{0:T(128)} %pad_add_fusion.scalars, f32[416,768]{1,0:T(8,128)} %get-tuple-element.54.s2_ref, f32[1,768]{1,0:T(1,128)} %get-tuple-element.268.gain_ref, f32[1,768]{1,0:T(1,128)} %get-tuple-element.267.shift_ref, ...), custom_call_target="tpu_custom_call" | custom-call | flops 3925868544 | bytes 17814528 | tf_op jit(solution)/shard_map/pallas_call | solution.py:344
  167.0 4.9 %collective-permute-done.37 = bf16[2,197,192]{2,1,0:T(8,128)(2,1)S(1)} collective-permute-done((bf16[2,197,192]{2,1,0:T(8,128)(2,1)S(1)}, bf16[2,197,192]{2,1,0:T(8,128)(2,1)S(1)}, u32[]{:S(2)}, u32[]{:S(2)}) %collective-permute-start.37) | collective-permute-done | bytes 151328 | tf_op jit(solution)/shard_map/ppermute | solution.py:39
  177.8 9.1 %collective-permute-done.29 = bf16[2,197,192]{2,1,0:T(8,128)(2,1)} collective-permute-done((bf16[2,197,192]{2,1,0:T(8,128)(2,1)}, bf16[2,197,192]{2,1,0:T(8,128)(2,1)}, u32[]{:S(2)}, u32[]{:S(2)}) %collective-permute-start.29) | collective-permute-done | bytes 151328 | tf_op jit(solution)/shard_map/ppermute | solution.py:39
  192.7 25.1 %shard_map.409 = (bf16[4,2,2,96,768]{4,3,2,1,0:T(8,128)(2,1)}, bf16[4,2,2,96,768]{4,3,2,1,0:T(8,128)(2,1)}, bf16[4,2,2,96,768]{4,3,2,1,0:T(8,128)(2,1)}, bf16[4,...) custom-call(s32[2]{0:T(128)} %pad_add_fusion.scalars, ...), custom_call_target="tpu_custom_call" | custom-call | flops 7851737088 | bytes 23556096 | tf_op jit(solution)/shard_map/pallas_call | solution.py:344
  217.8 29.8 %shard_map.410 = (bf16[4,2,2,96,768]{4,3,2,1,0:T(8,128)(2,1)}, bf16[4,2,2,96,768]{4,3,2,1,0:T(8,128)(2,1)}, f32[4,1,768]{2,1,0:T(1,128)}, f32[8,768]{1,0:T(8,128)}, f32[2,208,768]{2,1,0:T(8,128)}) custom-call(s32[2]{0:T(128)} %pad_add_fusion.scalars, f32[416,768]{1,0:T(8,128)} %get-tuple-element.58.g2_ref, bf16[2,208,768]{2,1,0:T(8,128)(2,1)} %fusion.30.x_ref, ...), custom_call_target="tpu_custom_call" | custom-call | flops 5888802816 | bytes 11493376 | tf_op jit(solution)/shard_map/pallas_call | solution.py:344
  255.8 4.4 collective-permute-start.52
  261.8 5.2 %pad_maximum_fusion = bf16[4,2,2,2,96,768]{5,4,3,2,0,1:T(8,128)(2,1)} fusion(bf16[4,1,2,2,96,768]{5,4,3,2,0,1:T(8,128)(2,1)} %bitcast.385, bf16[4,1,2,2,96,768]{5,4,3,2,0,1:T(8,128)(2,1)} %bitcast.384), kind=kLoop, calls=%fused_computation.12 | loop fusion | flops 2359296 | bytes 9437184 | tf_op jit(solution)/shard_map/stack | solution.py:677
  267.1 3.8 collective-permute-start.43
  273.6 5.6 %collective-permute-done.55 = f32[3,768]{1,0:T(4,128)S(1)} collective-permute-done((f32[3,768]{1,0:T(4,128)S(1)}, f32[3,768]{1,0:T(4,128)S(1)}, u32[]{:S(2)}, u32[]{:S(2)}) %collective-permute-start.55) | collective-permute-done | bytes 9248 | tf_op jit(solution)/shard_map/ppermute | solution.py:44
  291.6 3.7 collective-permute-start.42
  305.0 3.3 concatenate.173
  313.9 4.9 concatenate.174
  360.0 5.0 %collective-permute-done.61 = bf16[4,1,2,48,768]{4,3,0,2,1:T(8,128)(2,1)S(1)} collective-permute-done((bf16[4,1,2,48,768]{4,3,0,2,1:T(8,128)(2,1)S(1)}, bf16[4,1,2,48,768]{4,3,0,2,1:T(8,128)(2,1)S(1)}, u32[]{:S(2)}, u32[]{:S(2)}) %collective-permute-start.61) | collective-permute-done | bytes 589856 | tf_op jit(solution)/shard_map/ppermute | solution.py:44
  375.8 21.9 %collective-permute-done.59 = bf16[4,1,2,48,768]{4,3,0,2,1:T(8,128)(2,1)} collective-permute-done((bf16[4,1,2,48,768]{4,3,0,2,1:T(8,128)(2,1)}, bf16[4,1,2,48,768]{4,3,0,2,1:T(8,128)(2,1)}, u32[]{:S(2)}, u32[]{:S(2)}) %collective-permute-start.59) | collective-permute-done | bytes 589856 | tf_op jit(solution)/shard_map/ppermute | solution.py:44
  397.7 3.6 collective-permute-done.62
  408.4 4.6 collective-permute-done.60
  414.7 3.6 collective-permute-start.63
  418.3 3.7 collective-permute-done.73
  430.8 3.9 collective-permute-done.76
  434.6 6.0 %collective-permute-done.78 = bf16[2,96,768]{2,1,0:T(8,128)(2,1)S(1)} collective-permute-done((bf16[2,96,768]{2,1,0:T(8,128)(2,1)S(1)}, bf16[2,96,768]{2,1,0:T(8,128)(2,1)S(1)}, u32[]{:S(2)}, u32[]{:S(2)}) %collective-permute-start.78) | collective-permute-done | bytes 294944 | tf_op jit(solution)/shard_map/ppermute | solution.py:39
  440.7 10.6 %collective-permute-done.77 = bf16[2,96,768]{2,1,0:T(8,128)(2,1)S(1)} collective-permute-done((bf16[2,96,768]{2,1,0:T(8,128)(2,1)S(1)}, bf16[2,96,768]{2,1,0:T(8,128)(2,1)S(1)}, u32[]{:S(2)}, u32[]{:S(2)}) %collective-permute-start.77) | collective-permute-done | bytes 294944 | tf_op jit(solution)/shard_map/ppermute | solution.py:39
  459.4 3.1 collective-permute-done.79
  465.9 3.5 collective-permute-done.80
  (543 shorter events, 241.4 us)
Async XLA Ops:
  2.6 45.4 %collective-permute-start.22 = (bf16[2,96,768]{2,1,0:T(8,128)(2,1)}, bf16[2,96,768]{2,1,0:T(8,128)(2,1)}, u32[]{:S(2)}, u32[]{:S(2)}) collective-permute-start(bf16[2,96,768]{2,1,0:T(8,128)(2,1)} %pad_maximum_fusion.16), channel_id=1, source_target_pairs={{0,3},{1,0},{2,1},{3,2},{4,7},{5,4},{6,5},{7,6},{8,11},{9,8},{10,9... | collective-permute-start | bytes 884744 | tf_op jit(solution)/shard_map/ppermute | solution.py:39
  7.7 41.3 %collective-permute-start.21 = (bf16[2,96,768]{2,1,0:T(8,128)(2,1)}, bf16[2,96,768]{2,1,0:T(8,128)(2,1)}, u32[]{:S(2)}, u32[]{:S(2)}) collective-permute-start(bf16[2,96,768]{2,1,0:T(8,128)(2,1)} %pad_maximum_fusion.16), channel_id=1, source_target_pairs={{0,2},{1,3},{2,0},{3,1},{4,6},{5,7},{6,4},{7,5},{8,10},{9,11},{10,... | collective-permute-start | bytes 884744 | tf_op jit(solution)/shard_map/ppermute | solution.py:39
  7.7 42.3 %collective-permute-start.20 = (bf16[2,96,768]{2,1,0:T(8,128)(2,1)}, bf16[2,96,768]{2,1,0:T(8,128)(2,1)}, u32[]{:S(2)}, u32[]{:S(2)}) collective-permute-start(bf16[2,96,768]{2,1,0:T(8,128)(2,1)} %pad_maximum_fusion.16), channel_id=1, source_target_pairs={{0,1},{1,2},{2,3},{3,0},{4,5},{5,6},{6,7},{7,4},{8,9},{9,10},{10,1... | collective-permute-start | bytes 884744 | tf_op jit(solution)/shard_map/ppermute | solution.py:39
  17.9 19.0 %collective-permute-start.5 = (f32[12,768]{1,0:T(8,128)}, f32[12,768]{1,0:T(8,128)}, u32[]{:S(2)}, u32[]{:S(2)}) collective-permute-start(f32[12,768]{1,0:T(8,128)} %pad_maximum_fusion.26), channel_id=1, source_target_pairs={{0,3},{1,0},{2,1},{3,2},{4,7},{5,4},{6,5},{7,6},{8,11},{9,8},{10,9... | collective-permute-start | bytes 110600 | tf_op jit(solution)/shard_map/ppermute | solution.py:39
  20.7 17.0 %collective-permute-start.4 = (f32[12,768]{1,0:T(8,128)}, f32[12,768]{1,0:T(8,128)}, u32[]{:S(2)}, u32[]{:S(2)}) collective-permute-start(f32[12,768]{1,0:T(8,128)} %pad_maximum_fusion.26), channel_id=1, source_target_pairs={{0,2},{1,3},{2,0},{3,1},{4,6},{5,7},{6,4},{7,5},{8,10},{9,11},{10,... | collective-permute-start | bytes 110600 | tf_op jit(solution)/shard_map/ppermute | solution.py:39
  37.7 32.8 %collective-permute-start.14 = (bf16[1,96,768]{2,1,0:T(8,128)(2,1)}, bf16[1,96,768]{2,1,0:T(8,128)(2,1)S(1)}, u32[]{:S(2)}, u32[]{:S(2)}) collective-permute-start(bf16[1,96,768]{2,1,0:T(8,128)(2,1)} %fusion.64), channel_id=1, source_target_pairs={{0,3},{1,0},{2,1},{3,2},{4,7},{5,4},{6,5},{7,6},{8,11},{9,8},{10,9... | collective-permute-start | bytes 442376 | tf_op jit(solution)/shard_map/ppermute | solution.py:39
  43.3 28.8 %collective-permute-start.13 = (bf16[1,96,768]{2,1,0:T(8,128)(2,1)}, bf16[1,96,768]{2,1,0:T(8,128)(2,1)}, u32[]{:S(2)}, u32[]{:S(2)}) collective-permute-start(bf16[1,96,768]{2,1,0:T(8,128)(2,1)} %fusion.64), channel_id=1, source_target_pairs={{0,2},{1,3},{2,0},{3,1},{4,6},{5,7},{6,4},{7,5},{8,10},{9,11},{10,... | collective-permute-start | bytes 442376 | tf_op jit(solution)/shard_map/ppermute | solution.py:39
  52.7 16.1 %collective-permute-start.25 = (bf16[3,2,48,768]{3,2,1,0:T(8,128)(2,1)S(1)}, bf16[3,2,48,768]{3,2,1,0:T(8,128)(2,1)S(1)}, u32[]{:S(2)}, u32[]{:S(2)}) collective-permute-start(bf16[3,2,48,768]{3,2,1,0:T(8,128)(2,1)S(1)} %get-tuple-element.234), channel_id=1, source_target_pairs={{0,16},{4,20},{8,24},{12,28},{16,0},{20,4},{24,8},{28,12},{1,17},{... | collective-permute-start | bytes 1327112 | tf_op jit(solution)/shard_map/ppermute | solution.py:44
  65.5 29.7 %collective-permute-start = (bf16[2,197,192]{2,1,0:T(8,128)(2,1)S(1)}, bf16[2,197,192]{2,1,0:T(8,128)(2,1)S(1)}, u32[]{:S(2)}, u32[]{:S(2)}) collective-permute-start(bf16[2,197,192]{2,1,0:T(8,128)(2,1)S(1)} %copy-done.37), channel_id=1, source_target_pairs={{0,1},{1,2},{2,3},{3,0},{4,5},{5,6},{6,7},{7,4},{8,9},{9,10},{10,1... | collective-permute-start | bytes 453896 | tf_op jit(solution)/shard_map/ppermute | solution.py:39
  68.9 20.7 %collective-permute-start.24 = (bf16[2,3,2,48,768]{4,3,2,1,0:T(8,128)(2,1)S(1)}, bf16[2,3,2,48,768]{4,3,2,1,0:T(8,128)(2,1)S(1)}, u32[]{:S(2)}, u32[]{:S(2)}) collective-permute-start(bf16[2,3,2,48,768]{4,3,2,1,0:T(8,128)(2,1)S(1)} %pad_maximum_fusion.6), channel_id=1, source_target_pairs={{0,16},{4,20},{8,24},{12,28},{16,0},{20,4},{24,8},{28,12},{1,17},{... | collective-permute-start | bytes 2654216 | tf_op jit(solution)/shard_map/ppermute | solution.py:44
  70.5 20.7 %collective-permute-start.26 = (bf16[2,3,2,48,768]{4,3,2,1,0:T(8,128)(2,1)S(1)}, bf16[2,3,2,48,768]{4,3,2,1,0:T(8,128)(2,1)S(1)}, u32[]{:S(2)}, u32[]{:S(2)}) collective-permute-start(bf16[2,3,2,48,768]{4,3,2,1,0:T(8,128)(2,1)S(1)} %pad_maximum_fusion.7), channel_id=1, source_target_pairs={{0,8},{4,12},{8,0},{12,4},{16,24},{20,28},{24,16},{28,20},{1,9},{5... | collective-permute-start | bytes 2654216 | tf_op jit(solution)/shard_map/ppermute | solution.py:44
  72.1 23.5 %collective-permute-start.1 = (bf16[2,197,192]{2,1,0:T(8,128)(2,1)S(1)}, bf16[2,197,192]{2,1,0:T(8,128)(2,1)S(1)}, u32[]{:S(2)}, u32[]{:S(2)}) collective-permute-start(bf16[2,197,192]{2,1,0:T(8,128)(2,1)S(1)} %copy-done.36), channel_id=1, source_target_pairs={{0,2},{1,3},{2,0},{3,1},{4,6},{5,7},{6,4},{7,5},{8,10},{9,11},{10,... | collective-permute-start | bytes 453896 | tf_op jit(solution)/shard_map/ppermute | solution.py:39
  74.1 21.6 %collective-permute-start.2 = (bf16[2,197,192]{2,1,0:T(8,128)(2,1)S(1)}, bf16[2,197,192]{2,1,0:T(8,128)(2,1)S(1)}, u32[]{:S(2)}, u32[]{:S(2)}) collective-permute-start(bf16[2,197,192]{2,1,0:T(8,128)(2,1)S(1)} %copy-done.35), channel_id=1, source_target_pairs={{0,3},{1,0},{2,1},{3,2},{4,7},{5,4},{6,5},{7,6},{8,11},{9,8},{10,9... | collective-permute-start | bytes 453896 | tf_op jit(solution)/shard_map/ppermute | solution.py:39
  95.7 47.3 %collective-permute-start.27 = (bf16[2,4,3,2,48,768]{5,4,3,2,1,0:T(8,128)(2,1)}, bf16[2,4,3,2,48,768]{5,4,3,2,1,0:T(8,128)(2,1)}, u32[]{:S(2)}, u32[]{:S(2)}) collective-permute-start(bf16[2,4,3,2,48,768]{5,4,3,2,1,0:T(8,128)(2,1)} %pad_maximum_fusion.1.fc_near.proj_near), channel_id=1, source_target_pairs={{0,4},{4,0},{8,12},{12,8},{16,20},{20,16},{24,28},{28,24},{1,5},{5... | collective-permute-start | bytes 10616840 | tf_op jit(solution)/shard_map/ppermute | solution.py:44
  122.3 44.1 %collective-permute-start.39 = (bf16[2,197,192]{2,1,0:T(8,128)(2,1)}, bf16[2,197,192]{2,1,0:T(8,128)(2,1)S(1)}, u32[]{:S(2)}, u32[]{:S(2)}) collective-permute-start(bf16[2,197,192]{2,1,0:T(8,128)(2,1)} %copy.285), channel_id=1, source_target_pairs={{0,3},{1,0},{2,1},{3,2},{4,7},{5,4},{6,5},{7,6},{8,11},{9,8},{10,9... | collective-permute-start | bytes 453896 | tf_op jit(solution)/shard_map/ppermute | solution.py:39
  126.0 41.0 %collective-permute-start.38 = (bf16[2,197,192]{2,1,0:T(8,128)(2,1)}, bf16[2,197,192]{2,1,0:T(8,128)(2,1)}, u32[]{:S(2)}, u32[]{:S(2)}) collective-permute-start(bf16[2,197,192]{2,1,0:T(8,128)(2,1)} %copy.284), channel_id=1, source_target_pairs={{0,2},{1,3},{2,0},{3,1},{4,6},{5,7},{6,4},{7,5},{8,10},{9,11},{10,... | collective-permute-start | bytes 453896 | tf_op jit(solution)/shard_map/ppermute | solution.py:39
  166.4 20.5 %collective-permute-start.29 = (bf16[2,197,192]{2,1,0:T(8,128)(2,1)}, bf16[2,197,192]{2,1,0:T(8,128)(2,1)}, u32[]{:S(2)}, u32[]{:S(2)}) collective-permute-start(bf16[2,197,192]{2,1,0:T(8,128)(2,1)} %get-tuple-element.228), channel_id=1, source_target_pairs={{0,2},{1,3},{2,0},{3,1},{4,6},{5,7},{6,4},{7,5},{8,10},{9,11},{10,... | collective-permute-start | bytes 453896 | tf_op jit(solution)/shard_map/ppermute | solution.py:39
  253.2 19.1 %collective-permute-start.44 = (f32[2,768]{1,0:T(2,128)}, f32[2,768]{1,0:T(2,128)S(1)}, u32[]{:S(2)}, u32[]{:S(2)}) collective-permute-start(f32[2,768]{1,0:T(2,128)} %slice_bitcast_fusion.40), channel_id=1, source_target_pairs={{0,2},{1,3},{2,0},{3,1},{4,6},{5,7},{6,4},{7,5},{8,10},{9,11},{10,... | collective-permute-start | bytes 18440 | tf_op jit(solution)/shard_map/ppermute | solution.py:39
  253.2 19.1 %collective-permute-start.45 = (f32[2,768]{1,0:T(2,128)}, f32[2,768]{1,0:T(2,128)}, u32[]{:S(2)}, u32[]{:S(2)}) collective-permute-start(f32[2,768]{1,0:T(2,128)} %slice_bitcast_fusion.40), channel_id=1, source_target_pairs={{0,3},{1,0},{2,1},{3,2},{4,7},{5,4},{6,5},{7,6},{8,11},{9,8},{10,9... | collective-permute-start | bytes 18440 | tf_op jit(solution)/shard_map/ppermute | solution.py:39
  270.9 78.9 %collective-permute-start.71 = (bf16[4,2,2,2,96,768]{5,4,3,2,0,1:T(8,128)(2,1)}, bf16[4,2,2,2,96,768]{5,4,3,2,0,1:T(8,128)(2,1)}, u32[]{:S(2)}, u32[]{:S(2)}) collective-permute-start(bf16[4,2,2,2,96,768]{5,4,3,2,0,1:T(8,128)(2,1)} %pad_maximum_fusion), channel_id=1, source_target_pairs={{0,4},{4,0},{8,12},{12,8},{16,20},{20,16},{24,28},{28,24},{1,5},{5... | collective-permute-start | bytes 14155784 | tf_op jit(solution)/shard_map/ppermute | solution.py:44
  285.3 23.1 %collective-permute-start.40 = (bf16[2,197,192]{2,1,0:T(8,128)(2,1)}, bf16[2,197,192]{2,1,0:T(8,128)(2,1)}, u32[]{:S(2)}, u32[]{:S(2)}) collective-permute-start(bf16[2,197,192]{2,1,0:T(8,128)(2,1)} %get-tuple-element.223), channel_id=1, source_target_pairs={{0,1},{1,2},{2,3},{3,0},{4,5},{5,6},{6,7},{7,4},{8,9},{9,10},{10,1... | collective-permute-start | bytes 453896 | tf_op jit(solution)/shard_map/ppermute | solution.py:39
  285.4 24.1 %collective-permute-start.41 = (bf16[2,197,192]{2,1,0:T(8,128)(2,1)}, bf16[2,197,192]{2,1,0:T(8,128)(2,1)}, u32[]{:S(2)}, u32[]{:S(2)}) collective-permute-start(bf16[2,197,192]{2,1,0:T(8,128)(2,1)} %get-tuple-element.224), channel_id=1, source_target_pairs={{0,2},{1,3},{2,0},{3,1},{4,6},{5,7},{6,4},{7,5},{8,10},{9,11},{10,... | collective-permute-start | bytes 453896 | tf_op jit(solution)/shard_map/ppermute | solution.py:39
  291.6 17.8 %collective-permute-start.42 = (bf16[2,197,192]{2,1,0:T(8,128)(2,1)}, bf16[2,197,192]{2,1,0:T(8,128)(2,1)}, u32[]{:S(2)}, u32[]{:S(2)}) collective-permute-start(bf16[2,197,192]{2,1,0:T(8,128)(2,1)} %get-tuple-element.225), channel_id=1, source_target_pairs={{0,3},{1,0},{2,1},{3,2},{4,7},{5,4},{6,5},{7,6},{8,11},{9,8},{10,9... | collective-permute-start | bytes 453896 | tf_op jit(solution)/shard_map/ppermute | solution.py:39
  305.0 42.3 %collective-permute-start.58 = (bf16[4,1,2,2,96,768]{5,4,3,2,0,1:T(8,128)(2,1)}, bf16[4,1,2,2,96,768]{5,4,3,2,0,1:T(8,128)(2,1)}, u32[]{:S(2)}, u32[]{:S(2)}) collective-permute-start(bf16[4,1,2,2,96,768]{5,4,3,2,0,1:T(8,128)(2,1)} %bitcast.436), channel_id=1, source_target_pairs={{0,4},{4,0},{8,12},{12,8},{16,20},{20,16},{24,28},{28,24},{1,5},{5... | collective-permute-start | bytes 7077896 | tf_op jit(solution)/shard_map/ppermute | solution.py:44
  348.7 16.3 %collective-permute-start.61 = (bf16[4,1,2,48,768]{4,3,0,2,1:T(8,128)(2,1)S(1)}, bf16[4,1,2,48,768]{4,3,0,2,1:T(8,128)(2,1)S(1)}, u32[]{:S(2)}, u32[]{:S(2)}) collective-permute-start(bf16[4,1,2,48,768]{4,3,0,2,1:T(8,128)(2,1)S(1)} %fusion.38), channel_id=1, source_target_pairs={{0,16},{4,20},{8,24},{12,28},{16,0},{20,4},{24,8},{28,12},{1,17},{... | collective-permute-start | bytes 1769480 | tf_op jit(solution)/shard_map/ppermute | solution.py:44
  352.4 51.8 %collective-permute-start.74 = (bf16[4,2,2,48,768]{4,3,0,1,2:T(8,128)(2,1)}, bf16[4,2,2,48,768]{4,3,0,1,2:T(8,128)(2,1)}, u32[]{:S(2)}, u32[]{:S(2)}) collective-permute-start(bf16[4,2,2,48,768]{4,3,0,1,2:T(8,128)(2,1)} %fusion.10), channel_id=1, source_target_pairs={{0,16},{4,20},{8,24},{12,28},{16,0},{20,4},{24,8},{28,12},{1,17},{... | collective-permute-start | bytes 3538952 | tf_op jit(solution)/shard_map/ppermute | solution.py:44
  355.9 48.3 %collective-permute-start.72 = (bf16[4,2,2,48,768]{4,3,0,1,2:T(8,128)(2,1)}, bf16[4,2,2,48,768]{4,3,0,1,2:T(8,128)(2,1)}, u32[]{:S(2)}, u32[]{:S(2)}) collective-permute-start(bf16[4,2,2,48,768]{4,3,0,1,2:T(8,128)(2,1)} %fusion.9), channel_id=1, source_target_pairs={{0,8},{4,12},{8,0},{12,4},{16,24},{20,28},{24,16},{28,20},{1,9},{5... | collective-permute-start | bytes 3538952 | tf_op jit(solution)/shard_map/ppermute | solution.py:44
  359.0 38.7 %collective-permute-start.59 = (bf16[4,1,2,48,768]{4,3,0,2,1:T(8,128)(2,1)}, bf16[4,1,2,48,768]{4,3,0,2,1:T(8,128)(2,1)}, u32[]{:S(2)}, u32[]{:S(2)}) collective-permute-start(bf16[4,1,2,48,768]{4,3,0,2,1:T(8,128)(2,1)} %fusion.37), channel_id=1, source_target_pairs={{0,8},{4,12},{8,0},{12,4},{16,24},{20,28},{24,16},{28,20},{1,9},{5... | collective-permute-start | bytes 1769480 | tf_op jit(solution)/shard_map/ppermute | solution.py:44
  366.9 34.4 %collective-permute-start.62 = (bf16[4,1,48,768]{3,2,0,1:T(8,128)(2,1)}, bf16[4,1,48,768]{3,2,0,1:T(8,128)(2,1)}, u32[]{:S(2)}, u32[]{:S(2)}) collective-permute-start(bf16[4,1,48,768]{3,2,0,1:T(8,128)(2,1)} %fusion.43), channel_id=1, source_target_pairs={{0,8},{4,12},{8,0},{12,4},{16,24},{20,28},{24,16},{28,20},{1,9},{5... | collective-permute-start | bytes 884744 | tf_op jit(solution)/shard_map/ppermute | solution.py:44
  426.8 24.4 %collective-permute-start.77 = (bf16[2,96,768]{2,1,0:T(8,128)(2,1)S(1)}, bf16[2,96,768]{2,1,0:T(8,128)(2,1)S(1)}, u32[]{:S(2)}, u32[]{:S(2)}) collective-permute-start(bf16[2,96,768]{2,1,0:T(8,128)(2,1)S(1)} %get-tuple-element.206), channel_id=1, source_target_pairs={{0,2},{1,3},{2,0},{3,1},{4,6},{5,7},{6,4},{7,5},{8,10},{9,11},{10,... | collective-permute-start | bytes 884744 | tf_op jit(solution)/shard_map/ppermute | solution.py:39
  428.1 24.5 %collective-permute-start.68 = (bf16[1,48,768]{2,1,0:T(8,128)(2,1)S(1)}, bf16[1,48,768]{2,1,0:T(8,128)(2,1)S(1)}, u32[]{:S(2)}, u32[]{:S(2)}) collective-permute-start(bf16[1,48,768]{2,1,0:T(8,128)(2,1)S(1)} %get-tuple-element.254), channel_id=1, source_target_pairs={{0,16},{4,20},{8,24},{12,28},{16,0},{20,4},{24,8},{28,12},{1,17},{... | collective-permute-start | bytes 221192 | tf_op jit(solution)/shard_map/ppermute | solution.py:44
  429.3 24.9 %collective-permute-start.66 = (bf16[1,48,768]{2,1,0:T(8,128)(2,1)S(1)}, bf16[1,48,768]{2,1,0:T(8,128)(2,1)S(1)}, u32[]{:S(2)}, u32[]{:S(2)}) collective-permute-start(bf16[1,48,768]{2,1,0:T(8,128)(2,1)S(1)} %get-tuple-element.255), channel_id=1, source_target_pairs={{0,8},{4,12},{8,0},{12,4},{16,24},{20,28},{24,16},{28,20},{1,9},{5... | collective-permute-start | bytes 221192 | tf_op jit(solution)/shard_map/ppermute | solution.py:44
  (127 other events, 1246.9 us)

commit v2 on v1

v2 whole, which is shorter than its diff:
```python
import functools

import jax
import jax.numpy as jnp
from jax import lax
from jax.experimental import pallas as pl
from jax.experimental.pallas import tpu as pltpu
from jax.sharding import PartitionSpec as P

HS = 64
GROUP = 8

norm_eps = 1e-05
score_scale = 0.125
gelu_rate = 1.702
contrast_sharpness = 0.02
masked_score = -1000000000.0
exact = lax.Precision.HIGHEST
f32 = jnp.float32
bf16 = jnp.bfloat16

PIECES = ((0, 2, 4, 6), (0, 4, 2, 6))


def nn(left, right):
    return lax.dot_general(left, right, (((1,), (0,)), ((), ())), preferred_element_type=f32)


def nt(left, right):
    return lax.dot_general(left, right, (((1,), (1,)), ((), ())), preferred_element_type=f32)


def tn(left, right):
    return lax.dot_general(left, right, (((0,), (0,)), ((), ())), preferred_element_type=f32)


def to_heads(value, step):
    count = lax.axis_size("heads")
    return lax.ppermute(value, "heads", [(i, (i + step) % count) for i in range(count)])


def swap_frames(value, bit):
    count = lax.axis_size("frames")
    return lax.ppermute(value, "frames", [(i, i ^ bit) for i in range(count)])


def frame_bits(start=1):
    count = lax.axis_size("frames")
    bits = []
    bit = start
    while bit < count:
        bits.append(bit)
        bit *= 2
    return bits


def norm_stats(rows):
    center = jnp.mean(rows, axis=-1, keepdims=True)
    offset = rows - center
    factor = lax.rsqrt(jnp.mean(offset * offset, axis=-1, keepdims=True) + norm_eps)
    return offset * factor, factor


def norm_back(grad_out, normed, factor, gain):
    scaled = grad_out * gain
    first = jnp.mean(scaled, axis=-1, keepdims=True)
    second = jnp.mean(scaled * normed, axis=-1, keepdims=True)
    grad_in = factor * (scaled - first - normed * second)
    return (
        grad_in,
        jnp.sum(grad_out * normed, axis=0, keepdims=True),
        jnp.sum(grad_out, axis=0, keepdims=True),
    )


def place_weight(target, own, near, far, place, slot):
    block = target.shape[0] // GROUP
    half = block // 2

    @pl.when(slot == 0)
    def _():
        target[...] = own[...]

    @pl.when(slot > 0)
    def _():
        for q in range(2):
            for j in range(4):
                here = (place ^ PIECES[q][j]) * block + q * half
                there = (place ^ PIECES[q][j] ^ 1) * block + q * half
                target[pl.ds(pl.multiple_of(here, 16), half), :] = near[q, j]
                target[pl.ds(pl.multiple_of(there, 16), half), :] = far[q, j]


def spread_grad(keep, send, value, place):
    block = value.shape[0] // GROUP
    for owner in range(GROUP):
        part = value[owner * block : (owner + 1) * block].astype(bf16)
        offset = place ^ owner
        rest = offset // 2
        mine = offset % 2 == 0

        @pl.when(mine)
        def _():
            keep[rest % 2, rest // 2] = part

        @pl.when(jnp.logical_not(mine))
        def _():
            send[rest % 2, rest // 2] = part


def pick_rows(array, first, count):
    row = lax.broadcasted_iota(jnp.int32, (array.shape[0], 1), 0)
    return [
        jnp.sum(jnp.where(row == first + i, array, 0.0), axis=0, keepdims=True)
        for i in range(count)
    ]


def put_rows(rows, first, total):
    row = lax.broadcasted_iota(jnp.int32, (total, 1), 0)
    value = jnp.zeros((total, rows[0].shape[1]), f32)
    for i, line in enumerate(rows):
        value = jnp.where(row == first + i, line, value)
    return value


def join_features(pieces, i, head_index):
    values = [piece[i] for piece in pieces]
    count = len(values)
    blocks = []
    for block in range(count):
        value = values[0]
        slot = (head_index - block + count) % count
        for s in range(1, count):
            value = jnp.where(slot == s, values[s], value)
        blocks.append(value)
    return jnp.concatenate(blocks, axis=1)


def split_features(value, pieces, i, head_index):
    count = len(pieces)
    local = value.shape[1] // count
    blocks = [value[:, b * local : (b + 1) * local] for b in range(count)]
    for s, piece in enumerate(pieces):
        block = (head_index + s) % count
        part = blocks[0]
        for b in range(1, count):
            part = jnp.where(block == b, blocks[b], part)
        piece[i] = part


def message_forward(
    p0, p1, p2, p3, ids_col, ids_row, nat, weight, bias, courier,
    start_out, cls_out, rows_out, proj_out, probs_out, ctx_out, part_out, *, heads, block,
):
    width = nat.shape[1]
    local = heads * HS
    each = p0.shape[0]
    for j, piece in enumerate((p0, p1, p2, p3)):
        span = pl.ds(j * each, each)
        start_out[span, :] = piece[:, :width] + nat[block : block + 1, :]
        cls_out[span, :] = piece[:, width : width + local].astype(bf16)
    base, _ = norm_stats(start_out[...])
    rows = (base * nat[block + 1 : block + 2, :] + nat[block + 2 : block + 3, :]).astype(bf16)
    rows_out[...] = rows
    proj = [
        (nn(rows, weight[:, c, :]) + bias[:, c * local : (c + 1) * local]).astype(bf16)
        for c in range(3)
    ]
    proj_out[...] = jnp.concatenate(proj, axis=1)
    same = ids_col[...] == ids_row[...]
    context = []
    for j in range(heads):
        q, k, v = [p[:, j * HS : (j + 1) * HS] for p in proj]
        scores = jnp.where(same, nt(q, k) * score_scale, masked_score)
        scores = jnp.exp(scores - jnp.max(scores, axis=-1, keepdims=True))
        probs = scores / jnp.sum(scores, axis=-1, keepdims=True)
        probs_out[j] = probs
        context.append(nn(probs.astype(bf16), v).astype(bf16))
    context = jnp.concatenate(context, axis=1)
    ctx_out[...] = context
    part_out[...] = nn(context[:16], courier[...])[:block]


def message_back_one(
    p0, p1, p2, p3, rows, proj, probs_ref, ctx, weight, courier,
    grad_out, weight_out, courier_out, back_out, send_out, bias_out, sums_out, *, heads,
):
    local = heads * HS
    each = p0.shape[0]
    for j, piece in enumerate((p0, p1, p2, p3)):
        grad_out[pl.ds(j * each, each), :] = piece[...]
    grad = grad_out[...].astype(bf16)
    bias_out[...] = jnp.sum(grad.astype(f32), axis=0, keepdims=True)
    courier_out[...] = tn(ctx[...], grad)
    context_grad = nt(grad, courier[...]).astype(bf16)
    dq, dk, dv = [], [], []
    for j in range(heads):
        q, k, v = [
            proj[:, c * local + j * HS : c * local + (j + 1) * HS] for c in range(3)
        ]
        cg = context_grad[:, j * HS : (j + 1) * HS]
        probs = probs_ref[j]
        weighted = probs * nt(cg, v)
        score_grad = (weighted - probs * jnp.sum(weighted, axis=-1, keepdims=True)).astype(bf16)
        dq.append((nn(score_grad, k) * score_scale).astype(bf16))
        dk.append((tn(score_grad, q) * score_scale).astype(bf16))
        dv.append(tn(probs.astype(bf16), cg).astype(bf16))
    back = None
    for c, parts in enumerate((dq, dk, dv)):
        value = jnp.concatenate(parts, axis=1)
        weight_out[:, c, :] = tn(rows[...], value)
        sums_out[c : c + 1, :] = jnp.sum(value.astype(f32), axis=0, keepdims=True)
        term = nt(value, weight[:, c, :])
        back = term if back is None else back + term
    back_out[...] = back
    send_out[...] = back.astype(bf16)


def message_back_two(
    own, r1, r2, r3, grad, start, cls, nat, weight, weight_out, vec_out, cls_back_out, *, block
):
    total = own[...]
    for piece in (r1, r2, r3):
        total = total + piece[...].astype(f32)
    base, factor = norm_stats(start[...])
    grad_in, gain_grad, shift_grad = norm_back(total, base, factor, nat[block + 1 : block + 2, :])
    start_grad = (grad[...] + grad_in).astype(bf16)
    weight_out[...] = tn(cls[...], start_grad)
    vec_out[0:1, :] = gain_grad
    vec_out[1:2, :] = shift_grad
    vec_out[2:3, :] = jnp.sum(start_grad.astype(f32), axis=0, keepdims=True)
    cls_back_out[...] = nt(start_grad[:16], weight[...])[:block]


def contrast(
    p0, p1, p2, p3, ids_row, ids_col, group_col, group_row, loss_out, grad_out, *, videos, block
):
    each = p0.shape[0]
    padded = group_col.shape[0]
    video = lax.broadcasted_iota(jnp.int32, (padded, 1), 0)
    onehot = (ids_row[...] == video).astype(f32)
    counts = jnp.sum(onehot, axis=1, keepdims=True)
    counts = jnp.where(video < videos, counts, 1.0)
    pooled = None
    for j, piece in enumerate((p0, p1, p2, p3)):
        hot = (ids_row[:, j * each : (j + 1) * each] == video).astype(f32)
        term = jnp.dot(hot, piece[...], precision=exact, preferred_element_type=f32)
        pooled = term if pooled is None else pooled + term
    pooled = pooled / counts
    scale = lax.rsqrt(jnp.sum(pooled * pooled, axis=1, keepdims=True) + 1e-06)
    unit = pooled * scale
    logits = (
        lax.dot_general(
            unit, unit, (((1,), (1,)), ((), ())), precision=exact, preferred_element_type=f32
        )
        / contrast_sharpness
    )
    other = lax.broadcasted_iota(jnp.int32, (padded, padded), 1)
    this = lax.broadcasted_iota(jnp.int32, (padded, padded), 0)
    usable = jnp.logical_and(other != this, other < videos)
    logits = jnp.where(usable, logits, masked_score)
    top = jnp.max(logits, axis=1, keepdims=True)
    powers = jnp.exp(logits - top)
    total = jnp.sum(powers, axis=1, keepdims=True)
    log_total = top + jnp.log(total)
    real = jnp.logical_and(usable, this < videos)
    positive = jnp.where(
        jnp.logical_and(group_col[...] == group_row[...], real), 1.0, 0.0
    )
    weights = positive / jnp.maximum(jnp.sum(positive, axis=1, keepdims=True), 1.0)
    each_loss = jnp.where(real, weights * (log_total - logits), 0.0)
    loss_out[...] = jnp.sum(jnp.sum(each_loss, axis=1, keepdims=True), axis=0, keepdims=True)
    g_logits = jnp.sum(weights, axis=1, keepdims=True) * (powers / total) - weights
    g_logits = jnp.where(real, g_logits, 0.0)
    g_unit = jnp.dot(g_logits, unit, precision=exact, preferred_element_type=f32)
    g_unit = g_unit + lax.dot_general(
        g_logits, unit, (((0,), (0,)), ((), ())), precision=exact, preferred_element_type=f32
    )
    g_unit = g_unit / contrast_sharpness
    inner = jnp.sum(pooled * g_unit, axis=1, keepdims=True)
    g_pooled = scale * g_unit - scale * scale * scale * inner * pooled
    hot = (ids_col[:block, :] == lax.broadcasted_iota(jnp.int32, (block, padded), 1)).astype(f32)
    grad_out[...] = jnp.dot(hot, g_pooled / counts, precision=exact, preferred_element_type=f32)


def attention_forward(
    scalars, x0, x1, x2, x3, m0, m1, m2, m3, start, nat, bias_ref, own, near, far,
    qkv_out, probs_out, ctx_out, rows, normed, s2_out, weight, total, *, heads, block, tokens,
):
    slot = pl.program_id(0)
    head_index, place = scalars[0], scalars[1]
    frames, patches, _ = x0.shape
    width = nat.shape[1]
    local = heads * HS

    @pl.when(slot == 0)
    def _():
        lines = start[...] + m0[...] + m1[...] + m2[...] + m3[...] + nat[block + 3 : block + 4, :]
        message = pick_rows(lines, head_index * frames, frames)
        for i in range(frames):
            base = i * tokens
            rows[base : base + patches, :] = join_features((x0, x1, x2, x3), i, head_index).astype(f32)
            rows[base + patches : base + patches + 1, :] = message[i]
            rows[base + patches + 1 : base + tokens, :] = jnp.zeros(
                (tokens - patches - 1, width), f32
            )
        base, _ = norm_stats(rows[...])
        normed[...] = (
            base * nat[block + 4 : block + 5, :] + nat[block + 5 : block + 6, :]
        ).astype(bf16)
        total[...] = jnp.zeros_like(total)

    place_weight(weight, own, near, far, place, slot)
    projected = (nn(normed[...], weight[:, : 3 * local]) + bias_ref[...]).astype(bf16)
    qkv_out[...] = projected
    key_ok = lax.broadcasted_iota(jnp.int32, (tokens, tokens), 1) <= patches
    blank = jnp.zeros((tokens, width // 3 - local), bf16)
    for i in range(frames):
        part = projected[i * tokens : (i + 1) * tokens]
        pieces = [blank]
        for j in range(heads):
            q = part[:, j * HS : (j + 1) * HS]
            k = part[:, local + j * HS : local + (j + 1) * HS]
            v = part[:, 2 * local + j * HS : 2 * local + (j + 1) * HS]
            scores = jnp.where(key_ok, nt(q, k) * score_scale, masked_score)
            scores = jnp.exp(scores - jnp.max(scores, axis=-1, keepdims=True))
            probs = (scores * (1.0 / jnp.sum(scores, axis=-1, keepdims=True))).astype(bf16)
            probs_out[i * heads + j] = probs
            pieces.append(nn(probs, v).astype(bf16))
        context = jnp.concatenate(pieces, axis=1)
        ctx_out[pl.ds(i * tokens, tokens), :] = context
        total[pl.ds(i * tokens, tokens), :] += nt(context, weight[:, 2 * width // 3 :])

    @pl.when(slot == pl.num_programs(0) - 1)
    def _():
        s2_out[...] = rows[...] + total[...] + nat[block + 6 : block + 7, :]


def mlp_forward(
    scalars, s2_ref, nat, fc_bias_ref,
    fc_own, fc_near, fc_far, proj_own, proj_near, proj_far,
    pre_out, o0, o1, o2, o3, cls_out, normed, fc, proj, total, *, block, tokens,
):
    slot = pl.program_id(0)
    head_index, place = scalars[0], scalars[1]

    @pl.when(slot == 0)
    def _():
        base, _ = norm_stats(s2_ref[...])
        normed[...] = (
            base * nat[block + 7 : block + 8, :] + nat[block + 8 : block + 9, :]
        ).astype(bf16)
        total[...] = jnp.zeros_like(total)

    place_weight(fc, fc_own, fc_near, fc_far, place, slot)
    place_weight(proj, proj_own, proj_near, proj_far, place, slot)
    pre = nn(normed[...], fc[...]) + fc_bias_ref[...]
    pre_out[...] = pre
    hidden = (pre * jax.nn.sigmoid(gelu_rate * pre)).astype(bf16)
    total[...] += nn(hidden, proj[...])

    @pl.when(slot == pl.num_programs(0) - 1)
    def _():
        total[...] = s2_ref[...] + total[...] + nat[block + 9 : block + 10, :]
        frames, patches, _ = o0.shape
        cls = []
        for i in range(frames):
            base = i * tokens
            split_features(
                total[base : base + patches, :].astype(bf16), (o0, o1, o2, o3), i, head_index
            )
            cls.append(total[base : base + 1, :])
        cls_out[...] = put_rows(cls, head_index * frames, block)


def mlp_backward(
    scalars, u0, u1, u2, u3, cls_ref, s2_ref, pre_ref, nat,
    fc_own, fc_near, fc_far, proj_own, proj_near, proj_far,
    keep, send, fc_bias_out, vec_out, g2_out,
    normed, grad3, fc, proj, total, *, block, tokens,
):
    slot = pl.program_id(0)
    head_index, place = scalars[0], scalars[1]
    frames, patches, _ = u0.shape
    width = nat.shape[1]

    @pl.when(slot == 0)
    def _():
        base, _ = norm_stats(s2_ref[...])
        normed[...] = (
            base * nat[block + 7 : block + 8, :] + nat[block + 8 : block + 9, :]
        ).astype(bf16)
        lines = pick_rows(cls_ref[...], head_index * frames, frames)
        token = lax.broadcasted_iota(jnp.int32, (patches, 1), 0)
        for i in range(frames):
            base = i * tokens
            value = join_features((u0, u1, u2, u3), i, head_index).astype(f32)
            grad3[base : base + patches, :] = value + jnp.where(token == 0, lines[i], 0.0)
            grad3[base + patches : base + tokens, :] = jnp.zeros((tokens - patches, width), f32)
        total[...] = jnp.zeros_like(total)

    place_weight(fc, fc_own, fc_near, fc_far, place, slot)
    place_weight(proj, proj_own, proj_near, proj_far, place, slot)
    mlp_grad = grad3[...].astype(bf16)
    pre = pre_ref[...]
    gate = jax.nn.sigmoid(gelu_rate * pre)
    hidden = (pre * gate).astype(bf16)
    spread_grad(keep.at[1], send.at[1], tn(hidden, mlp_grad), place)
    hidden_grad = nt(mlp_grad, proj[...])
    pre_grad = (hidden_grad * (gate + gelu_rate * pre * gate * (1.0 - gate))).astype(bf16)
    fc_bias_out[...] = jnp.sum(pre_grad.astype(f32), axis=0, keepdims=True)
    spread_grad(keep.at[0], send.at[0], tn(normed[...], pre_grad), place)
    total[...] += nt(pre_grad, fc[...])

    @pl.when(slot == pl.num_programs(0) - 1)
    def _():
        base, factor = norm_stats(s2_ref[...])
        grad_in, gain_grad, shift_grad = norm_back(
            total[...], base, factor, nat[block + 7 : block + 8, :]
        )
        g2_out[...] = grad3[...] + grad_in
        vec_out[0:1, :] = gain_grad
        vec_out[1:2, :] = shift_grad
        vec_out[2:3, :] = jnp.sum(grad3[...].astype(bf16).astype(f32), axis=0, keepdims=True)
        vec_out[3:8, :] = jnp.zeros((5, width), f32)


def attention_backward(
    scalars, g2_ref, rows, qkv_ref, probs_ref, nat, mlp_vec, fc_bias_grad, own, near, far,
    dproj, v0, v1, v2, v3, o0, o1, o2, o3, msg_out,
    grad, sums, weight, total, *, heads, block, tokens,
):
    slot = pl.program_id(0)
    head_index, place = scalars[0], scalars[1]
    frames, patches, _ = o0.shape
    width = nat.shape[1]
    local = heads * HS
    wide = width // 3

    @pl.when(slot == 0)
    def _():
        grad[...] = g2_ref[...].astype(bf16)
        total[...] = jnp.zeros_like(total)

    place_weight(weight, own, near, far, place, slot)
    context_grad = nn(grad[...], weight[:, 2 * wide :]).astype(bf16)
    skip = wide - local
    for i in range(frames):
        span = slice(i * tokens, (i + 1) * tokens)
        dq, dk, dv = [], [], []
        for j in range(heads):
            q = qkv_ref[span, j * HS : (j + 1) * HS]
            k = qkv_ref[span, local + j * HS : local + (j + 1) * HS]
            v = qkv_ref[span, 2 * local + j * HS : 2 * local + (j + 1) * HS]
            cg = context_grad[span, skip + j * HS : skip + (j + 1) * HS]
            low = probs_ref[i * heads + j]
            probs = low.astype(f32)
            weighted = probs * nt(cg, v)
            score_grad = (
                weighted - probs * jnp.sum(weighted, axis=-1, keepdims=True)
            ).astype(bf16)
            dq.append((nn(score_grad, k) * score_scale).astype(bf16))
            dk.append((tn(score_grad, q) * score_scale).astype(bf16))
            dv.append(tn(low, cg).astype(bf16))
        dproj[pl.ds(i * tokens, tokens), :] = jnp.concatenate(
            dq + dk + dv + [jnp.zeros((tokens, width - 3 * local), bf16)], axis=1
        )
    all_grads = dproj[...]
    sums[pl.ds(slot, 1), :] = jnp.sum(all_grads.astype(f32), axis=0, keepdims=True)
    total[...] += nt(all_grads[:, : 3 * local], weight[:, : 3 * local])

    @pl.when(slot == pl.num_programs(0) - 1)
    def _():
        base, factor = norm_stats(rows[...])
        grad_in, gain_grad, shift_grad = norm_back(
            total[...], base, factor, nat[block + 4 : block + 5, :]
        )
        total[...] = grad_in + g2_ref[...]
        message = []
        for i in range(frames):
            first = i * tokens
            split_features(
                total[first : first + patches, :].astype(bf16), (o0, o1, o2, o3), i, head_index
            )
            message.append(total[first + patches : first + patches + 1, :])
        msg_out[...] = put_rows(message, head_index * frames, block)
        out_grad = jnp.sum(grad[...].astype(f32), axis=0, keepdims=True)
        for s, vec in enumerate((v0, v1, v2, v3)):
            vec[0:1, :] = gain_grad
            vec[1:2, :] = shift_grad
            vec[2:3, :] = out_grad
            vec[3:6, :] = mlp_vec[0:3, :]
            vec[6:7, :] = fc_bias_grad[s]
            vec[7:8, :] = sums[s : s + 1, :]


def attention_weights(scalars, g2_ref, normed, dproj, ctx, keep, send, grad):
    slot = pl.program_id(0)
    wide = normed.shape[1] // 3

    @pl.when(slot == 0)
    def _():
        grad[...] = g2_ref[...].astype(bf16)

    low_part = tn(normed[...], dproj[:, : 2 * wide])
    high_part = tn(normed[...], dproj[:, 2 * wide :]) + tn(grad[...], ctx[...])
    spread_grad(
        keep.at[0], send.at[0], jnp.concatenate([low_part, high_part], axis=1), scalars[1]
    )


def finish_mlp(scalars, near, far, fc_out, proj_out):
    here = (pl.program_id(0) ^ scalars[1]) % 2 == 0

    @pl.when(here)
    def _():
        fc_out[...] = near[0].astype(f32)
        proj_out[...] = near[1].astype(f32)

    @pl.when(jnp.logical_not(here))
    def _():
        fc_out[...] = far[0].astype(f32)
        proj_out[...] = far[1].astype(f32)


def finish_attention(scalars, near, far, qkv_out, out_out, rows):
    place = scalars[1]
    block = near.shape[2]
    for k in range(near.shape[0]):
        for c, piece in enumerate((near, far)):
            first = ((2 * k + c) ^ place) * block
            rows[pl.ds(pl.multiple_of(first, 32), block), :] = piece[k, 0].astype(f32)
    local = qkv_out.shape[2]
    for c in range(3):
        qkv_out[:, c, :] = rows[:, c * local : (c + 1) * local]
    out_out[...] = rows[:, 3 * local :].T


def finish_frames(scalars, p0, p1, p2, p3, add, out):
    frames = p0.shape[0]
    for s, piece in enumerate((p0, p1, p2, p3)):
        first = ((scalars[0] - s + 4) % 4) * frames
        for i in range(frames):
            out[first + i] = piece[i].astype(out.dtype)
    if add is not None:
        for i in range(out.shape[0]):
            out[i, 0:1, :] = out[i, 0:1, :] + add[i : i + 1, :]


def finish_output(scalars, p0, p1, p2, p3, out):
    finish_frames(scalars, p0, p1, p2, p3, None, out)

def whole(array):
    count = array.ndim
    return pl.BlockSpec(array.shape, lambda s, sc: (0,) * count)


def first_rows(array, rows):
    return pl.BlockSpec((rows, array.shape[1]), lambda s, sc: (0, 0))


def per_slot(array):
    count = array.ndim - 1
    return pl.BlockSpec((None,) + array.shape[1:], lambda s, sc: (s,) + (0,) * count)


def weight_specs(own, near, which):
    def pick(s, sc):
        return (0, 0, jnp.maximum(s - 1, 0), which, 0, 0)

    far_spec = pl.BlockSpec((2, 4, None, None) + near.shape[4:], pick)
    return [pl.BlockSpec(own.shape, lambda s, sc: (0, 0)), far_spec, far_spec]


def shaped(shape, dtype):
    return jax.ShapeDtypeStruct(tuple(shape), dtype)


def slot_out(shape, dtype, slots):
    count = len(shape)
    return (
        shaped((slots,) + tuple(shape), dtype),
        pl.BlockSpec((None,) + tuple(shape), lambda s, sc: (s,) + (0,) * count),
    )


def full_out(shape, dtype):
    count = len(shape)
    return shaped(shape, dtype), pl.BlockSpec(tuple(shape), lambda s, sc: (0,) * count)


def call(kernel, steps, scalars, inputs, outs, scratch=(), flops=0):
    inputs = [a if isinstance(a, tuple) else (a, whole(a)) for a in inputs]
    arrays, specs = zip(*inputs)
    shapes, out_specs = zip(*outs)
    moved = sum(a.size * a.dtype.itemsize for a in arrays + shapes)
    return pl.pallas_call(
        kernel,
        grid_spec=pltpu.PrefetchScalarGridSpec(
            num_scalar_prefetch=1,
            grid=(steps,),
            in_specs=list(specs),
            out_specs=list(out_specs),
            scratch_shapes=list(scratch),
        ),
        out_shape=list(shapes),
        cost_estimate=pl.CostEstimate(flops=flops, bytes_accessed=moved, transcendentals=0),
    )(scalars, *arrays)


def call_once(kernel, inputs, outs):
    moved = sum(a.size * a.dtype.itemsize for a in list(inputs) + list(outs))
    return pl.pallas_call(
        kernel,
        in_specs=[pl.BlockSpec(memory_space=pltpu.VMEM)] * len(inputs),
        out_specs=[pl.BlockSpec(memory_space=pltpu.VMEM)] * len(outs),
        out_shape=list(outs),
        cost_estimate=pl.CostEstimate(flops=0, bytes_accessed=moved, transcendentals=0),
    )(*inputs)


def tie(first, second):
    return lax.optimization_barrier((first, second))


def gather_rows(value):
    for bit in frame_bits(GROUP):
        value = jnp.concatenate([value, swap_frames(value, bit)], axis=0)
    value = jnp.concatenate([value, swap_frames(value, 1)], axis=0)
    return [value] + [swap_frames(value, bit) for bit in (2, 4, 6)]


def gathered_places(frame_index):
    count = lax.axis_size("frames")
    far = jnp.arange(count // GROUP) * GROUP
    near = jnp.arange(GROUP)
    return frame_index ^ (near.reshape(4, 2, 1) + far).reshape(-1)


def gather_weights(mine):
    half = mine.shape[1] // 2
    count = lax.axis_size("heads")
    got = [to_heads(mine, step) for step in range(1, count)]
    first = jnp.stack([g[:, :half] for g in got])
    second = jnp.stack([g[:, half:] for g in got])
    first = jnp.stack([first, swap_frames(first, 2)])
    second = jnp.stack([second, swap_frames(second, 4)])
    first_far = swap_frames(first, 4)
    second_far = swap_frames(second, 2)
    near = jnp.stack(
        [
            jnp.concatenate([first, first_far], axis=0),
            jnp.concatenate([second, second_far], axis=0),
        ]
    )
    return near, swap_frames(near, 1)


def reduce_first(keep, got):
    half = keep.shape[4] // 2

    def summed(x, y, low):
        rows = slice(0, half) if low else slice(half, 2 * half)
        index = (slice(None), slice(None), x, y, rows)
        return keep[index].astype(f32) + got[index].astype(f32)

    both = slice(None)
    first_got = swap_frames(summed(1, both, True).astype(bf16), 2)
    second_got = swap_frames(summed(both, 1, False).astype(bf16), 4)
    return summed, first_got, second_got


def reduce_second(summed, first_got, second_got):
    def next_first(y):
        return summed(0, y, True) + first_got[:, :, y].astype(f32)

    def next_second(x):
        return summed(x, 0, False) + second_got[:, :, x].astype(f32)

    first_last = swap_frames(next_first(1).astype(bf16), 4)
    second_last = swap_frames(next_second(1).astype(bf16), 2)
    return next_first(0), next_second(0), first_last, second_last


def reduce_last(first, second, first_last, second_last):
    first = first + first_last.astype(f32)
    second = second + second_last.astype(f32)
    total = jnp.concatenate([first, second], axis=2).astype(bf16)
    for bit in frame_bits(GROUP):
        total = (total.astype(f32) + swap_frames(total, bit).astype(f32)).astype(bf16)
    own = total[0].astype(f32)
    for step in range(1, total.shape[0]):
        own = own + to_heads(total[step], -step).astype(f32)
    return own.astype(bf16)


def regather(rows):
    half = rows.shape[1] // 2
    first, second = rows[:, :half], rows[:, half:]
    first = jnp.stack([first, swap_frames(first, 2)])
    second = jnp.stack([second, swap_frames(second, 4)])
    first = jnp.concatenate([first, swap_frames(first, 4)], axis=0)
    second = jnp.concatenate([second, swap_frames(second, 2)], axis=0)
    second = jnp.stack([second[0], second[2], second[1], second[3]])
    near = jnp.concatenate([first, second], axis=2)
    return near, swap_frames(near, 1)


def on_device(
    frames_in,
    upstream,
    video_of_frame,
    group_ids,
    msg_fc_weight,
    msg_fc_bias,
    msg_gain,
    msg_shift,
    msg_qkv_weight,
    msg_qv_bias,
    courier_result_kernel,
    msg_out_bias,
    ln1_gain,
    ln1_shift,
    qkv_weight,
    qv_bias,
    picture_result_kernel,
    out_bias,
    ln2_gain,
    ln2_shift,
    fc_weight,
    fc_bias,
    proj_weight,
    proj_bias,
):
    block, patches, local = frames_in.shape
    width = msg_qkv_weight.shape[0]
    slots = lax.axis_size("heads")
    own_frames = block // slots
    heads = local // HS
    tokens = -(-(patches + 1) // 16) * 16
    rows = own_frames * tokens
    hidden_local = fc_weight.shape[1]
    frame_index = lax.axis_index("frames")
    head_index = lax.axis_index("heads")
    place = frame_index % GROUP
    scalars = jnp.stack([head_index, place]).astype(jnp.int32)
    steps = range(1, slots)
    sizes = dict(block=block, tokens=tokens)

    def exchange(array):
        def frames_of(step):
            start = jnp.mod(head_index + step, slots) * own_frames
            return lax.dynamic_slice_in_dim(array, start, own_frames, axis=0)

        return [frames_of(0)] + [to_heads(frames_of(s), s) for s in steps]

    def to_all_heads(value):
        return [value] + [to_heads(value, s) for s in steps]

    def own_features(array):
        return lax.dynamic_slice_in_dim(array, head_index * local, local, axis=array.ndim - 1)

    def my_rows(array):
        size = array.shape[0] // GROUP
        return lax.dynamic_slice_in_dim(array, place * size, size, axis=0)

    cls_own = frames_in[:, 0, :]
    vectors = jnp.concatenate(
        [
            msg_fc_bias, msg_gain, msg_shift, msg_out_bias, ln1_gain, ln1_shift,
            out_bias, ln2_gain, ln2_shift, proj_bias,
        ]
    ).reshape(-1, local)
    lane = jnp.arange(width, dtype=jnp.int32)[None, :] // local
    vectors = jnp.where(lane == head_index, jnp.tile(vectors, (1, slots)), 0.0)
    qkv_bias = jnp.concatenate([qv_bias[0], jnp.zeros((local,), bf16), qv_bias[1], jnp.zeros((local,), bf16)])
    small = jnp.concatenate(
        [
            nn(cls_own, msg_fc_weight),
            vectors.astype(f32),
            fc_bias.reshape(1, -1).astype(f32),
            qkv_bias.reshape(1, -1).astype(f32),
            jnp.zeros((24 - block - 12, width), f32),
        ],
        axis=0,
    )
    small = to_all_heads(small)
    nat = sum(small)
    fc_bias_slots = jnp.stack([part[block + 10 : block + 11] for part in small])
    qkv_bias_slots = jnp.stack([part[block + 11 : block + 12, : 3 * local] for part in small])

    x_pieces = exchange(frames_in)

    attn_own = jnp.concatenate(
        [qkv_weight.reshape(width, 3 * local), picture_result_kernel.T], axis=1
    )
    attn_near, attn_far = gather_weights(my_rows(attn_own)[None])
    mlp_near, mlp_far = gather_weights(jnp.stack([my_rows(fc_weight), my_rows(proj_weight)]))
    attn_weights = list(
        zip((attn_own, attn_near, attn_far), weight_specs(attn_own, attn_near, 0))
    )
    mlp_weights = list(
        zip(
            (fc_weight, mlp_near, mlp_far, proj_weight, mlp_near, mlp_far),
            weight_specs(fc_weight, mlp_near, 0) + weight_specs(proj_weight, mlp_near, 1),
        )
    )

    sent = jnp.concatenate(
        [nat[:block], cls_own.astype(f32), jnp.zeros((block, 64), f32)], axis=1
    )
    start_pieces = gather_rows(sent)
    ids = video_of_frame.reshape(-1, block)[gathered_places(frame_index)].reshape(-1)
    ids_row, ids_col = ids[None, :], ids[:, None]
    total_frames = ids.shape[0]
    msg_bias = jnp.concatenate([msg_qv_bias[0], jnp.zeros((local,), bf16), msg_qv_bias[1]])
    start, cls_all, msg_rows, msg_proj, msg_probs, msg_context, msg_part = call_once(
        functools.partial(message_forward, heads=heads, block=block),
        start_pieces
        + [ids_col, ids_row, nat, msg_qkv_weight, msg_bias[None].astype(f32), courier_result_kernel],
        [
            shaped((total_frames, width), f32),
            shaped((total_frames, local), bf16),
            shaped((total_frames, width), bf16),
            shaped((total_frames, 3 * local), bf16),
            shaped((heads, total_frames, total_frames), f32),
            shaped((total_frames, local), bf16),
            shaped((block, width), f32),
        ],
    )
    msg_parts = to_all_heads(msg_part)

    wide = width // 3
    qkv, probs, context, stream_one, normed_one, stream_two = call(
        functools.partial(attention_forward, heads=heads, **sizes),
        slots,
        scalars,
        x_pieces
        + msg_parts
        + [(start, first_rows(start, block)), nat, (qkv_bias_slots, per_slot(qkv_bias_slots))]
        + attn_weights,
        [
            slot_out((rows, 3 * local), bf16, slots),
            slot_out((own_frames * heads, tokens, tokens), bf16, slots),
            slot_out((rows, wide), bf16, slots),
            full_out((rows, width), f32),
            full_out((rows, width), bf16),
            full_out((rows, width), f32),
        ],
        [pltpu.VMEM((width, width), bf16), pltpu.VMEM((rows, width), f32)],
        2 * rows * width * width * slots,
    )

    frame_out = shaped((own_frames, patches, local), bf16)
    pre, out_0, out_1, out_2, out_3, cls_block = call(
        functools.partial(mlp_forward, **sizes),
        slots,
        scalars,
        [stream_two, nat, (fc_bias_slots, per_slot(fc_bias_slots))] + mlp_weights,
        [slot_out((rows, hidden_local), f32, slots)]
        + [full_out(frame_out.shape, bf16)] * slots
        + [full_out((block, width), f32)],
        [
            pltpu.VMEM((rows, width), bf16),
            pltpu.VMEM((width, hidden_local), bf16),
            pltpu.VMEM((hidden_local, width), bf16),
            pltpu.VMEM((rows, width), f32),
        ],
        4 * rows * width * hidden_local * slots,
    )

    cls_pieces = gather_rows(sum(to_all_heads(cls_block)))
    videos = group_ids.shape[0]
    groups = jnp.pad(group_ids, (0, -videos % 8), constant_values=-1)
    loss_value, cls_grad = call_once(
        functools.partial(contrast, videos=videos, block=block),
        cls_pieces + [ids_row, ids_col, groups[:, None], groups[None, :]],
        [shaped((1, 1), f32), shaped((block, width), f32)],
    )

    up_pieces = exchange(upstream)
    out_pieces = [out_0] + [to_heads(o, s) for s, o in zip(steps, (out_1, out_2, out_3))]

    piece = (2, 2, width // GROUP, width)
    keep, send, fc_bias_grad, mlp_vec, grad_two = call(
        functools.partial(mlp_backward, **sizes),
        slots,
        scalars,
        up_pieces + [cls_grad, stream_two, (pre, per_slot(pre)), nat] + mlp_weights,
        [
            slot_out((2,) + piece, bf16, slots),
            slot_out((2,) + piece, bf16, slots),
            slot_out((1, hidden_local), f32, slots),
            full_out((8, width), f32),
            full_out((rows, width), f32),
        ],
        [
            pltpu.VMEM((rows, width), bf16),
            pltpu.VMEM((rows, width), f32),
            pltpu.VMEM((width, hidden_local), bf16),
            pltpu.VMEM((hidden_local, width), bf16),
            pltpu.VMEM((rows, width), f32),
        ],
        8 * rows * width * hidden_local * slots,
    )
    mlp_got = swap_frames(send, 1)

    dproj, vec_0, vec_1, vec_2, vec_3, gi_0, gi_1, gi_2, gi_3, grad_msg_block = call(
        functools.partial(attention_backward, heads=heads, **sizes),
        slots,
        scalars,
        [grad_two, stream_one, (qkv, per_slot(qkv)), (probs, per_slot(probs)), nat, mlp_vec, fc_bias_grad]
        + attn_weights,
        [slot_out((rows, width), bf16, slots)]
        + [full_out((8, width), f32)] * slots
        + [full_out(frame_out.shape, bf16)] * slots
        + [full_out((block, width), f32)],
        [
            pltpu.VMEM((rows, width), bf16),
            pltpu.VMEM((8, width), f32),
            pltpu.VMEM((width, width), bf16),
            pltpu.VMEM((rows, width), f32),
        ],
        6 * rows * width * width * slots,
    )
    dproj, mlp_got = tie(dproj, mlp_got)
    mlp_state = reduce_first(keep, mlp_got)
    attn_keep, attn_send = call(
        attention_weights,
        slots,
        scalars,
        [grad_two, normed_one, (dproj, per_slot(dproj)), (context, per_slot(context))],
        [slot_out((1,) + piece, bf16, slots), slot_out((1,) + piece, bf16, slots)],
        [pltpu.VMEM((rows, width), bf16)],
        2 * rows * width * width * slots,
    )
    attn_got = swap_frames(attn_send, 1)
    msg_heads = to_all_heads(grad_msg_block)
    msg_pieces = gather_rows(sum(msg_heads))

    (
        grad_message, grad_msg_qkv_weight, grad_msg_out_weight, back_own, back_send, msg_bias_sum, msg_sums,
    ) = call_once(
        functools.partial(message_back_one, heads=heads),
        msg_pieces + [msg_rows, msg_proj, msg_probs, msg_context, msg_qkv_weight, courier_result_kernel],
        [
            shaped((total_frames, width), f32),
            shaped((width, 3, local), f32),
            shaped((local, width), f32),
            shaped((total_frames, width), f32),
            shaped((total_frames, width), bf16),
            shaped((1, width), f32),
            shaped((3, local), f32),
        ],
    )
    back = [back_own] + [to_heads(back_send, s) for s in steps]
    attn_state = reduce_first(attn_keep, attn_got)
    mlp_state = reduce_second(*mlp_state)
    grad_msg_fc_weight, msg_vec, cls_back = call_once(
        functools.partial(message_back_two, block=block),
        back + [grad_message, start, cls_all, nat, msg_fc_weight],
        [shaped((local, width), f32), shaped((3, width), f32), shaped((block, local), f32)],
    )
    attn_state = reduce_second(*attn_state)
    grad_pieces = [gi_0] + [to_heads(g, s) for s, g in zip(steps, (gi_1, gi_2, gi_3))]

    mlp_near, mlp_far = regather(reduce_last(*mlp_state))
    attn_near, attn_far = regather(reduce_last(*attn_state))

    vec = vec_0 + sum(to_heads(v, -s) for s, v in zip(steps, (vec_1, vec_2, vec_3)))
    for bit in frame_bits():
        vec = vec + swap_frames(vec, bit)

    def picked(s, sc):
        return ((s ^ sc[1]) // 2, 0, 0, 0)

    part_spec = pl.BlockSpec((None,) + mlp_near.shape[1:], picked)
    out_spec = pl.BlockSpec((width // GROUP, width), lambda s, sc: (s, 0))
    grad_fc_weight, grad_proj_weight = call(
        finish_mlp,
        GROUP,
        scalars,
        [(mlp_near, part_spec), (mlp_far, part_spec)],
        [(shaped((width, width), f32), out_spec)] * 2,
    )
    grad_qkv_weight, grad_out_weight = call(
        finish_attention,
        1,
        scalars,
        [attn_near, attn_far],
        [full_out((width, 3, local), f32), full_out((local, width), f32)],
        [pltpu.VMEM((width, width), f32)],
    )
    (output,) = call(
        finish_output, 1, scalars, out_pieces, [full_out((block, patches, local), bf16)]
    )
    (grad_input,) = call(
        finish_frames, 1, scalars, grad_pieces + [cls_back], [full_out((block, patches, local), f32)]
    )
    own = own_features(jnp.concatenate([vec[:6], msg_vec, msg_bias_sum], axis=0))
    return (
        output,
        loss_value.reshape(()),
        grad_input,
        grad_msg_fc_weight,
        own[8],
        own[6],
        own[7],
        grad_msg_qkv_weight,
        jnp.stack([msg_sums[0], msg_sums[2]]),
        grad_msg_out_weight,
        own[9],
        own[0],
        own[1],
        grad_qkv_weight,
        jnp.stack([vec[7, :local], vec[7, 2 * local : 3 * local]]),
        grad_out_weight,
        own[2],
        own[3],
        own[4],
        grad_fc_weight,
        vec[6],
        grad_proj_weight,
        own[5],
    )


def solution(mesh):
    placed = (
        P("frames", None, "heads"),
        P("frames", None, "heads"),
        P(),
        P(),
        P("heads", None),
        P("heads"),
        P("heads"),
        P("heads"),
        P(None, None, "heads"),
        P(None, "heads"),
        P("heads", None),
        P("heads"),
        P("heads"),
        P("heads"),
        P(None, None, "heads"),
        P(None, "heads"),
        P("heads", None),
        P("heads"),
        P("heads"),
        P("heads"),
        P(None, "heads"),
        P("heads"),
        P("heads", None),
        P("heads"),
    )
    return jax.shard_map(
        on_device,
        mesh=mesh,
        in_specs=placed,
        out_specs=(
            P("frames", None, "heads"),
            P(),
            P("frames", None, "heads"),
            P("heads", None),
            P("heads"),
            P("heads"),
            P("heads"),
            P(None, None, "heads"),
            P(None, "heads"),
            P("heads", None),
            P("heads"),
            P("heads"),
            P("heads"),
            P(None, None, "heads"),
            P(None, "heads"),
            P("heads", None),
            P("heads"),
            P("heads"),
            P("heads"),
            P(None, "heads"),
            P("heads"),
            P("heads", None),
            P("heads"),
        ),
        check_vma=False,
    )
```

time: 501 us -> 503 us (level)
  the two profiles are of different devices: /device:TPU:0 before, /device:TPU:9 now
where the time goes in v2:
time: 503 us; the launch traced here: 493 us
  waiting for transfers between devices  165 us (33%)
  Pallas kernels  124 us (25%)
  starting transfers between devices  105 us (21%)
  local copies, waits for them, and re-layouts  61.9 us (12%)
  other arithmetic  34.4 us (7%)
    ppermute x42, waiting for transfers between devices, to_heads(): lax.ppermute(value, 'heads', [(i, (i + step) % count) for i in range(coun...  107 us
    pallas_call x9, Pallas kernels, call(): pl.pallas_call(kernel, grid_spec=pltpu.PrefetchScalarGridSpec(num_scalar_...  106 us
    ppermute x45, waiting for transfers between devices, swap_frames(): return lax.ppermute(value, 'frames', [(i, i ^ bit) for i in range(count)])  58.1 us
    ppermute x45, starting transfers between devices, swap_frames(): return lax.ppermute(value, 'frames', [(i, i ^ bit) for i in range(count)])  57.5 us
    ppermute x42, starting transfers between devices, to_heads(): lax.ppermute(value, 'heads', [(i, (i + step) % count) for i in range(coun...  47.7 us
    unnamed x131, local copies, waits for them, and re-layouts  28.2 us
    pallas_call x4, Pallas kernels, call_once(): pl.pallas_call(kernel, in_specs=[pl.BlockSpec(memory_space=pltpu.VMEM)] *...  18.6 us
  transfers between devices with their start and end apart: 87, of which 43 were waited for; matrix products, arithmetic and copies ran while one was open for 15% of the time, Pallas kernels for 16%

profile of v2, /device:TPU:9, one launch (start us, length us, event | category | flops | bytes accessed | tf_op | source)
XLA Modules:
  0.0 493.5 jit_solution(2721879194728927948)
XLA Ops:
  2.0 6.8 %concatenate.92 = bf16[1920]{0:T(1024)(128)(2,1)S(1)} concatenate(bf16[192]{0:T(256)(128)(2,1)} %param.29, bf16[192]{0:T(256)(128)(2,1)} %param.30, bf16[192]{0:T(256)(128)(2,1)} %param.31, bf16[192]{0:T(256)(128)(2,1)} %param.35, bf16[192]{0:T(256)(128)(2,1)} %param.36, bf16[192]{0:T(256)(128)(2,1)} %param.37, bf16[192]{0:T(256)(128)(2,1)} %param.41, bf16[192]{0:T(256)(128)(2,1)} %param.42, ...), dimensions={0} | concatenate | bytes 7680 | tf_op jit(solution)/shard_map/concatenate | solution.py:769
  24.0 5.8 %collective-permute-done.23 = bf16[2,96,768]{2,1,0:T(8,128)(2,1)S(1)} collective-permute-done((bf16[2,96,768]{2,1,0:T(8,128)(2,1)S(1)}, bf16[2,96,768]{2,1,0:T(8,128)(2,1)S(1)}, u32[]{:S(2)}, u32[]{:S(2)}) %collective-permute-start.23) | collective-permute-done | bytes 294944 | tf_op jit(solution)/shard_map/ppermute | solution.py:39
  29.9 11.2 %collective-permute-done.22 = bf16[2,96,768]{2,1,0:T(8,128)(2,1)S(1)} collective-permute-done((bf16[2,96,768]{2,1,0:T(8,128)(2,1)S(1)}, bf16[2,96,768]{2,1,0:T(8,128)(2,1)S(1)}, u32[]{:S(2)}, u32[]{:S(2)}) %collective-permute-start.22) | collective-permute-done | bytes 294944 | tf_op jit(solution)/shard_map/ppermute | solution.py:39
  41.2 8.8 %collective-permute-done.21 = bf16[2,96,768]{2,1,0:T(8,128)(2,1)S(1)} collective-permute-done((bf16[2,96,768]{2,1,0:T(8,128)(2,1)S(1)}, bf16[2,96,768]{2,1,0:T(8,128)(2,1)S(1)}, u32[]{:S(2)}, u32[]{:S(2)}) %collective-permute-start.21) | collective-permute-done | bytes 294944 | tf_op jit(solution)/shard_map/ppermute | solution.py:39
  53.7 7.0 %collective-permute-done.26 = bf16[3,2,48,768]{3,2,1,0:T(8,128)(2,1)S(1)} collective-permute-done((bf16[3,2,48,768]{3,2,1,0:T(8,128)(2,1)S(1)}, bf16[3,2,48,768]{3,2,1,0:T(8,128)(2,1)S(1)}, u32[]{:S(2)}, u32[]{:S(2)}) %collective-permute-start.26) | collective-permute-done | bytes 442400 | tf_op jit(solution)/shard_map/ppermute | solution.py:44
  79.1 4.3 collective-permute-done.14
  94.1 5.1 %collective-permute-done.18 = bf16[3,1,48,768]{3,2,0,1:T(8,128)(2,1)S(1)} collective-permute-done((bf16[3,1,48,768]{3,2,0,1:T(8,128)(2,1)S(1)}, bf16[3,1,48,768]{3,2,0,1:T(8,128)(2,1)S(1)}, u32[]{:S(2)}, u32[]{:S(2)}) %collective-permute-start.18) | collective-permute-done | bytes 221216 | tf_op jit(solution)/shard_map/ppermute | solution.py:44
  104.2 5.0 %collective-permute-done.19 = bf16[2,3,1,48,768]{4,3,1,0,2:T(8,128)(2,1)S(1)} collective-permute-done((bf16[2,3,1,48,768]{4,3,1,0,2:T(8,128)(2,1)S(1)}, bf16[2,3,1,48,768]{4,3,1,0,2:T(8,128)(2,1)S(1)}, u32[]{:S(2)}, u32[]{:S(2)}) %collective-permute-start.19) | collective-permute-done | bytes 442400 | tf_op jit(solution)/shard_map/ppermute | solution.py:44
  127.1 5.4 %shard_map.407 = (f32[64,768]{1,0:T(8,128)}, bf16[64,192]{1,0:T(8,128)(2,1)}, bf16[64,768]{1,0:T(8,128)(2,1)}, bf16[64,576]{1,0:T(8,128)(2,1)}, f32[3,64,64]{2,1...) custom-call(f32[16,1024]{1,0:T(8,128)} %copy-done.17, f32[16,1024]{1,0:T(8,128)} %copy-done.26, ...), custom_call_target="tpu_custom_call" | custom-call | bytes 2009856 | tf_op jit(solution)/shard_map/pallas_call | solution.py:614
  147.4 17.4 %shard_map.408 = (bf16[4,416,576]{2,1,0:T(8,128)(2,1)}, bf16[4,6,208,208]{3,2,1,0:T(8,128)(2,1)}, bf16[4,416,256]{2,1,0:T(8,128)(2,1)}, f32[416,768]{1,0:T(8,128...) custom-call(s32[2]{0:T(128)} %pad_add_fusion.scalars, bf16[2,197,192]{2,1,0:T(8,128)(2,1)} %copy.131.x0, ...), custom_call_target="tpu_custom_call" | custom-call | flops 1962934272 | bytes 13742080 | tf_op jit(solution)/shard_map/pallas_call | solution.py:598
  164.8 13.4 %shard_map.409 = (f32[4,416,768]{2,1,0:T(8,128)}, bf16[2,197,192]{2,1,0:T(8,128)(2,1)}, bf16[2,197,192]{2,1,0:T(8,128)(2,1)}, bf16[2,197,192]{2,1,0:T(8,128)(2,1...) custom-call(s32[2]{0:T(128)} %pad_add_fusion.scalars, f32[416,768]{1,0:T(8,128)} %get-tuple-element.79.s2_ref, ...), custom_call_target="tpu_custom_call" | custom-call | flops 3925868544 | bytes 23620608 | tf_op jit(solution)/shard_map/pallas_call | solution.py:598
  184.3 5.2 %collective-permute-start.35 = (f32[8,768]{1,0:T(8,128)S(1)}, f32[8,768]{1,0:T(8,128)S(1)}, u32[]{:S(2)}, u32[]{:S(2)}) collective-permute-start(f32[8,768]{1,0:T(8,128)S(1)} %add_add_fusion.3), channel_id=1, source_target_pairs={{0,4},{4,0},{8,12},{12,8},{16,20},{20,16},{24,28},{28,24},{1,5},{5... | collective-permute-start | bytes 73736 | tf_op jit(solution)/shard_map/ppermute | solution.py:44
  204.8 6.0 %collective-permute-done.40.u2 = bf16[2,197,192]{2,1,0:T(8,128)(2,1)S(1)} collective-permute-done((bf16[2,197,192]{2,1,0:T(8,128)(2,1)S(1)}, bf16[2,197,192]{2,1,0:T(8,128)(2,1)S(1)}, u32[]{:S(2)}, u32[]{:S(2)}) %collective-permute-start.40) | collective-permute-done | bytes 151328 | tf_op jit(solution)/shard_map/ppermute | solution.py:39
  214.6 25.6 %shard_map.412 = (bf16[4,2,2,2,96,768]{5,4,3,2,1,0:T(8,128)(2,1)}, bf16[4,2,2,2,96,768]{5,4,3,2,1,0:T(8,128)(2,1)}, f32[4,1,768]{2,1,0:T(1,128)}, f32[8,768]{1,0:T(8,128)}, f32[416,768]{1,0:T(8,128)}) custom-call(s32[2]{0:T(128)} %pad_add_fusion.scalars, bf16[2,197,192]{2,1,0:T(8,128)(2,1)} %copy.136.u0, bf16[2,197,192]{2,1,0:T(8,128)(2,1)} %copy-done.50, ...), custom_call_target="tpu_custom_call" | custom-call | flops 7851737088 | bytes 34360320 | tf_op jit(solution)/shard_map/pallas_call | solution.py:598
  240.2 4.9 copy.110
  246.3 21.1 %shard_map.413 = (bf16[4,416,768]{2,1,0:T(8,128)(2,1)}, f32[8,768]{1,0:T(8,128)}, f32[8,768]{1,0:T(8,128)}, f32[8,768]{1,0:T(8,128)}, f32[8,768]{1,0:T(8,128)}, ...) custom-call(s32[2]{0:T(128)} %pad_add_fusion.scalars, ...), custom_call_target="tpu_custom_call" | custom-call | flops 5888802816 | bytes 14662656 | tf_op jit(solution)/shard_map/pallas_call | solution.py:598
  269.7 9.1 %shard_map.417 = (bf16[4,1,2,2,96,768]{5,4,3,2,1,0:T(8,128)(2,1)}, bf16[4,1,2,2,96,768]{5,4,3,2,1,0:T(8,128)(2,1)}) custom-call(s32[2]{0:T(128)} %pad_add_fusion.scalars, f32[416,768]{1,0:T(8,128)} %get-tuple-element.88.g2_ref, bf16[416,768]{1,0:T(8,128)(2,1)} %get-tuple-element.118.normed, bf16[4,416,768]{2,1,0:T(8,128)(2,1)} %get-tuple-element.121.dproj, ...), custom_call_target="tpu_custom_call" | custom-call | flops 1962934272 | bytes 10043392 | tf_op jit(solution)/shard_map/pallas_call | solution.py:598
  284.7 12.3 %collective-permute-done.75 = bf16[4,2,2,48,768]{4,3,1,0,2:T(8,128)(2,1)S(1)} collective-permute-done((bf16[4,2,2,48,768]{4,3,1,0,2:T(8,128)(2,1)S(1)}, bf16[4,2,2,48,768]{4,3,1,0,2:T(8,128)(2,1)S(1)}, u32[]{:S(2)}, u32[]{:S(2)}) %collective-permute-start.75) | collective-permute-done | bytes 1179680 | tf_op jit(solution)/shard_map/ppermute | solution.py:44
  311.1 4.7 collective-permute-start.58
  319.1 5.2 %collective-permute-done.76 = bf16[4,2,48,768]{3,2,1,0:T(8,128)(2,1)S(1)} collective-permute-done((bf16[4,2,48,768]{3,2,1,0:T(8,128)(2,1)S(1)}, bf16[4,2,48,768]{3,2,1,0:T(8,128)(2,1)S(1)}, u32[]{:S(2)}, u32[]{:S(2)}) %collective-permute-start.76) | collective-permute-done | bytes 589856 | tf_op jit(solution)/shard_map/ppermute | solution.py:44
  345.8 7.3 %shard_map.414 = (f32[64,768]{1,0:T(8,128)}, f32[768,3,192]{2,1,0:T(4,128)}, f32[192,768]{1,0:T(8,128)}, f32[64,768]{1,0:T(8,128)}, bf16[64,768]{1,0:T(8,128)(2,1)}, /*index=5*/f32[1,768]{1,0:T(1,128)}, f32[3,192]{1,0:T(4,128)}) custom-call(f32[16,768]{1,0:T(8,128)} %copy-done.21, f32[16,768]{1,0:T(8,128)} %copy-done.32, f32[16,768]{1,0:T(8,128)} %copy-done.33, ...), custom_call_target="tpu_custom_call" | custom-call | bytes 4478208 | tf_op jit(solution)/shard_map/pallas_call | solution.py:614
  353.0 4.4 copy.129
  369.5 16.8 %collective-permute-done.80 = bf16[2,96,768]{2,1,0:T(8,128)(2,1)S(1)} collective-permute-done((bf16[2,96,768]{2,1,0:T(8,128)(2,1)S(1)}, bf16[2,96,768]{2,1,0:T(8,128)(2,1)S(1)}, u32[]{:S(2)}, u32[]{:S(2)}) %collective-permute-start.80) | collective-permute-done | bytes 294944 | tf_op jit(solution)/shard_map/ppermute | solution.py:39
  386.3 4.5 collective-permute-done.79
  409.9 9.1 %collective-permute-done.67 = bf16[1,96,768]{2,1,0:T(8,128)(2,1)S(1)} collective-permute-done((bf16[1,96,768]{2,1,0:T(8,128)(2,1)S(1)}, bf16[1,96,768]{2,1,0:T(8,128)(2,1)S(1)}, u32[]{:S(2)}, u32[]{:S(2)}) %collective-permute-start.67) | collective-permute-done | bytes 147488 | tf_op jit(solution)/shard_map/ppermute | solution.py:39
  420.7 5.0 %collective-permute-done.72 = bf16[1,48,768]{2,1,0:T(8,128)(2,1)S(1)} collective-permute-done((bf16[1,48,768]{2,1,0:T(8,128)(2,1)S(1)}, bf16[1,48,768]{2,1,0:T(8,128)(2,1)S(1)}, u32[]{:S(2)}, u32[]{:S(2)}) %collective-permute-start.72) | collective-permute-done | bytes 73760 | tf_op jit(solution)/shard_map/ppermute | solution.py:44
  429.4 8.8 %collective-permute-start.86 = (bf16[4,2,96,768]{3,2,1,0:T(8,128)(2,1)S(1)}, bf16[4,2,96,768]{3,2,1,0:T(8,128)(2,1)S(1)}, u32[]{:S(2)}, u32[]{:S(2)}) collective-permute-start(bf16[4,2,96,768]{3,2,1,0:T(8,128)(2,1)S(1)} %maximum_maximum_fusion.near), channel_id=1, source_target_pairs={{0,4},{4,0},{8,12},{12,8},{16,20},{20,16},{24,28},{28,24},{1,5},{5... | collective-permute-start | bytes 3538952 | tf_op jit(solution)/shard_map/ppermute | solution.py:44
  453.3 8.2 %collective-permute-done.42.p1 = bf16[2,197,192]{2,1,0:T(8,128)(2,1)} collective-permute-done((bf16[2,197,192]{2,1,0:T(8,128)(2,1)}, bf16[2,197,192]{2,1,0:T(8,128)(2,1)}, u32[]{:S(2)}, u32[]{:S(2)}) %collective-permute-start.42) | collective-permute-done | bytes 151328 | tf_op jit(solution)/shard_map/ppermute | solution.py:39
  461.5 4.4 collective-permute-done.43.p2
  475.0 5.5 %shard_map.418 = (f32[768,3,192]{2,1,0:T(4,128)}, f32[192,768]{1,0:T(8,128)}) custom-call(s32[2]{0:T(128)} %pad_add_fusion.scalars, bf16[4,1,96,768]{3,2,1,0:T(8,128)(2,1)} %copy-done.3, bf16[4,1,96,768]{3,2,1,0:T(8,128)(2,1)} %copy-done.15), custom_call_target="tpu_custom_call" | custom-call | bytes 3538944 | tf_op jit(solution)/shard_map/pallas_call | solution.py:598
  480.6 4.2 copy.130
  485.9 7.4 %shard_map.419 = (f32[768,768]{1,0:T(8,128)}, f32[768,768]{1,0:T(8,128)}) custom-call(s32[2]{0:T(128)} %pad_add_fusion.scalars, bf16[4,2,96,768]{3,2,1,0:T(8,128)(2,1)} %copy-done.1, bf16[4,2,96,768]{3,2,1,0:T(8,128)(2,1)} %copy-done.6), custom_call_target="tpu_custom_call" | custom-call | bytes 7077888 | tf_op jit(solution)/shard_map/pallas_call | solution.py:598
  (395 shorter events, 221.6 us)
Async XLA Ops:
  14.3 85.3 %collective-permute-start.5 = (f32[24,768]{1,0:T(8,128)}, f32[24,768]{1,0:T(8,128)}, u32[]{:S(2)}, u32[]{:S(2)}) collective-permute-start(f32[24,768]{1,0:T(8,128)} %concatenate.95), channel_id=1, source_target_pairs={{0,3},{1,0},{2,1},{3,2},{4,7},{5,4},{6,5},{7,6},{8,11},{9,8},{10,9... | collective-permute-start | bytes 221192 | tf_op jit(solution)/shard_map/ppermute | solution.py:39
  14.3 87.1 %collective-permute-start.4 = (f32[24,768]{1,0:T(8,128)}, f32[24,768]{1,0:T(8,128)}, u32[]{:S(2)}, u32[]{:S(2)}) collective-permute-start(f32[24,768]{1,0:T(8,128)} %concatenate.95), channel_id=1, source_target_pairs={{0,2},{1,3},{2,0},{3,1},{4,6},{5,7},{6,4},{7,5},{8,10},{9,11},{10,... | collective-permute-start | bytes 221192 | tf_op jit(solution)/shard_map/ppermute | solution.py:39
  18.9 22.2 %collective-permute-start.22 = (bf16[2,96,768]{2,1,0:T(8,128)(2,1)S(1)}, bf16[2,96,768]{2,1,0:T(8,128)(2,1)S(1)}, u32[]{:S(2)}, u32[]{:S(2)}) collective-permute-start(bf16[2,96,768]{2,1,0:T(8,128)(2,1)S(1)} %pad_maximum_fusion.10), channel_id=1, source_target_pairs={{0,2},{1,3},{2,0},{3,1},{4,6},{5,7},{6,4},{7,5},{8,10},{9,11},{10,... | collective-permute-start | bytes 884744 | tf_op jit(solution)/shard_map/ppermute | solution.py:39
  21.3 28.7 %collective-permute-start.21 = (bf16[2,96,768]{2,1,0:T(8,128)(2,1)S(1)}, bf16[2,96,768]{2,1,0:T(8,128)(2,1)S(1)}, u32[]{:S(2)}, u32[]{:S(2)}) collective-permute-start(bf16[2,96,768]{2,1,0:T(8,128)(2,1)S(1)} %pad_maximum_fusion.10), channel_id=1, source_target_pairs={{0,1},{1,2},{2,3},{3,0},{4,5},{5,6},{6,7},{7,4},{8,9},{9,10},{10,1... | collective-permute-start | bytes 884744 | tf_op jit(solution)/shard_map/ppermute | solution.py:39
  29.8 48.3 %collective-permute-start.15 = (bf16[1,96,768]{2,1,0:T(8,128)(2,1)}, bf16[1,96,768]{2,1,0:T(8,128)(2,1)}, u32[]{:S(2)}, u32[]{:S(2)}) collective-permute-start(bf16[1,96,768]{2,1,0:T(8,128)(2,1)} %fusion.39), channel_id=1, source_target_pairs={{0,3},{1,0},{2,1},{3,2},{4,7},{5,4},{6,5},{7,6},{8,11},{9,8},{10,9... | collective-permute-start | bytes 442376 | tf_op jit(solution)/shard_map/ppermute | solution.py:39
  61.6 24.0 %collective-permute-start.27 = (bf16[2,3,2,48,768]{4,3,2,1,0:T(8,128)(2,1)}, bf16[2,3,2,48,768]{4,3,2,1,0:T(8,128)(2,1)}, u32[]{:S(2)}, u32[]{:S(2)}) collective-permute-start(bf16[2,3,2,48,768]{4,3,2,1,0:T(8,128)(2,1)} %pad_maximum_fusion.4), channel_id=1, source_target_pairs={{0,8},{4,12},{8,0},{12,4},{16,24},{20,28},{24,16},{28,20},{1,9},{5... | collective-permute-start | bytes 2654216 | tf_op jit(solution)/shard_map/ppermute | solution.py:44
  63.8 23.1 %collective-permute-start.25 = (bf16[2,3,2,48,768]{4,3,2,1,0:T(8,128)(2,1)}, bf16[2,3,2,48,768]{4,3,2,1,0:T(8,128)(2,1)}, u32[]{:S(2)}, u32[]{:S(2)}) collective-permute-start(bf16[2,3,2,48,768]{4,3,2,1,0:T(8,128)(2,1)} %pad_maximum_fusion.3), channel_id=1, source_target_pairs={{0,16},{4,20},{8,24},{12,28},{16,0},{20,4},{24,8},{28,12},{1,17},{... | collective-permute-start | bytes 2654216 | tf_op jit(solution)/shard_map/ppermute | solution.py:44
  88.7 76.0 %collective-permute-start.28 = (bf16[2,4,3,2,48,768]{5,4,3,2,1,0:T(8,128)(2,1)S(1)}, bf16[2,4,3,2,48,768]{5,4,3,2,1,0:T(8,128)(2,1)}, u32[]{:S(2)}, u32[]{:S(2)}) collective-permute-start(bf16[2,4,3,2,48,768]{5,4,3,2,1,0:T(8,128)(2,1)S(1)} %pad_maximum_fusion.fc_near.proj_near), channel_id=1, source_target_pairs={{0,4},{4,0},{8,12},{12,8},{16,20},{20,16},{24,28},{28,24},{1,5},{5... | collective-permute-start | bytes 10616840 | tf_op jit(solution)/shard_map/ppermute | solution.py:44
  110.8 36.6 %collective-permute-start.20 = (bf16[2,4,3,1,48,768]{5,4,3,2,1,0:T(8,128)(2,1)}, bf16[2,4,3,1,48,768]{5,4,3,2,1,0:T(8,128)(2,1)}, u32[]{:S(2)}, u32[]{:S(2)}) collective-permute-start(bf16[2,4,3,1,48,768]{5,4,3,2,1,0:T(8,128)(2,1)} %pad_maximum_fusion.1.near), channel_id=1, source_target_pairs={{0,4},{4,0},{8,12},{12,8},{16,20},{20,16},{24,28},{28,24},{1,5},{5... | collective-permute-start | bytes 5308424 | tf_op jit(solution)/shard_map/ppermute | solution.py:44
  124.4 16.7 %collective-permute-start.1 = (bf16[2,197,192]{2,1,0:T(8,128)(2,1)}, bf16[2,197,192]{2,1,0:T(8,128)(2,1)}, u32[]{:S(2)}, u32[]{:S(2)}) collective-permute-start(bf16[2,197,192]{2,1,0:T(8,128)(2,1)} %copy.133), channel_id=1, source_target_pairs={{0,2},{1,3},{2,0},{3,1},{4,6},{5,7},{6,4},{7,5},{8,10},{9,11},{10,... | collective-permute-start | bytes 453896 | tf_op jit(solution)/shard_map/ppermute | solution.py:39
  125.0 19.2 %collective-permute-start.2 = (bf16[2,197,192]{2,1,0:T(8,128)(2,1)}, bf16[2,197,192]{2,1,0:T(8,128)(2,1)}, u32[]{:S(2)}, u32[]{:S(2)}) collective-permute-start(bf16[2,197,192]{2,1,0:T(8,128)(2,1)} %copy.134), channel_id=1, source_target_pairs={{0,3},{1,0},{2,1},{3,2},{4,7},{5,4},{6,5},{7,6},{8,11},{9,8},{10,9... | collective-permute-start | bytes 453896 | tf_op jit(solution)/shard_map/ppermute | solution.py:39
  194.0 16.8 %collective-permute-start.40 = (bf16[2,197,192]{2,1,0:T(8,128)(2,1)S(1)}, bf16[2,197,192]{2,1,0:T(8,128)(2,1)S(1)}, u32[]{:S(2)}, u32[]{:S(2)}) collective-permute-start(bf16[2,197,192]{2,1,0:T(8,128)(2,1)S(1)} %copy.138), channel_id=1, source_target_pairs={{0,2},{1,3},{2,0},{3,1},{4,6},{5,7},{6,4},{7,5},{8,10},{9,11},{10,... | collective-permute-start | bytes 453896 | tf_op jit(solution)/shard_map/ppermute | solution.py:39
  196.9 17.0 %collective-permute-start.41 = (bf16[2,197,192]{2,1,0:T(8,128)(2,1)S(1)}, bf16[2,197,192]{2,1,0:T(8,128)(2,1)S(1)}, u32[]{:S(2)}, u32[]{:S(2)}) collective-permute-start(bf16[2,197,192]{2,1,0:T(8,128)(2,1)S(1)} %copy.139), channel_id=1, source_target_pairs={{0,3},{1,0},{2,1},{3,2},{4,7},{5,4},{6,5},{7,6},{8,11},{9,8},{10,9... | collective-permute-start | bytes 453896 | tf_op jit(solution)/shard_map/ppermute | solution.py:39
  245.2 22.3 %collective-permute-start.61 = (bf16[4,2,2,2,96,768]{5,4,1,0,3,2:T(8,128)(2,1)}, bf16[4,2,2,2,96,768]{5,4,1,0,3,2:T(8,128)(2,1)}, u32[]{:S(2)}, u32[]{:S(2)}) collective-permute-start(bf16[4,2,2,2,96,768]{5,4,1,0,3,2:T(8,128)(2,1)} %copy.110), channel_id=1, source_target_pairs={{0,4},{4,0},{8,12},{12,8},{16,20},{20,16},{24,28},{28,24},{1,5},{5... | collective-permute-start | bytes 14155784 | tf_op jit(solution)/shard_map/ppermute | solution.py:44
  269.4 27.6 %collective-permute-start.75 = (bf16[4,2,2,48,768]{4,3,1,0,2:T(8,128)(2,1)S(1)}, bf16[4,2,2,48,768]{4,3,1,0,2:T(8,128)(2,1)S(1)}, u32[]{:S(2)}, u32[]{:S(2)}) collective-permute-start(bf16[4,2,2,48,768]{4,3,1,0,2:T(8,128)(2,1)S(1)} %fusion), channel_id=1, source_target_pairs={{0,8},{4,12},{8,0},{12,4},{16,24},{20,28},{24,16},{28,20},{1,9},{5... | collective-permute-start | bytes 3538952 | tf_op jit(solution)/shard_map/ppermute | solution.py:44
  282.1 75.4 %collective-permute-start.62 = (bf16[4,1,2,2,96,768]{5,4,0,3,2,1:T(8,128)(2,1)}, bf16[4,1,2,2,96,768]{5,4,0,3,2,1:T(8,128)(2,1)}, u32[]{:S(2)}, u32[]{:S(2)}) collective-permute-start(bf16[4,1,2,2,96,768]{5,4,0,3,2,1:T(8,128)(2,1)} %copy.112), channel_id=1, source_target_pairs={{0,4},{4,0},{8,12},{12,8},{16,20},{20,16},{24,28},{28,24},{1,5},{5... | collective-permute-start | bytes 7077896 | tf_op jit(solution)/shard_map/ppermute | solution.py:44
  284.3 33.1 %collective-permute-start.77 = (bf16[4,2,2,48,768]{4,3,1,0,2:T(8,128)(2,1)S(1)}, bf16[4,2,2,48,768]{4,3,1,0,2:T(8,128)(2,1)S(1)}, u32[]{:S(2)}, u32[]{:S(2)}) collective-permute-start(bf16[4,2,2,48,768]{4,3,1,0,2:T(8,128)(2,1)S(1)} %fusion.1), channel_id=1, source_target_pairs={{0,16},{4,20},{8,24},{12,28},{16,0},{20,4},{24,8},{28,12},{1,17},{... | collective-permute-start | bytes 3538952 | tf_op jit(solution)/shard_map/ppermute | solution.py:44
  298.4 25.9 %collective-permute-start.76 = (bf16[4,2,48,768]{3,2,1,0:T(8,128)(2,1)S(1)}, bf16[4,2,48,768]{3,2,1,0:T(8,128)(2,1)S(1)}, u32[]{:S(2)}, u32[]{:S(2)}) collective-permute-start(bf16[4,2,48,768]{3,2,1,0:T(8,128)(2,1)S(1)} %fusion.5), channel_id=1, source_target_pairs={{0,16},{4,20},{8,24},{12,28},{16,0},{20,4},{24,8},{28,12},{1,17},{... | collective-permute-start | bytes 1769480 | tf_op jit(solution)/shard_map/ppermute | solution.py:44
  309.3 19.5 %collective-permute-start.29 = (bf16[2,197,192]{2,1,0:T(8,128)(2,1)S(1)}, bf16[2,197,192]{2,1,0:T(8,128)(2,1)S(1)}, u32[]{:S(2)}, u32[]{:S(2)}) collective-permute-start(bf16[2,197,192]{2,1,0:T(8,128)(2,1)S(1)} %copy-done.49), channel_id=1, source_target_pairs={{0,1},{1,2},{2,3},{3,0},{4,5},{5,6},{6,7},{7,4},{8,9},{9,10},{10,1... | collective-permute-start | bytes 453896 | tf_op jit(solution)/shard_map/ppermute | solution.py:39
  328.8 31.1 %collective-permute-start.78 = (bf16[4,2,48,768]{3,2,1,0:T(8,128)(2,1)S(1)}, bf16[4,2,48,768]{3,2,1,0:T(8,128)(2,1)}, u32[]{:S(2)}, u32[]{:S(2)}) collective-permute-start(bf16[4,2,48,768]{3,2,1,0:T(8,128)(2,1)S(1)} %get-tuple-element.178), channel_id=1, source_target_pairs={{0,8},{4,12},{8,0},{12,4},{16,24},{20,28},{24,16},{28,20},{1,9},{5... | collective-permute-start | bytes 1769480 | tf_op jit(solution)/shard_map/ppermute | solution.py:44
  344.6 20.3 %collective-permute-start.60 = (f32[8,768]{1,0:T(8,128)}, f32[8,768]{1,0:T(8,128)}, u32[]{:S(2)}, u32[]{:S(2)}) collective-permute-start(f32[8,768]{1,0:T(8,128)} %add.344), channel_id=1, source_target_pairs={{0,16},{4,20},{8,24},{12,28},{16,0},{20,4},{24,8},{28,12},{1,17},{... | collective-permute-start | bytes 73736 | tf_op jit(solution)/shard_map/ppermute | solution.py:44
  358.7 32.3 %collective-permute-start.63 = (bf16[4,1,2,48,768]{4,3,0,2,1:T(8,128)(2,1)S(1)}, bf16[4,1,2,48,768]{4,3,0,2,1:T(8,128)(2,1)S(1)}, u32[]{:S(2)}, u32[]{:S(2)}) collective-permute-start(bf16[4,1,2,48,768]{4,3,0,2,1:T(8,128)(2,1)S(1)} %fusion.8), channel_id=1, source_target_pairs={{0,8},{4,12},{8,0},{12,4},{16,24},{20,28},{24,16},{28,20},{1,9},{5... | collective-permute-start | bytes 1769480 | tf_op jit(solution)/shard_map/ppermute | solution.py:44
  361.8 24.5 %collective-permute-start.80 = (bf16[2,96,768]{2,1,0:T(8,128)(2,1)S(1)}, bf16[2,96,768]{2,1,0:T(8,128)(2,1)S(1)}, u32[]{:S(2)}, u32[]{:S(2)}) collective-permute-start(bf16[2,96,768]{2,1,0:T(8,128)(2,1)S(1)} %get-tuple-element.181), channel_id=1, source_target_pairs={{0,2},{1,3},{2,0},{3,1},{4,6},{5,7},{6,4},{7,5},{8,10},{9,11},{10,... | collective-permute-start | bytes 884744 | tf_op jit(solution)/shard_map/ppermute | solution.py:39
  362.3 28.5 %collective-permute-start.79 = (bf16[2,96,768]{2,1,0:T(8,128)(2,1)S(1)}, bf16[2,96,768]{2,1,0:T(8,128)(2,1)S(1)}, u32[]{:S(2)}, u32[]{:S(2)}) collective-permute-start(bf16[2,96,768]{2,1,0:T(8,128)(2,1)S(1)} %get-tuple-element.179), channel_id=1, source_target_pairs={{0,3},{1,0},{2,1},{3,2},{4,7},{5,4},{6,5},{7,6},{8,11},{9,8},{10,9... | collective-permute-start | bytes 884744 | tf_op jit(solution)/shard_map/ppermute | solution.py:39
  364.9 28.5 %collective-permute-start.65 = (bf16[4,1,2,48,768]{4,3,0,2,1:T(8,128)(2,1)S(1)}, bf16[4,1,2,48,768]{4,3,0,2,1:T(8,128)(2,1)S(1)}, u32[]{:S(2)}, u32[]{:S(2)}) collective-permute-start(bf16[4,1,2,48,768]{4,3,0,2,1:T(8,128)(2,1)S(1)} %fusion.9), channel_id=1, source_target_pairs={{0,16},{4,20},{8,24},{12,28},{16,0},{20,4},{24,8},{28,12},{1,17},{... | collective-permute-start | bytes 1769480 | tf_op jit(solution)/shard_map/ppermute | solution.py:44
  369.2 76.1 %collective-permute-start.52 = (bf16[64,768]{1,0:T(8,128)(2,1)S(1)}, bf16[64,768]{1,0:T(8,128)(2,1)S(1)}, u32[]{:S(2)}, u32[]{:S(2)}) collective-permute-start(bf16[64,768]{1,0:T(8,128)(2,1)S(1)} %copy-done.53), channel_id=1, source_target_pairs={{0,1},{1,2},{2,3},{3,0},{4,5},{5,6},{6,7},{7,4},{8,9},{9,10},{10,1... | collective-permute-start | bytes 294920 | tf_op jit(solution)/shard_map/ppermute | solution.py:39
  405.5 42.5 %collective-permute-start.53 = (bf16[64,768]{1,0:T(8,128)(2,1)S(1)}, bf16[64,768]{1,0:T(8,128)(2,1)S(1)}, u32[]{:S(2)}, u32[]{:S(2)}) collective-permute-start(bf16[64,768]{1,0:T(8,128)(2,1)S(1)} %copy-done.53), channel_id=1, source_target_pairs={{0,2},{1,3},{2,0},{3,1},{4,6},{5,7},{6,4},{7,5},{8,10},{9,11},{10,... | collective-permute-start | bytes 294920 | tf_op jit(solution)/shard_map/ppermute | solution.py:39
  407.5 40.5 %collective-permute-start.54 = (bf16[64,768]{1,0:T(8,128)(2,1)S(1)}, bf16[64,768]{1,0:T(8,128)(2,1)S(1)}, u32[]{:S(2)}, u32[]{:S(2)}) collective-permute-start(bf16[64,768]{1,0:T(8,128)(2,1)S(1)} %copy-done.53), channel_id=1, source_target_pairs={{0,3},{1,0},{2,1},{3,2},{4,7},{5,4},{6,5},{7,6},{8,11},{9,8},{10,9... | collective-permute-start | bytes 294920 | tf_op jit(solution)/shard_map/ppermute | solution.py:39
  429.4 55.4 %collective-permute-start.86 = (bf16[4,2,96,768]{3,2,1,0:T(8,128)(2,1)S(1)}, bf16[4,2,96,768]{3,2,1,0:T(8,128)(2,1)S(1)}, u32[]{:S(2)}, u32[]{:S(2)}) collective-permute-start(bf16[4,2,96,768]{3,2,1,0:T(8,128)(2,1)S(1)} %maximum_maximum_fusion.near), channel_id=1, source_target_pairs={{0,4},{4,0},{8,12},{12,8},{16,20},{20,16},{24,28},{28,24},{1,5},{5... | collective-permute-start | bytes 3538952 | tf_op jit(solution)/shard_map/ppermute | solution.py:44
  442.3 31.9 %collective-permute-start.74 = (bf16[4,1,96,768]{3,2,1,0:T(8,128)(2,1)S(1)}, bf16[4,1,96,768]{3,2,1,0:T(8,128)(2,1)S(1)}, u32[]{:S(2)}, u32[]{:S(2)}) collective-permute-start(bf16[4,1,96,768]{3,2,1,0:T(8,128)(2,1)S(1)} %maximum_maximum_fusion.1.near), channel_id=1, source_target_pairs={{0,4},{4,0},{8,12},{12,8},{16,20},{20,16},{24,28},{28,24},{1,5},{5... | collective-permute-start | bytes 1769480 | tf_op jit(solution)/shard_map/ppermute | solution.py:44
  448.0 17.9 %collective-permute-start.43 = (bf16[2,197,192]{2,1,0:T(8,128)(2,1)}, bf16[2,197,192]{2,1,0:T(8,128)(2,1)}, u32[]{:S(2)}, u32[]{:S(2)}) collective-permute-start(bf16[2,197,192]{2,1,0:T(8,128)(2,1)} %get-tuple-element.96), channel_id=1, source_target_pairs={{0,2},{1,3},{2,0},{3,1},{4,6},{5,7},{6,4},{7,5},{8,10},{9,11},{10,... | collective-permute-start | bytes 453896 | tf_op jit(solution)/shard_map/ppermute | solution.py:39
  448.0 18.9 %collective-permute-start.44 = (bf16[2,197,192]{2,1,0:T(8,128)(2,1)}, bf16[2,197,192]{2,1,0:T(8,128)(2,1)}, u32[]{:S(2)}, u32[]{:S(2)}) collective-permute-start(bf16[2,197,192]{2,1,0:T(8,128)(2,1)} %get-tuple-element.97), channel_id=1, source_target_pairs={{0,3},{1,0},{2,1},{3,2},{4,7},{5,4},{6,5},{7,6},{8,11},{9,8},{10,9... | collective-permute-start | bytes 453896 | tf_op jit(solution)/shard_map/ppermute | solution.py:39
  (113 other events, 1158.9 us)

commit v3 on v2

v3 whole, which is shorter than its diff:
```python
import functools

import jax
import jax.numpy as jnp
from jax import lax
from jax.experimental import pallas as pl
from jax.experimental.pallas import tpu as pltpu
from jax.sharding import PartitionSpec as P

HS = 64
GROUP = 8

norm_eps = 1e-05
score_scale = 0.125
gelu_rate = 1.702
contrast_sharpness = 0.02
masked_score = -1000000000.0
exact = lax.Precision.HIGHEST
f32 = jnp.float32
bf16 = jnp.bfloat16

PIECES = ((0, 2, 4, 6), (0, 4, 2, 6))


def nn(left, right):
    return lax.dot_general(left, right, (((1,), (0,)), ((), ())), preferred_element_type=f32)


def nt(left, right):
    return lax.dot_general(left, right, (((1,), (1,)), ((), ())), preferred_element_type=f32)


def tn(left, right):
    return lax.dot_general(left, right, (((0,), (0,)), ((), ())), preferred_element_type=f32)


def to_heads(value, step):
    count = lax.axis_size("heads")
    return lax.ppermute(value, "heads", [(i, (i + step) % count) for i in range(count)])


def swap_frames(value, bit):
    count = lax.axis_size("frames")
    return lax.ppermute(value, "frames", [(i, i ^ bit) for i in range(count)])


def frame_bits(start=1):
    count = lax.axis_size("frames")
    bits = []
    bit = start
    while bit < count:
        bits.append(bit)
        bit *= 2
    return bits


def norm_stats(rows):
    center = jnp.mean(rows, axis=-1, keepdims=True)
    offset = rows - center
    factor = lax.rsqrt(jnp.mean(offset * offset, axis=-1, keepdims=True) + norm_eps)
    return offset * factor, factor


def norm_back(grad_out, normed, factor, gain):
    scaled = grad_out * gain
    first = jnp.mean(scaled, axis=-1, keepdims=True)
    second = jnp.mean(scaled * normed, axis=-1, keepdims=True)
    grad_in = factor * (scaled - first - normed * second)
    return (
        grad_in,
        jnp.sum(grad_out * normed, axis=0, keepdims=True),
        jnp.sum(grad_out, axis=0, keepdims=True),
    )


def place_weight(target, own, near, far, place, slot):
    block = target.shape[0] // GROUP
    half = block // 2

    @pl.when(slot == 0)
    def _():
        target[...] = own[...]

    @pl.when(slot > 0)
    def _():
        for q in range(2):
            for j in range(4):
                here = (place ^ PIECES[q][j]) * block + q * half
                there = (place ^ PIECES[q][j] ^ 1) * block + q * half
                target[pl.ds(pl.multiple_of(here, 16), half), :] = near[q, j]
                target[pl.ds(pl.multiple_of(there, 16), half), :] = far[q, j]


def pick_rows(array, first, count):
    row = lax.broadcasted_iota(jnp.int32, (array.shape[0], 1), 0)
    return [
        jnp.sum(jnp.where(row == first + i, array, 0.0), axis=0, keepdims=True)
        for i in range(count)
    ]


def put_rows(rows, first, total):
    row = lax.broadcasted_iota(jnp.int32, (total, 1), 0)
    value = jnp.zeros((total, rows[0].shape[1]), f32)
    for i, line in enumerate(rows):
        value = jnp.where(row == first + i, line, value)
    return value


def contrast(
    p0, p1, p2, p3, ids_row, ids_col, group_col, group_row, loss_out, grad_out, *, videos, block
):
    each = p0.shape[0]
    padded = group_col.shape[0]
    video = lax.broadcasted_iota(jnp.int32, (padded, 1), 0)
    onehot = (ids_row[...] == video).astype(f32)
    counts = jnp.sum(onehot, axis=1, keepdims=True)
    counts = jnp.where(video < videos, counts, 1.0)
    pooled = None
    for j, piece in enumerate((p0, p1, p2, p3)):
        hot = (ids_row[:, j * each : (j + 1) * each] == video).astype(f32)
        term = jnp.dot(hot, piece[...], precision=exact, preferred_element_type=f32)
        pooled = term if pooled is None else pooled + term
    pooled = pooled / counts
    scale = lax.rsqrt(jnp.sum(pooled * pooled, axis=1, keepdims=True) + 1e-06)
    unit = pooled * scale
    logits = (
        lax.dot_general(
            unit, unit, (((1,), (1,)), ((), ())), precision=exact, preferred_element_type=f32
        )
        / contrast_sharpness
    )
    other = lax.broadcasted_iota(jnp.int32, (padded, padded), 1)
    this = lax.broadcasted_iota(jnp.int32, (padded, padded), 0)
    usable = jnp.logical_and(other != this, other < videos)
    logits = jnp.where(usable, logits, masked_score)
    top = jnp.max(logits, axis=1, keepdims=True)
    powers = jnp.exp(logits - top)
    total = jnp.sum(powers, axis=1, keepdims=True)
    log_total = top + jnp.log(total)
    real = jnp.logical_and(usable, this < videos)
    positive = jnp.where(
        jnp.logical_and(group_col[...] == group_row[...], real), 1.0, 0.0
    )
    weights = positive / jnp.maximum(jnp.sum(positive, axis=1, keepdims=True), 1.0)
    each_loss = jnp.where(real, weights * (log_total - logits), 0.0)
    loss_out[...] = jnp.sum(jnp.sum(each_loss, axis=1, keepdims=True), axis=0, keepdims=True)
    g_logits = jnp.sum(weights, axis=1, keepdims=True) * (powers / total) - weights
    g_logits = jnp.where(real, g_logits, 0.0)
    g_unit = jnp.dot(g_logits, unit, precision=exact, preferred_element_type=f32)
    g_unit = g_unit + lax.dot_general(
        g_logits, unit, (((0,), (0,)), ((), ())), precision=exact, preferred_element_type=f32
    )
    g_unit = g_unit / contrast_sharpness
    inner = jnp.sum(pooled * g_unit, axis=1, keepdims=True)
    g_pooled = scale * g_unit - scale * scale * scale * inner * pooled
    hot = (ids_col[:block, :] == lax.broadcasted_iota(jnp.int32, (block, padded), 1)).astype(f32)
    grad_out[...] = jnp.dot(hot, g_pooled / counts, precision=exact, preferred_element_type=f32)


def spread_grad(keep, send, matrix, slot_value, place):
    block = slot_value.shape[0] // GROUP
    for owner in range(GROUP):
        part = slot_value[owner * block : (owner + 1) * block].astype(bf16)
        offset = place ^ owner
        rest = offset // 2
        mine = offset % 2 == 0

        @pl.when(mine)
        def _():
            keep[rest % 2, rest // 2, matrix, 0:block, :] = part

        @pl.when(jnp.logical_not(mine))
        def _():
            send[rest % 2, rest // 2, matrix, 0:block, :] = part


def join_features(pieces, own, i, head_index, turned, tokens):
    local, patches = own.shape[1:]
    count = turned.shape[0] // local
    for s in range(count):
        block = (head_index - s + count) % count
        value = own[i] if s == 0 else pieces(s, i)
        turned[pl.ds(pl.multiple_of(block * local, 64), local), 0:patches] = value
    token = lax.broadcasted_iota(jnp.int32, (tokens, 1), 0)
    return jnp.where(token < patches, turned[...].T[:tokens], 0)


def split_features(value, pieces, i, head_index, turned):
    local, patches = pieces[0].shape[1:]
    turned[:, 0 : value.shape[0]] = value.T
    for s, piece in enumerate(pieces):
        block = (head_index + s) % len(pieces)
        piece[i] = turned[pl.ds(pl.multiple_of(block * local, 64), local), 0:patches]


SMALL = 32


def pack_first(
    scalars, x, fc, qkv, out, b0, b1, b2, b3, b4, b5, b6, b7, b8, b9, qv, fcb,
    weight, cls, s1, s2, s3,
):
    head_index, place = scalars[0], scalars[1]
    block, local, patches = x.shape
    width = fc.shape[1]
    slots = width // local
    rows = width // GROUP
    for c in range(3):
        weight[c * local : (c + 1) * local, :] = qkv[c]
    weight[3 * local :, :] = out[...]
    lane = lax.broadcasted_iota(jnp.int32, (1, width), 1) // local
    zero = jnp.zeros((1, local), f32)
    starts = []
    for f in range(block):
        part = x[f, :, 0:128]
        starts.append(tn(part, fc[...])[0:1])
        cls[f : f + 1, :] = part.T[0:1].astype(f32)
    start = jnp.concatenate(starts, axis=0)
    high = start.astype(bf16).astype(f32)
    lines = [high, start - high]
    for vec in (b0, b1, b2, b3, b4, b5, b6, b7, b8, b9):
        value = vec[...].reshape(1, local).astype(f32)
        lines.append(jnp.where(lane == head_index, jnp.concatenate([value] * slots, axis=1), 0.0))
    lines.append(fcb[...].reshape(1, width).astype(f32))
    lines.append(
        jnp.concatenate([qv[0:1, :].astype(f32), zero, qv[1:2, :].astype(f32), zero], axis=1)
    )
    lines.append(jnp.zeros((SMALL - 2 * block - 12, width), f32))
    small = jnp.concatenate(lines, axis=0).astype(bf16)
    mine = weight[pl.ds(pl.multiple_of(place * rows, 32), rows), :]
    third = 2 * local // 3
    for step, send in enumerate((s1, s2, s3)):
        send[0:SMALL, :] = small
        send[SMALL : SMALL + rows, :] = mine
        first = ((head_index + step + 1) % slots) * 2
        base = SMALL + rows
        rest = local - third
        send[base : base + third, 0:patches] = x[first, 0:third, :]
        send[base : base + rest, 256 : 256 + patches] = x[first, third:local, :]
        send[base + rest : base + third, 256 : 256 + patches] = x[first + 1, 0 : third - rest, :]
        send[base : base + third, 512 : 512 + patches] = x[first + 1, third - rest : local, :]


def unpack_first(
    scalars, x, cls, own, r1, r2, r3,
    nat, fc_bias, qkv_bias, sent, first_half, second_half, stream, turned, *, block, tokens,
):
    head_index = scalars[0]
    frames, local, patches = x.shape
    width = own.shape[1]
    rows = width // GROUP
    received = (own, r1, r2, r3)
    start = None
    vectors = None
    for s, piece in enumerate(received):
        small = piece[0:SMALL, :].astype(f32)
        value = small[0:block] + small[block : 2 * block]
        vec = small[2 * block : 2 * block + 10]
        start = value if start is None else start + value
        vectors = vec if vectors is None else vectors + vec
        fc_bias[s] = small[2 * block + 10 : 2 * block + 11]
        qkv_bias[s] = small[2 * block + 11 : 2 * block + 12, : 3 * local]
    nat[0:10, :] = vectors
    nat[10:16, :] = jnp.zeros((6, width), f32)
    sent[:, 0:width] = start + vectors[0:1]
    sent[:, width : width + local] = cls[...]
    sent[:, width + local :] = jnp.zeros((block, sent.shape[1] - width - local), f32)
    for s in range(1, len(received)):
        piece = received[s]
        first_half[s - 1, 0] = piece[SMALL : SMALL + rows // 2, :]
        second_half[s - 1, 0] = piece[SMALL + rows // 2 : SMALL + rows, :]
    base = SMALL + rows
    third = 2 * local // 3
    rest = local - third

    def pieces(s, i):
        piece = received[s]
        if i == 0:
            low = piece[base : base + third, 0:patches]
            high = piece[base : base + rest, 256 : 256 + patches]
        else:
            low = piece[base + rest : base + third, 256 : 256 + patches]
            high = piece[base : base + third, 512 : 512 + patches]
        return jnp.concatenate([low, high], axis=0)

    for i in range(frames):
        stream[i * tokens : (i + 1) * tokens, :] = join_features(
            pieces, x, i, head_index, turned, tokens
        )


def message_forward(
    p0, p1, p2, p3, ids_col, ids_row, nat, weight, qv, courier,
    start_out, cls_out, rows_out, proj_out, probs_out, ctx_out, part_out, *, heads, block,
):
    width = nat.shape[1]
    local = heads * HS
    each = p0.shape[0]
    for j, piece in enumerate((p0, p1, p2, p3)):
        span = pl.ds(j * each, each)
        start_out[span, :] = piece[:, :width]
        cls_out[span, :] = piece[:, width : width + local].astype(bf16)
    base, _ = norm_stats(start_out[...])
    rows = (base * nat[1:2, :] + nat[2:3, :]).astype(bf16)
    rows_out[...] = rows
    bias = (qv[0:1, :].astype(f32), jnp.zeros((1, local), f32), qv[1:2, :].astype(f32))
    proj = [(nt(rows, weight[c]) + bias[c]).astype(bf16) for c in range(3)]
    proj_out[...] = jnp.concatenate(proj, axis=1)
    same = ids_col[...] == ids_row[...]
    context = []
    for j in range(heads):
        q, k, v = [p[:, j * HS : (j + 1) * HS] for p in proj]
        scores = jnp.where(same, nt(q, k) * score_scale, masked_score)
        scores = jnp.exp(scores - jnp.max(scores, axis=-1, keepdims=True))
        probs = scores / jnp.sum(scores, axis=-1, keepdims=True)
        probs_out[j] = probs
        context.append(nn(probs.astype(bf16), v).astype(bf16))
    context = jnp.concatenate(context, axis=1)
    ctx_out[...] = context
    part_out[...] = nn(context[:16], courier[...])[:block]


def message_back_one(
    scalars, p0, p1, p2, p3, rows, proj, probs_ref, ctx, weight, courier,
    grad_out, weight_out, courier_out, back_out, send_out, bias_out, qv_out, *, heads,
):
    local = heads * HS
    each = p0.shape[0]
    for j, piece in enumerate((p0, p1, p2, p3)):
        grad_out[pl.ds(j * each, each), :] = piece[...]
    grad = grad_out[...].astype(bf16)
    bias_out[...] = own_part(
        jnp.sum(grad.astype(f32), axis=0, keepdims=True), local, scalars[0]
    ).reshape(local)
    courier_out[...] = tn(ctx[...], grad)
    context_grad = nt(grad, courier[...]).astype(bf16)
    dq, dk, dv = [], [], []
    for j in range(heads):
        q, k, v = [
            proj[:, c * local + j * HS : c * local + (j + 1) * HS] for c in range(3)
        ]
        cg = context_grad[:, j * HS : (j + 1) * HS]
        probs = probs_ref[j]
        weighted = probs * nt(cg, v)
        score_grad = (weighted - probs * jnp.sum(weighted, axis=-1, keepdims=True)).astype(bf16)
        dq.append((nn(score_grad, k) * score_scale).astype(bf16))
        dk.append((tn(score_grad, q) * score_scale).astype(bf16))
        dv.append(tn(probs.astype(bf16), cg).astype(bf16))
    back = None
    for c, parts in enumerate((dq, dk, dv)):
        value = jnp.concatenate(parts, axis=1)
        weight_out[c] = tn(value, rows[...])
        if c != 1:
            qv_out[c // 2 : c // 2 + 1, :] = jnp.sum(value.astype(f32), axis=0, keepdims=True)
        term = nn(value, weight[c])
        back = term if back is None else back + term
    back_out[...] = back
    send_out[...] = back.astype(bf16)


def own_part(line, local, head_index):
    part = line[:, 0:local]
    for b in range(1, line.shape[1] // local):
        part = jnp.where(head_index == b, line[:, b * local : (b + 1) * local], part)
    return part


def message_back_two(
    scalars, own, r1, r2, r3, grad, start, cls, nat, weight,
    weight_out, gain_out, shift_out, bias_out, cls_back_out,
):
    total = own[...]
    for piece in (r1, r2, r3):
        total = total + piece[...].astype(f32)
    base, factor = norm_stats(start[...])
    grad_in, gain_grad, shift_grad = norm_back(total, base, factor, nat[1:2, :])
    start_grad = (grad[...] + grad_in).astype(bf16)
    weight_out[...] = tn(cls[...], start_grad)
    local = weight.shape[0]
    lines = (gain_grad, shift_grad, jnp.sum(start_grad.astype(f32), axis=0, keepdims=True))
    for out, line in zip((gain_out, shift_out, bias_out), lines):
        out[...] = own_part(line, local, scalars[0]).reshape(local)
    cls_back_out[...] = nt(weight[...], start_grad[:16])


def attention_forward(
    scalars, stream, m0, m1, m2, m3, start, nat, bias_ref, own, near, far,
    qkv_out, probs_out, ctx_out, rows, normed, s2_out, weight, total, *, heads, tokens, patches,
):
    slot = pl.program_id(0)
    head_index, place = scalars[0], scalars[1]
    frames = stream.shape[0] // tokens
    local = heads * HS

    @pl.when(slot == 0)
    def _():
        lines = start[...] + m0[...] + m1[...] + m2[...] + m3[...] + nat[3:4, :]
        message = pick_rows(lines, head_index * frames, frames)
        token = lax.broadcasted_iota(jnp.int32, (tokens, 1), 0)
        for i in range(frames):
            span = slice(i * tokens, (i + 1) * tokens)
            rows[span, :] = jnp.where(token == patches, message[i], stream[span, :].astype(f32))
        base, _ = norm_stats(rows[...])
        normed[...] = (base * nat[4:5, :] + nat[5:6, :]).astype(bf16)
        total[...] = jnp.zeros_like(total)

    place_weight(weight, own, near, far, place, slot)
    projected = (nt(normed[...], weight[: 3 * local, :]) + bias_ref[...]).astype(bf16)
    qkv_out[...] = projected
    key_ok = lax.broadcasted_iota(jnp.int32, (tokens, tokens), 1) <= patches
    for i in range(frames):
        part = projected[i * tokens : (i + 1) * tokens]
        pieces = []
        for j in range(heads):
            q = part[:, j * HS : (j + 1) * HS]
            k = part[:, local + j * HS : local + (j + 1) * HS]
            v = part[:, 2 * local + j * HS : 2 * local + (j + 1) * HS]
            scores = jnp.where(key_ok, nt(q, k) * score_scale, masked_score)
            scores = jnp.exp(scores - jnp.max(scores, axis=-1, keepdims=True))
            probs = (scores * (1.0 / jnp.sum(scores, axis=-1, keepdims=True))).astype(bf16)
            probs_out[i * heads + j] = probs
            pieces.append(nn(probs, v).astype(bf16))
        ctx_out[pl.ds(i * tokens, tokens), :] = jnp.concatenate(pieces, axis=1)
    total[...] += nn(ctx_out[...], weight[3 * local :, :])

    @pl.when(slot == pl.num_programs(0) - 1)
    def _():
        s2_out[...] = rows[...] + total[...] + nat[6:7, :]


def mlp_forward(
    scalars, s2_ref, nat, fc_bias_ref,
    fc_own, fc_near, fc_far, proj_own, proj_near, proj_far,
    pre_out, o0, o1, o2, o3, cls_out, normed, fc, proj, total, turned, *, block, tokens,
):
    slot = pl.program_id(0)
    head_index, place = scalars[0], scalars[1]

    @pl.when(slot == 0)
    def _():
        base, _ = norm_stats(s2_ref[...])
        normed[...] = (base * nat[7:8, :] + nat[8:9, :]).astype(bf16)
        total[...] = jnp.zeros_like(total)

    place_weight(fc, fc_own, fc_near, fc_far, place, slot)
    place_weight(proj, proj_own, proj_near, proj_far, place, slot)
    pre = nn(normed[...], fc[...]) + fc_bias_ref[...]
    pre_out[...] = pre
    hidden = (pre * jax.nn.sigmoid(gelu_rate * pre)).astype(bf16)
    total[...] += nn(hidden, proj[...])

    @pl.when(slot == pl.num_programs(0) - 1)
    def _():
        total[...] = s2_ref[...] + total[...] + nat[9:10, :]
        frames = o0.shape[0]
        cls = []
        for i in range(frames):
            base = i * tokens
            split_features(
                total[base : base + tokens, :].astype(bf16), (o0, o1, o2, o3), i, head_index, turned
            )
            cls.append(total[base : base + 1, :])
        cls_out[...] = put_rows(cls, head_index * frames, block)


def mlp_backward(
    scalars, u0, u1, u2, u3, cls_ref, s2_ref, pre_ref, nat,
    fc_own, fc_near, fc_far, proj_own, proj_near, proj_far,
    keep, send, fc_bias_out, vec_out, g2_out,
    normed, grad3, fc, proj, total, turned, *, tokens,
):
    slot = pl.program_id(0)
    head_index, place = scalars[0], scalars[1]
    frames = u0.shape[0]
    width = nat.shape[1]

    @pl.when(slot == 0)
    def _():
        base, _ = norm_stats(s2_ref[...])
        normed[...] = (base * nat[7:8, :] + nat[8:9, :]).astype(bf16)
        lines = pick_rows(cls_ref[...], head_index * frames, frames)
        token = lax.broadcasted_iota(jnp.int32, (tokens, 1), 0)
        others = (u0, u1, u2, u3)
        for i in range(frames):
            value = join_features(
                lambda s, i: others[s][i], u0, i, head_index, turned, tokens
            ).astype(f32)
            grad3[i * tokens : (i + 1) * tokens, :] = value + jnp.where(token == 0, lines[i], 0.0)
        total[...] = jnp.zeros_like(total)

    place_weight(fc, fc_own, fc_near, fc_far, place, slot)
    place_weight(proj, proj_own, proj_near, proj_far, place, slot)
    mlp_grad = grad3[...].astype(bf16)
    pre = pre_ref[...]
    gate = jax.nn.sigmoid(gelu_rate * pre)
    hidden = (pre * gate).astype(bf16)
    spread_grad(keep, send, 1, tn(hidden, mlp_grad), place)
    hidden_grad = nt(mlp_grad, proj[...])
    pre_grad = (hidden_grad * (gate + gelu_rate * pre * gate * (1.0 - gate))).astype(bf16)
    fc_bias_out[...] = jnp.sum(pre_grad.astype(f32), axis=0, keepdims=True)
    spread_grad(keep, send, 0, tn(normed[...], pre_grad), place)
    total[...] += nt(pre_grad, fc[...])

    @pl.when(slot == pl.num_programs(0) - 1)
    def _():
        base, factor = norm_stats(s2_ref[...])
        grad_in, gain_grad, shift_grad = norm_back(total[...], base, factor, nat[7:8, :])
        g2_out[...] = grad3[...] + grad_in
        vec_out[0:1, :] = gain_grad
        vec_out[1:2, :] = shift_grad
        vec_out[2:3, :] = jnp.sum(grad3[...].astype(bf16).astype(f32), axis=0, keepdims=True)
        vec_out[3:8, :] = jnp.zeros((5, width), f32)


def attention_backward(
    scalars, g2_ref, rows, qkv_ref, probs_ref, nat, mlp_vec, fc_bias_grad, own, near, far,
    dproj, vec_out, o0, o1, o2, o3, msg_out,
    grad, sums, weight, total, turned, *, heads, block, tokens,
):
    slot = pl.program_id(0)
    head_index, place = scalars[0], scalars[1]
    frames, _, patches = o0.shape
    width = nat.shape[1]
    local = heads * HS

    @pl.when(slot == 0)
    def _():
        grad[...] = g2_ref[...].astype(bf16)
        total[...] = jnp.zeros_like(total)
        sums[...] = jnp.zeros_like(sums)

    place_weight(weight, own, near, far, place, slot)
    context_grad = nt(grad[...], weight[3 * local :, :]).astype(bf16)
    for i in range(frames):
        span = slice(i * tokens, (i + 1) * tokens)
        dq, dk, dv = [], [], []
        for j in range(heads):
            q = qkv_ref[span, j * HS : (j + 1) * HS]
            k = qkv_ref[span, local + j * HS : local + (j + 1) * HS]
            v = qkv_ref[span, 2 * local + j * HS : 2 * local + (j + 1) * HS]
            cg = context_grad[span, j * HS : (j + 1) * HS]
            low = probs_ref[i * heads + j]
            probs = low.astype(f32)
            weighted = probs * nt(cg, v)
            score_grad = (
                weighted - probs * jnp.sum(weighted, axis=-1, keepdims=True)
            ).astype(bf16)
            dq.append((nn(score_grad, k) * score_scale).astype(bf16))
            dk.append((tn(score_grad, q) * score_scale).astype(bf16))
            dv.append(tn(low, cg).astype(bf16))
        dproj[pl.ds(i * tokens, tokens), :] = jnp.concatenate(dq + dk + dv, axis=1)
    all_grads = dproj[...]
    sums[pl.ds(slot, 1), 0 : 3 * local] = jnp.sum(all_grads.astype(f32), axis=0, keepdims=True)
    total[...] += nn(all_grads, weight[: 3 * local, :])

    @pl.when(slot == pl.num_programs(0) - 1)
    def _():
        base, factor = norm_stats(rows[...])
        grad_in, gain_grad, shift_grad = norm_back(total[...], base, factor, nat[4:5, :])
        total[...] = grad_in + g2_ref[...]
        message = []
        for i in range(frames):
            first = i * tokens
            split_features(
                total[first : first + tokens, :].astype(bf16), (o0, o1, o2, o3), i, head_index, turned
            )
            message.append(total[first + patches : first + patches + 1, :])
        msg_out[...] = put_rows(message, head_index * frames, block)
        out_grad = jnp.sum(grad[...].astype(f32), axis=0, keepdims=True)
        for s in range(vec_out.shape[0]):
            vec_out[s, 0:1, :] = gain_grad
            vec_out[s, 1:2, :] = shift_grad
            vec_out[s, 2:3, :] = out_grad
            vec_out[s, 3:6, :] = mlp_vec[0:3, :]
            vec_out[s, 6:7, :] = fc_bias_grad[s]
            vec_out[s, 7:8, :] = sums[s : s + 1, :]


def attention_weights(scalars, g2_ref, normed, dproj, ctx, vec, keep, send, grad):
    slot = pl.program_id(0)
    place = scalars[1]

    @pl.when(slot == 0)
    def _():
        grad[...] = g2_ref[...].astype(bf16)

    value = jnp.concatenate([tn(dproj[...], normed[...]), tn(ctx[...], grad[...])], axis=0)
    spread_grad(keep, send, 0, value, place)
    block, width = value.shape[0] // GROUP, value.shape[1]
    blank = jnp.zeros((keep.shape[3] - block - 1, width), f32)
    for owner in range(GROUP):
        offset = place ^ owner
        rest = offset // 2
        tail = jnp.concatenate([vec[owner : owner + 1, :], blank], axis=0).astype(bf16)

        @pl.when(offset % 2 == 0)
        def _():
            keep[rest % 2, rest // 2, 0, block:, :] = tail

        @pl.when(offset % 2 == 1)
        def _():
            send[rest % 2, rest // 2, 0, block:, :] = tail


def finish_weights(scalars, near, far, fc_out, proj_out, qkv_out, out_out, vec_out, *, block):
    step = pl.program_id(0)
    here = (step ^ scalars[1]) % 2 == 0
    value = jnp.where(here, near[...], far[...]).astype(f32)
    fc_out[...] = value[0:block]
    proj_out[...] = value[block : 2 * block]
    vec_out[pl.ds(step, 1), :] = value[3 * block : 3 * block + 1]

    @pl.when(step < 6)
    def _():
        qkv_out[...] = value[2 * block : 3 * block]

    @pl.when(step >= 6)
    def _():
        out_out[...] = value[2 * block : 3 * block]


def finish_vectors(scalars, vec, o0, o1, o2, o3, o4, o5, fc_out, qv_out):
    local = o0.shape[0]
    for i, out in enumerate((o0, o1, o2, o3, o4, o5)):
        out[...] = own_part(vec[i : i + 1, :], local, scalars[0]).reshape(local)
    fc_out[...] = vec[6:7, :].reshape(vec.shape[1])
    qv_out[0:1, :] = vec[7:8, 0:local]
    qv_out[1:2, :] = vec[7:8, 2 * local : 3 * local]


def finish_output(scalars, p0, p1, p2, p3, out):
    frames = p0.shape[0]
    for s, piece in enumerate((p0, p1, p2, p3)):
        first = ((scalars[0] - s + 4) % 4) * frames
        for i in range(frames):
            out[first + i] = piece[i]


def finish_grads(scalars, p0, p1, p2, p3, add, out):
    frames, local, patches = p0.shape
    for s, piece in enumerate((p0, p1, p2, p3)):
        first = ((scalars[0] - s + 4) % 4) * frames
        for i in range(frames):
            out[first + i] = piece[i].astype(f32)
    lane = lax.broadcasted_iota(jnp.int32, (local, 128), 1)
    for f in range(out.shape[0]):
        out[f, :, 0:128] = out[f, :, 0:128] + jnp.where(lane == 0, add[:, f : f + 1], 0.0)


def whole(array):
    count = array.ndim
    return pl.BlockSpec(array.shape, lambda s, sc: (0,) * count)


def first_rows(array, rows):
    return pl.BlockSpec((rows, array.shape[1]), lambda s, sc: (0, 0))


def per_slot(array):
    count = array.ndim - 1
    return pl.BlockSpec((None,) + array.shape[1:], lambda s, sc: (s,) + (0,) * count)


def weight_specs(own, near, which):
    def pick(s, sc):
        return (0, 0, jnp.maximum(s - 1, 0), which, 0, 0)

    far_spec = pl.BlockSpec((2, 4, None, None) + near.shape[4:], pick)
    return [pl.BlockSpec(own.shape, lambda s, sc: (0, 0)), far_spec, far_spec]


def shaped(shape, dtype):
    return jax.ShapeDtypeStruct(tuple(shape), dtype)


def slot_out(shape, dtype, slots):
    count = len(shape)
    return (
        shaped((slots,) + tuple(shape), dtype),
        pl.BlockSpec((None,) + tuple(shape), lambda s, sc: (s,) + (0,) * count),
    )


def full_out(shape, dtype):
    count = len(shape)
    return shaped(shape, dtype), pl.BlockSpec(tuple(shape), lambda s, sc: (0,) * count)


def call(kernel, steps, scalars, inputs, outs, scratch=(), flops=0):
    inputs = [a if isinstance(a, tuple) else (a, whole(a)) for a in inputs]
    arrays, specs = zip(*inputs)
    shapes, out_specs = zip(*outs)
    moved = sum(a.size * a.dtype.itemsize for a in arrays + shapes)
    return pl.pallas_call(
        kernel,
        grid_spec=pltpu.PrefetchScalarGridSpec(
            num_scalar_prefetch=1,
            grid=(steps,),
            in_specs=list(specs),
            out_specs=list(out_specs),
            scratch_shapes=list(scratch),
        ),
        out_shape=list(shapes),
        cost_estimate=pl.CostEstimate(flops=flops, bytes_accessed=moved, transcendentals=0),
    )(scalars, *arrays)


def call_once(kernel, scalars, inputs, outs, scratch=()):
    moved = sum(a.size * a.dtype.itemsize for a in list(inputs) + list(outs))
    space = pl.BlockSpec(memory_space=pltpu.VMEM)
    first = [] if scalars is None else [scalars]
    return pl.pallas_call(
        kernel,
        in_specs=[pl.BlockSpec(memory_space=pltpu.SMEM)] * len(first) + [space] * len(inputs),
        out_specs=[space] * len(outs),
        out_shape=list(outs),
        scratch_shapes=list(scratch),
        cost_estimate=pl.CostEstimate(flops=0, bytes_accessed=moved, transcendentals=0),
    )(*first, *inputs)


def tie(first, second):
    return lax.optimization_barrier((first, second))


def gather_rows(value):
    for bit in frame_bits(GROUP):
        value = jnp.concatenate([value, swap_frames(value, bit)], axis=0)
    value = jnp.concatenate([value, swap_frames(value, 1)], axis=0)
    return [value] + [swap_frames(value, bit) for bit in (2, 4, 6)]


def gathered_places(frame_index):
    count = lax.axis_size("frames")
    far = jnp.arange(count // GROUP) * GROUP
    near = jnp.arange(GROUP)
    return frame_index ^ (near.reshape(4, 2, 1) + far).reshape(-1)


def gather_halves(first, second):
    first = jnp.stack([first, swap_frames(first, 2)])
    second = jnp.stack([second, swap_frames(second, 4)])
    first_far = swap_frames(first, 4)
    second_far = swap_frames(second, 2)
    near = jnp.stack(
        [
            jnp.concatenate([first, first_far], axis=0),
            jnp.concatenate([second, second_far], axis=0),
        ]
    )
    return near, swap_frames(near, 1)


def reduce_first(keep, got):
    half = keep.shape[4] // 2

    def summed(x, y, low):
        rows = slice(0, half) if low else slice(half, 2 * half)
        index = (x, y, slice(None), slice(None), rows)
        return keep[index].astype(f32) + got[index].astype(f32)

    both = slice(None)
    first_got = swap_frames(summed(1, both, True).astype(bf16), 2)
    second_got = swap_frames(summed(both, 1, False).astype(bf16), 4)
    return summed, first_got, second_got


def reduce_second(summed, first_got, second_got):
    def next_first(y):
        return summed(0, y, True) + first_got[y].astype(f32)

    def next_second(x):
        return summed(x, 0, False) + second_got[x].astype(f32)

    first_last = swap_frames(next_first(1).astype(bf16), 4)
    second_last = swap_frames(next_second(1).astype(bf16), 2)
    return next_first(0), next_second(0), first_last, second_last


def reduce_last(first, second, first_last, second_last):
    def quarter(slot):
        low = first[slot] + first_last[slot].astype(f32)
        high = second[slot] + second_last[slot].astype(f32)
        value = jnp.concatenate([low, high], axis=1)
        return value.reshape(-1, value.shape[2])

    quarters = [quarter(s) for s in range(first.shape[0])]
    for bit in frame_bits(GROUP):
        quarters = [q + swap_frames(q.astype(bf16), bit).astype(f32) for q in quarters]
    own = quarters[0]
    for step in range(1, len(quarters)):
        own = own + to_heads(quarters[step].astype(bf16), -step).astype(f32)
    return own.astype(bf16)


def regather(rows):
    half = rows.shape[0] // 2
    first, second = rows[:half], rows[half:]
    first = jnp.stack([first, swap_frames(first, 2)])
    second = jnp.stack([second, swap_frames(second, 4)])
    first = jnp.concatenate([first, swap_frames(first, 4)], axis=0)
    second = jnp.concatenate([second, swap_frames(second, 2)], axis=0)
    second = jnp.stack([second[0], second[2], second[1], second[3]])
    near = jnp.concatenate([first, second], axis=1)
    return near, swap_frames(near, 1)


def on_device(
    frames_in,
    upstream,
    video_of_frame,
    group_ids,
    msg_fc_weight,
    msg_fc_bias,
    msg_gain,
    msg_shift,
    msg_qkv_weight,
    msg_qv_bias,
    courier_result_kernel,
    msg_out_bias,
    ln1_gain,
    ln1_shift,
    qkv_weight,
    qv_bias,
    picture_result_kernel,
    out_bias,
    ln2_gain,
    ln2_shift,
    fc_weight,
    fc_bias,
    proj_weight,
    proj_bias,
):
    block, patches, local = frames_in.shape
    width = msg_qkv_weight.shape[0]
    slots = lax.axis_size("heads")
    own_frames = block // slots
    heads = local // HS
    tokens = -(-(patches + 1) // 16) * 16
    rows = own_frames * tokens
    hidden_local = fc_weight.shape[1]
    share = width // GROUP
    frame_index = lax.axis_index("frames")
    head_index = lax.axis_index("heads")
    place = frame_index % GROUP
    scalars = jnp.stack([head_index, place]).astype(jnp.int32)
    steps = range(1, slots)
    turned = pltpu.VMEM((width, 256), bf16)
    frame_spec = pl.BlockSpec((own_frames, local, patches), lambda s, sc: (sc[0], 0, 0))

    def to_all_heads(value):
        return [value] + [to_heads(value, s) for s in steps]

    def my_rows(array):
        return lax.dynamic_slice_in_dim(array, place * share, share, axis=0)

    x_turned = jnp.transpose(frames_in, (0, 2, 1))
    up_turned = jnp.transpose(upstream, (0, 2, 1))
    msg_qkv = jnp.transpose(msg_qkv_weight, (1, 2, 0))
    sent_rows = SMALL + share + 2 * local // 3
    attn_own, cls_own, send_1, send_2, send_3 = call_once(
        pack_first,
        scalars,
        [x_turned, msg_fc_weight, jnp.transpose(qkv_weight, (1, 2, 0)), picture_result_kernel,
         msg_fc_bias, msg_gain, msg_shift, msg_out_bias, ln1_gain, ln1_shift,
         out_bias, ln2_gain, ln2_shift, proj_bias, qv_bias, fc_bias],
        [shaped((width, width), bf16), shaped((block, local), f32)]
        + [shaped((sent_rows, width), bf16)] * 3,
    )
    received = [send_1] + [to_heads(v, s) for s, v in zip(steps, (send_1, send_2, send_3))]
    nat, fc_bias_slots, qkv_bias_slots, sent, first_half, second_half, stream = call(
        functools.partial(unpack_first, block=block, tokens=tokens),
        1,
        scalars,
        [(x_turned, frame_spec), cls_own] + received,
        [
            full_out((16, width), f32),
            full_out((slots, 1, width), f32),
            full_out((slots, 1, 3 * local), f32),
            full_out((block, 1024), f32),
            full_out((slots - 1, 1, share // 2, width), bf16),
            full_out((slots - 1, 1, share // 2, width), bf16),
            full_out((rows, width), bf16),
        ],
        [turned],
    )
    start_pieces = gather_rows(sent)
    attn_near, attn_far = gather_halves(first_half, second_half)
    mine = jnp.stack([my_rows(fc_weight), my_rows(proj_weight)])
    mine, start_pieces = tie(mine, start_pieces)
    got = [to_heads(mine, s) for s in steps]
    mlp_near, mlp_far = gather_halves(
        jnp.stack([g[:, : share // 2] for g in got]), jnp.stack([g[:, share // 2 :] for g in got])
    )
    attn_weights = list(
        zip((attn_own, attn_near, attn_far), weight_specs(attn_own, attn_near, 0))
    )
    mlp_weights = list(
        zip(
            (fc_weight, mlp_near, mlp_far, proj_weight, mlp_near, mlp_far),
            weight_specs(fc_weight, mlp_near, 0) + weight_specs(proj_weight, mlp_near, 1),
        )
    )

    ids = video_of_frame.reshape(-1, block)[gathered_places(frame_index)].reshape(-1)
    ids_row, ids_col = ids[None, :], ids[:, None]
    total_frames = ids.shape[0]
    start, cls_all, msg_rows, msg_proj, msg_probs, msg_context, msg_part = call_once(
        functools.partial(message_forward, heads=heads, block=block),
        None,
        list(start_pieces) + [ids_col, ids_row, nat, msg_qkv, msg_qv_bias, courier_result_kernel],
        [
            shaped((total_frames, width), f32),
            shaped((total_frames, local), bf16),
            shaped((total_frames, width), bf16),
            shaped((total_frames, 3 * local), bf16),
            shaped((heads, total_frames, total_frames), f32),
            shaped((total_frames, local), bf16),
            shaped((block, width), f32),
        ],
    )
    msg_parts = to_all_heads(msg_part)

    qkv, probs, context, stream_one, normed_one, stream_two = call(
        functools.partial(attention_forward, heads=heads, tokens=tokens, patches=patches),
        slots,
        scalars,
        [stream]
        + msg_parts
        + [(start, first_rows(start, block)), nat, (qkv_bias_slots, per_slot(qkv_bias_slots))]
        + attn_weights,
        [
            slot_out((rows, 3 * local), bf16, slots),
            slot_out((own_frames * heads, tokens, tokens), bf16, slots),
            slot_out((rows, local), bf16, slots),
            full_out((rows, width), f32),
            full_out((rows, width), bf16),
            full_out((rows, width), f32),
        ],
        [pltpu.VMEM((width, width), bf16), pltpu.VMEM((rows, width), f32)],
        2 * rows * width * width * slots,
    )

    frame_out = full_out((own_frames, local, patches), bf16)
    pre, out_0, out_1, out_2, out_3, cls_block = call(
        functools.partial(mlp_forward, block=block, tokens=tokens),
        slots,
        scalars,
        [stream_two, nat, (fc_bias_slots, per_slot(fc_bias_slots))] + mlp_weights,
        [slot_out((rows, hidden_local), f32, slots)]
        + [frame_out] * slots
        + [full_out((block, width), f32)],
        [
            pltpu.VMEM((rows, width), bf16),
            pltpu.VMEM((width, hidden_local), bf16),
            pltpu.VMEM((hidden_local, width), bf16),
            pltpu.VMEM((rows, width), f32),
            turned,
        ],
        4 * rows * width * hidden_local * slots,
    )

    cls_pieces = gather_rows(sum(to_all_heads(cls_block)))
    videos = group_ids.shape[0]
    groups = jnp.pad(group_ids, (0, -videos % 8), constant_values=-1)
    loss_value, cls_grad = call_once(
        functools.partial(contrast, videos=videos, block=block),
        None,
        cls_pieces + [ids_row, ids_col, groups[:, None], groups[None, :]],
        [shaped((1, 1), f32), shaped((block, width), f32)],
    )

    def frames_of(array, step):
        start = jnp.mod(head_index + step, slots) * own_frames
        return lax.dynamic_slice_in_dim(array, start, own_frames, axis=0)

    up_pieces = [(up_turned, frame_spec)] + [to_heads(frames_of(up_turned, s), s) for s in steps]
    out_pieces = [out_0] + [to_heads(o, s) for s, o in zip(steps, (out_1, out_2, out_3))]

    def grad_out(matrices, size):
        shape = (2, 2, slots, matrices, size, width)
        return shaped(shape, bf16), pl.BlockSpec(
            (2, 2, None, matrices, size, width), lambda s, sc: (0, 0, s, 0, 0, 0)
        )

    keep, send, fc_bias_grad, mlp_vec, grad_two = call(
        functools.partial(mlp_backward, tokens=tokens),
        slots,
        scalars,
        up_pieces + [cls_grad, stream_two, (pre, per_slot(pre)), nat] + mlp_weights,
        [
            grad_out(2, share),
            grad_out(2, share),
            slot_out((1, hidden_local), f32, slots),
            full_out((8, width), f32),
            full_out((rows, width), f32),
        ],
        [
            pltpu.VMEM((rows, width), bf16),
            pltpu.VMEM((rows, width), f32),
            pltpu.VMEM((width, hidden_local), bf16),
            pltpu.VMEM((hidden_local, width), bf16),
            pltpu.VMEM((rows, width), f32),
            turned,
        ],
        8 * rows * width * hidden_local * slots,
    )
    mlp_got = swap_frames(send, 1)

    dproj, vec, gi_0, gi_1, gi_2, gi_3, grad_msg_block = call(
        functools.partial(attention_backward, heads=heads, block=block, tokens=tokens),
        slots,
        scalars,
        [grad_two, stream_one, (qkv, per_slot(qkv)), (probs, per_slot(probs)), nat, mlp_vec, fc_bias_grad]
        + attn_weights,
        [slot_out((rows, 3 * local), bf16, slots), full_out((slots, 8, width), f32)]
        + [frame_out] * slots
        + [full_out((block, width), f32)],
        [
            pltpu.VMEM((rows, width), bf16),
            pltpu.VMEM((8, width), f32),
            pltpu.VMEM((width, width), bf16),
            pltpu.VMEM((rows, width), f32),
            turned,
        ],
        6 * rows * width * width * slots,
    )
    dproj, mlp_got = tie(dproj, mlp_got)
    mlp_state = reduce_first(keep, mlp_got)
    attn_keep, attn_send = call(
        attention_weights,
        slots,
        scalars,
        [grad_two, normed_one, (dproj, per_slot(dproj)), (context, per_slot(context)), (vec, per_slot(vec))],
        [grad_out(1, share + 16), grad_out(1, share + 16)],
        [pltpu.VMEM((rows, width), bf16)],
        2 * rows * width * width * slots,
    )
    attn_got = swap_frames(attn_send, 1)
    msg_pieces = gather_rows(sum(to_all_heads(grad_msg_block)))
    vector = shaped((local,), f32)
    (
        grad_message, grad_msg_qkv, grad_msg_out_weight, back_own, back_send, grad_msg_out_bias,
        grad_msg_qv_bias,
    ) = call_once(
        functools.partial(message_back_one, heads=heads),
        scalars,
        msg_pieces + [msg_rows, msg_proj, msg_probs, msg_context, msg_qkv, courier_result_kernel],
        [
            shaped((total_frames, width), f32),
            shaped((3, local, width), f32),
            shaped((local, width), f32),
            shaped((total_frames, width), f32),
            shaped((total_frames, width), bf16),
            vector,
            shaped((2, local), f32),
        ],
    )
    back = [back_own] + [to_heads(back_send, s) for s in steps]
    grad_msg_fc_weight, grad_msg_gain, grad_msg_shift, grad_msg_fc_bias, cls_back = call_once(
        message_back_two,
        scalars,
        back + [grad_message, start, cls_all, nat, msg_fc_weight],
        [shaped((local, width), f32), vector, vector, vector, shaped((local, 16), f32)],
    )
    grad_pieces = [gi_0] + [to_heads(g, s) for s, g in zip(steps, (gi_1, gi_2, gi_3))]

    mlp_state = reduce_second(*mlp_state)
    attn_state = reduce_second(*reduce_first(attn_keep, attn_got))
    near, far = regather(
        jnp.concatenate([reduce_last(*mlp_state), reduce_last(*attn_state)], axis=0)
    )

    def picked(s, sc):
        return ((s ^ sc[1]) // 2, 0, 0)

    part_spec = pl.BlockSpec((None,) + near.shape[1:], picked)
    flat = shaped((width, width), f32)
    flat_spec = pl.BlockSpec((share, width), lambda s, sc: (s, 0))
    grad_fc_weight, grad_proj_weight, grad_qkv, grad_out_weight, vectors = call(
        functools.partial(finish_weights, block=share),
        GROUP,
        scalars,
        [(near, part_spec), (far, part_spec)],
        [
            (flat, flat_spec),
            (flat, flat_spec),
            (
                shaped((3 * local, width), f32),
                pl.BlockSpec((share, width), lambda s, sc: (jnp.minimum(s, 5), 0)),
            ),
            (
                shaped((local, width), f32),
                pl.BlockSpec((share, width), lambda s, sc: (jnp.maximum(s - 6, 0), 0)),
            ),
            full_out((8, width), f32),
        ],
    )
    *features, grad_fc_bias, grad_qv_bias = call_once(
        finish_vectors,
        scalars,
        [vectors],
        [vector] * 6 + [shaped((width,), f32), shaped((2, local), f32)],
    )
    (output,) = call_once(
        finish_output, scalars, out_pieces, [shaped((block, local, patches), bf16)]
    )
    (grad_input,) = call_once(
        finish_grads, scalars, grad_pieces + [cls_back], [shaped((block, local, patches), f32)]
    )
    return (
        jnp.transpose(output, (0, 2, 1)),
        loss_value.reshape(()),
        jnp.transpose(grad_input, (0, 2, 1)),
        grad_msg_fc_weight,
        grad_msg_fc_bias,
        grad_msg_gain,
        grad_msg_shift,
        jnp.transpose(grad_msg_qkv, (2, 0, 1)),
        grad_msg_qv_bias,
        grad_msg_out_weight,
        grad_msg_out_bias,
        features[0],
        features[1],
        jnp.transpose(grad_qkv.reshape(3, local, width), (2, 0, 1)),
        grad_qv_bias,
        grad_out_weight,
        features[2],
        features[3],
        features[4],
        grad_fc_weight,
        grad_fc_bias,
        grad_proj_weight,
        features[5],
    )


def solution(mesh):
    placed = (
        P("frames", None, "heads"),
        P("frames", None, "heads"),
        P(),
        P(),
        P("heads", None),
        P("heads"),
        P("heads"),
        P("heads"),
        P(None, None, "heads"),
        P(None, "heads"),
        P("heads", None),
        P("heads"),
        P("heads"),
        P("heads"),
        P(None, None, "heads"),
        P(None, "heads"),
        P("heads", None),
        P("heads"),
        P("heads"),
        P("heads"),
        P(None, "heads"),
        P("heads"),
        P("heads", None),
        P("heads"),
    )
    return jax.shard_map(
        on_device,
        mesh=mesh,
        in_specs=placed,
        out_specs=(
            P("frames", None, "heads"),
            P(),
            P("frames", None, "heads"),
            P("heads", None),
            P("heads"),
            P("heads"),
            P("heads"),
            P(None, None, "heads"),
            P(None, "heads"),
            P("heads", None),
            P("heads"),
            P("heads"),
            P("heads"),
            P(None, None, "heads"),
            P(None, "heads"),
            P("heads", None),
            P("heads"),
            P("heads"),
            P("heads"),
            P(None, "heads"),
            P("heads"),
            P("heads", None),
            P("heads"),
        ),
        check_vma=False,
    )
```

time: 503 us -> 448 us (0.89)
  the two profiles are of different devices: /device:TPU:9 before, /device:TPU:0 now
where the time goes in v3:
time: 448 us; the launch traced here: 446 us
  waiting for transfers between devices  212 us (47%)
  Pallas kernels  118 us (26%)
  starting transfers between devices  92.4 us (21%)
  other arithmetic  12.7 us (3%)
  local copies, waits for them, and re-layouts  10 us (2%)
    ppermute x37, waiting for transfers between devices, swap_frames(): return lax.ppermute(value, 'frames', [(i, i ^ bit) for i in range(count)])  126 us
    pallas_call x7, Pallas kernels, call(): pl.pallas_call(kernel, grid_spec=pltpu.PrefetchScalarGridSpec(num_scalar_...  93.8 us
    ppermute x33, waiting for transfers between devices, to_heads(): lax.ppermute(value, 'heads', [(i, (i + step) % count) for i in range(coun...  86.4 us
    ppermute x33, starting transfers between devices, to_heads(): lax.ppermute(value, 'heads', [(i, (i + step) % count) for i in range(coun...  59.3 us
    ppermute x37, starting transfers between devices, swap_frames(): return lax.ppermute(value, 'frames', [(i, i ^ bit) for i in range(count)])  33 us
    pallas_call x8, Pallas kernels, call_once(): pl.pallas_call(kernel, in_specs=[pl.BlockSpec(memory_space=pltpu.SMEM)] *...  24.2 us
  transfers between devices with their start and end apart: 70, of which 47 were waited for; matrix products, arithmetic and copies ran while one was open for 3% of the time, Pallas kernels for 12%

profile of v3, /device:TPU:0, one launch (start us, length us, event | category | flops | bytes accessed | tf_op | source)
XLA Modules:
  0.0 446.4 jit_solution(6296966650788051010)
XLA Ops:
  1.3 3.7 shard_map.407
  5.0 4.1 collective-permute-start.1
  12.1 16.5 %collective-permute-done.1.r2 = bf16[256,768]{1,0:T(8,128)(2,1)S(1)} collective-permute-done((bf16[256,768]{1,0:T(8,128)(2,1)}, bf16[256,768]{1,0:T(8,128)(2,1)S(1)}, u32[]{:S(2)}, u32[]{:S(2)}) %collective-permute-start.1) | collective-permute-done | bytes 393248 | tf_op jit(solution)/shard_map/ppermute | solution.py:39
  28.6 7.9 %collective-permute-done.r1 = bf16[256,768]{1,0:T(8,128)(2,1)S(1)} collective-permute-done((bf16[256,768]{1,0:T(8,128)(2,1)}, bf16[256,768]{1,0:T(8,128)(2,1)S(1)}, u32[]{:S(2)}, u32[]{:S(2)}) %collective-permute-start) | collective-permute-done | bytes 393248 | tf_op jit(solution)/shard_map/ppermute | solution.py:39
  52.0 7.8 %collective-permute-start.16 = (bf16[2,96,768]{2,1,0:T(8,128)(2,1)S(1)}, bf16[2,96,768]{2,1,0:T(8,128)(2,1)S(1)}, u32[]{:S(2)}, u32[]{:S(2)}) collective-permute-start(bf16[2,96,768]{2,1,0:T(8,128)(2,1)S(1)} %pad_maximum_fusion.11), channel_id=1, source_target_pairs={{0,2},{1,3},{2,0},{3,1},{4,6},{5,7},{6,4},{7,5},{8,10},{9,11},{10,... | collective-permute-start | bytes 884744 | tf_op jit(solution)/shard_map/ppermute | solution.py:39
  63.4 20.4 %collective-permute-done.16 = bf16[2,96,768]{2,1,0:T(8,128)(2,1)S(1)} collective-permute-done((bf16[2,96,768]{2,1,0:T(8,128)(2,1)S(1)}, bf16[2,96,768]{2,1,0:T(8,128)(2,1)S(1)}, u32[]{:S(2)}, u32[]{:S(2)}) %collective-permute-start.16) | collective-permute-done | bytes 294944 | tf_op jit(solution)/shard_map/ppermute | solution.py:39
  86.4 9.6 %collective-permute-done.18 = bf16[3,2,48,768]{3,2,1,0:T(8,128)(2,1)S(1)} collective-permute-done((bf16[3,2,48,768]{3,2,1,0:T(8,128)(2,1)S(1)}, bf16[3,2,48,768]{3,2,1,0:T(8,128)(2,1)S(1)}, u32[]{:S(2)}, u32[]{:S(2)}) %collective-permute-start.18) | collective-permute-done | bytes 442400 | tf_op jit(solution)/shard_map/ppermute | solution.py:44
  98.1 18.5 %collective-permute-done.19 = bf16[2,3,2,48,768]{4,3,2,1,0:T(8,128)(2,1)S(1)} collective-permute-done((bf16[2,3,2,48,768]{4,3,2,1,0:T(8,128)(2,1)S(1)}, bf16[2,3,2,48,768]{4,3,2,1,0:T(8,128)(2,1)S(1)}, u32[]{:S(2)}, u32[]{:S(2)}) %collective-permute-start.19) | collective-permute-done | bytes 884768 | tf_op jit(solution)/shard_map/ppermute | solution.py:44
  121.1 5.0 %collective-permute-done.12 = bf16[3,1,48,768]{3,2,0,1:T(8,128)(2,1)S(1)} collective-permute-done((bf16[3,1,48,768]{3,2,0,1:T(8,128)(2,1)S(1)}, bf16[3,1,48,768]{3,2,0,1:T(8,128)(2,1)S(1)}, u32[]{:S(2)}, u32[]{:S(2)}) %collective-permute-start.12) | collective-permute-done | bytes 221216 | tf_op jit(solution)/shard_map/ppermute | solution.py:44
  128.6 8.8 %collective-permute-done.13 = bf16[2,3,1,48,768]{4,3,1,0,2:T(8,128)(2,1)S(1)} collective-permute-done((bf16[2,3,1,48,768]{4,3,1,0,2:T(8,128)(2,1)S(1)}, bf16[2,3,1,48,768]{4,3,1,0,2:T(8,128)(2,1)S(1)}, u32[]{:S(2)}, u32[]{:S(2)}) %collective-permute-start.13) | collective-permute-done | bytes 442400 | tf_op jit(solution)/shard_map/ppermute | solution.py:44
  141.3 3.7 shard_map.409
  151.7 15.3 %shard_map.410 = (bf16[4,416,576]{2,1,0:T(8,128)(2,1)}, bf16[4,6,208,208]{3,2,1,0:T(8,128)(2,1)}, bf16[4,416,192]{2,1,0:T(8,128)(2,1)}, f32[416,768]{1,0:T(8,128...) custom-call(s32[2]{0:T(128)} %pad_add_fusion.scalars, bf16[416,768]{1,0:T(8,128)(2,1)} %get-tuple-element.106.stream, ...), custom_call_target="tpu_custom_call" | custom-call | flops 1962934272 | bytes 13538304 | tf_op jit(solution)/shard_map/pallas_call | solution.py:695
  167.1 12.4 %shard_map.411 = (f32[4,416,768]{2,1,0:T(8,128)}, bf16[2,192,197]{2,1,0:T(8,128)(2,1)}, bf16[2,192,197]{2,1,0:T(8,128)(2,1)}, bf16[2,192,197]{2,1,0:T(8,128)(2,1...) custom-call(s32[2]{0:T(128)} %pad_add_fusion.scalars, f32[416,768]{1,0:T(8,128)} %get-tuple-element.119.s2_ref, ...), custom_call_target="tpu_custom_call" | custom-call | flops 3925868544 | bytes 23596032 | tf_op jit(solution)/shard_map/pallas_call | solution.py:695
  203.5 6.1 %collective-permute-done.34.u2 = bf16[2,192,197]{2,1,0:T(8,128)(2,1)S(1)} collective-permute-done((bf16[2,192,197]{2,1,0:T(8,128)(2,1)S(1)}, bf16[2,192,197]{2,1,0:T(8,128)(2,1)S(1)}, u32[]{:S(2)}, u32[]{:S(2)}) %collective-permute-start.34) | collective-permute-done | bytes 151328 | tf_op jit(solution)/shard_map/ppermute | solution.py:39
  210.3 25.3 %shard_map.414 = (bf16[2,2,4,2,96,768]{5,4,3,2,1,0:T(8,128)(2,1)}, bf16[2,2,4,2,96,768]{5,4,3,2,1,0:T(8,128)(2,1)}, f32[4,1,768]{2,1,0:T(1,128)}, f32[8,768]{1,0:T(8,128)}, f32[416,768]{1,0:T(8,128)}) custom-call(s32[2]{0:T(128)} %pad_add_fusion.scalars, bf16[8,192,197]{2,1,0:T(8,128)(2,1)} %bitcast.242, bf16[2,192,197]{2,1,0:T(8,128)(2,1)} %copy-done.38, ...), custom_call_target="tpu_custom_call" | custom-call | flops 7851737088 | bytes 34789632 | tf_op jit(solution)/shard_map/pallas_call | solution.py:695
  235.6 19.7 %shard_map.415 = (bf16[4,416,576]{2,1,0:T(8,128)(2,1)}, f32[4,8,768]{2,1,0:T(8,128)}, bf16[2,192,197]{2,1,0:T(8,128)(2,1)}, bf16[2,192,197]{2,1,0:T(8,128)(2,1)}...) custom-call(s32[2]{0:T(128)} %pad_add_fusion.scalars, ...), custom_call_target="tpu_custom_call" | custom-call | flops 5888802816 | bytes 13999104 | tf_op jit(solution)/shard_map/pallas_call | solution.py:695
  255.4 9.0 %shard_map.419 = (bf16[2,2,4,1,112,768]{5,4,3,2,1,0:T(8,128)(2,1)}, bf16[2,2,4,1,112,768]{5,4,3,2,1,0:T(8,128)(2,1)}) custom-call(s32[2]{0:T(128)} %pad_add_fusion.scalars, f32[416,768]{1,0:T(8,128)} %get-tuple-element.130.g2_ref, bf16[416,768]{1,0:T(8,128)(2,1)} %get-tuple-element.162.normed, bf16[4,416,576]{2,1,0:T(8,128)(2,1)} %get-tuple-element.163.dproj, ...), custom_call_target="tpu_custom_call" | custom-call | flops 1962934272 | bytes 10076160 | tf_op jit(solution)/shard_map/pallas_call | solution.py:695
  270.7 26.1 %collective-permute-done.52 = bf16[2,4,2,48,768]{4,3,2,1,0:T(8,128)(2,1)S(1)} collective-permute-done((bf16[2,4,2,48,768]{4,3,2,1,0:T(8,128)(2,1)S(1)}, bf16[2,4,2,48,768]{4,3,2,1,0:T(8,128)(2,1)S(1)}, u32[]{:S(2)}, u32[]{:S(2)}) %collective-permute-start.52) | collective-permute-done | bytes 1179680 | tf_op jit(solution)/shard_map/ppermute | solution.py:44
  304.9 11.7 %collective-permute-done.51 = bf16[4,2,48,768]{3,2,1,0:T(8,128)(2,1)S(1)} collective-permute-done((bf16[4,2,48,768]{3,2,1,0:T(8,128)(2,1)S(1)}, bf16[4,2,48,768]{3,2,1,0:T(8,128)(2,1)S(1)}, u32[]{:S(2)}, u32[]{:S(2)}) %collective-permute-start.51) | collective-permute-done | bytes 589856 | tf_op jit(solution)/shard_map/ppermute | solution.py:44
  317.8 3.6 collective-permute-start.56
  321.7 8.1 %collective-permute-done.60 = bf16[2,4,1,56,768]{4,3,1,2,0:T(8,128)(2,1)S(1)} collective-permute-done((bf16[2,4,1,56,768]{4,3,1,2,0:T(8,128)(2,1)S(1)}, bf16[2,4,1,56,768]{4,3,1,2,0:T(8,128)(2,1)S(1)}, u32[]{:S(2)}, u32[]{:S(2)}) %collective-permute-start.60) | collective-permute-done | bytes 688160 | tf_op jit(solution)/shard_map/ppermute | solution.py:44
  332.5 5.4 %collective-permute-done.61 = bf16[4,1,56,768]{3,2,1,0:T(8,128)(2,1)S(1)} collective-permute-done((bf16[4,1,56,768]{3,2,1,0:T(8,128)(2,1)S(1)}, bf16[4,1,56,768]{3,2,1,0:T(8,128)(2,1)S(1)}, u32[]{:S(2)}, u32[]{:S(2)}) %collective-permute-start.61) | collective-permute-done | bytes 344096 | tf_op jit(solution)/shard_map/ppermute | solution.py:44
  339.1 3.6 collective-permute-start.66
  343.2 10.3 %collective-permute-done.65 = bf16[112,768]{1,0:T(8,128)(2,1)S(1)} collective-permute-done((bf16[112,768]{1,0:T(8,128)(2,1)S(1)}, bf16[112,768]{1,0:T(8,128)(2,1)S(1)}, u32[]{:S(2)}, u32[]{:S(2)}) %collective-permute-start.65) | collective-permute-done | bytes 172064 | tf_op jit(solution)/shard_map/ppermute | solution.py:39
  356.2 4.2 collective-permute-done.67
  363.0 8.4 %collective-permute-done.68 = bf16[2,152,768]{2,1,0:T(8,128)(2,1)S(1)} collective-permute-done((bf16[2,152,768]{2,1,0:T(8,128)(2,1)S(1)}, bf16[2,152,768]{2,1,0:T(8,128)(2,1)S(1)}, u32[]{:S(2)}, u32[]{:S(2)}) %collective-permute-start.68) | collective-permute-done | bytes 466976 | tf_op jit(solution)/shard_map/ppermute | solution.py:44
  375.8 3.9 collective-permute-start.40
  397.3 4.6 %shard_map.416 = (f32[64,768]{1,0:T(8,128)}, f32[3,192,768]{2,1,0:T(8,128)}, f32[192,768]{1,0:T(8,128)}, f32[64,768]{1,0:T(8,128)}, bf16[64,768]{1,0:T(8,128)(2,1)}, /*index=5*/f32[192]{0:T(256)}, f32[2,192]{1,0:T(2,128)}) custom-call(s32[2]{0:T(128)} %pad_add_fusion.scalars, f32[16,768]{1,0:T(8,128)} %copy-done.10, f32[16,768]{1,0:T(8,128)} %copy-done.27, ...), custom_call_target="tpu_custom_call" | custom-call | bytes 4475136 | tf_op jit(solution)/shard_map/pallas_call | solution.py:713
  405.4 5.1 %collective-permute-start.36 = (bf16[2,192,197]{2,1,0:T(8,128)(2,1)}, bf16[2,192,197]{2,1,0:T(8,128)(2,1)S(1)}, u32[]{:S(2)}, u32[]{:S(2)}) collective-permute-start(bf16[2,192,197]{2,1,0:T(8,128)(2,1)} %get-tuple-element.137), channel_id=1, source_target_pairs={{0,1},{1,2},{2,3},{3,0},{4,5},{5,6},{6,7},{7,4},{8,9},{9,10},{10,1... | collective-permute-start | bytes 453896 | tf_op jit(solution)/shard_map/ppermute | solution.py:39
  413.9 7.1 %collective-permute-start.38 = (bf16[2,192,197]{2,1,0:T(8,128)(2,1)S(1)}, bf16[2,192,197]{2,1,0:T(8,128)(2,1)S(1)}, u32[]{:S(2)}, u32[]{:S(2)}) collective-permute-start(bf16[2,192,197]{2,1,0:T(8,128)(2,1)S(1)} %copy-done.36), channel_id=1, source_target_pairs={{0,3},{1,0},{2,1},{3,2},{4,7},{5,4},{6,5},{7,6},{8,11},{9,8},{10,9... | collective-permute-start | bytes 453896 | tf_op jit(solution)/shard_map/ppermute | solution.py:39
  424.6 4.6 %collective-permute-done.46.r1 = bf16[64,768]{1,0:T(8,128)(2,1)S(1)} collective-permute-done((bf16[64,768]{1,0:T(8,128)(2,1)}, bf16[64,768]{1,0:T(8,128)(2,1)S(1)}, u32[]{:S(2)}, u32[]{:S(2)}) %collective-permute-start.46) | collective-permute-done | bytes 98336 | tf_op jit(solution)/shard_map/ppermute | solution.py:39
  436.2 8.8 %shard_map.420 = (f32[768,768]{1,0:T(8,128)}, f32[768,768]{1,0:T(8,128)}, f32[576,768]{1,0:T(8,128)}, f32[192,768]{1,0:T(8,128)}, f32[8,768]{1,0:T(8,128)}) custom-call(s32[2]{0:T(128)} %pad_add_fusion.scalars, bf16[4,304,768]{2,1,0:T(8,128)(2,1)} %copy-done.1, bf16[4,304,768]{2,1,0:T(8,128)(2,1)} %collective-permute-done.69.far), custom_call_target="tpu_custom_call" | custom-call | bytes 10838016 | tf_op jit(solution)/shard_map/pallas_call | solution.py:695
  (263 shorter events, 136.1 us)
Async XLA Ops:
  5.0 23.6 %collective-permute-start.1 = (bf16[256,768]{1,0:T(8,128)(2,1)}, bf16[256,768]{1,0:T(8,128)(2,1)S(1)}, u32[]{:S(2)}, u32[]{:S(2)}) collective-permute-start(bf16[256,768]{1,0:T(8,128)(2,1)} %get-tuple-element.104), channel_id=1, source_target_pairs={{0,2},{1,3},{2,0},{3,1},{4,6},{5,7},{6,4},{7,5},{8,10},{9,11},{10,... | collective-permute-start | bytes 1179656 | tf_op jit(solution)/shard_map/ppermute | solution.py:39
  9.1 19.5 %collective-permute-start.2 = (bf16[256,768]{1,0:T(8,128)(2,1)}, bf16[256,768]{1,0:T(8,128)(2,1)S(1)}, u32[]{:S(2)}, u32[]{:S(2)}) collective-permute-start(bf16[256,768]{1,0:T(8,128)(2,1)} %get-tuple-element.105), channel_id=1, source_target_pairs={{0,3},{1,0},{2,1},{3,2},{4,7},{5,4},{6,5},{7,6},{8,11},{9,8},{10,9... | collective-permute-start | bytes 1179656 | tf_op jit(solution)/shard_map/ppermute | solution.py:39
  10.4 26.0 %collective-permute-start = (bf16[256,768]{1,0:T(8,128)(2,1)}, bf16[256,768]{1,0:T(8,128)(2,1)S(1)}, u32[]{:S(2)}, u32[]{:S(2)}) collective-permute-start(bf16[256,768]{1,0:T(8,128)(2,1)} %get-tuple-element.103.own), channel_id=1, source_target_pairs={{0,1},{1,2},{2,3},{3,0},{4,5},{5,6},{6,7},{7,4},{8,9},{9,10},{10,1... | collective-permute-start | bytes 1179656 | tf_op jit(solution)/shard_map/ppermute | solution.py:39
  49.2 14.1 %collective-permute-start.17 = (bf16[2,96,768]{2,1,0:T(8,128)(2,1)S(1)}, bf16[2,96,768]{2,1,0:T(8,128)(2,1)S(1)}, u32[]{:S(2)}, u32[]{:S(2)}) collective-permute-start(bf16[2,96,768]{2,1,0:T(8,128)(2,1)S(1)} %pad_maximum_fusion.11), channel_id=1, source_target_pairs={{0,3},{1,0},{2,1},{3,2},{4,7},{5,4},{6,5},{7,6},{8,11},{9,8},{10,9... | collective-permute-start | bytes 884744 | tf_op jit(solution)/shard_map/ppermute | solution.py:39
  52.0 31.8 %collective-permute-start.16 = (bf16[2,96,768]{2,1,0:T(8,128)(2,1)S(1)}, bf16[2,96,768]{2,1,0:T(8,128)(2,1)S(1)}, u32[]{:S(2)}, u32[]{:S(2)}) collective-permute-start(bf16[2,96,768]{2,1,0:T(8,128)(2,1)S(1)} %pad_maximum_fusion.11), channel_id=1, source_target_pairs={{0,2},{1,3},{2,0},{3,1},{4,6},{5,7},{6,4},{7,5},{8,10},{9,11},{10,... | collective-permute-start | bytes 884744 | tf_op jit(solution)/shard_map/ppermute | solution.py:39
  59.7 24.0 %collective-permute-start.15 = (bf16[2,96,768]{2,1,0:T(8,128)(2,1)S(1)}, bf16[2,96,768]{2,1,0:T(8,128)(2,1)S(1)}, u32[]{:S(2)}, u32[]{:S(2)}) collective-permute-start(bf16[2,96,768]{2,1,0:T(8,128)(2,1)S(1)} %pad_maximum_fusion.11), channel_id=1, source_target_pairs={{0,1},{1,2},{2,3},{3,0},{4,5},{5,6},{6,7},{7,4},{8,9},{9,10},{10,1... | collective-permute-start | bytes 884744 | tf_op jit(solution)/shard_map/ppermute | solution.py:39
  96.1 20.5 %collective-permute-start.19 = (bf16[2,3,2,48,768]{4,3,2,1,0:T(8,128)(2,1)S(1)}, bf16[2,3,2,48,768]{4,3,2,1,0:T(8,128)(2,1)S(1)}, u32[]{:S(2)}, u32[]{:S(2)}) collective-permute-start(bf16[2,3,2,48,768]{4,3,2,1,0:T(8,128)(2,1)S(1)} %pad_maximum_fusion.2), channel_id=1, source_target_pairs={{0,16},{4,20},{8,24},{12,28},{16,0},{20,4},{24,8},{28,12},{1,17},{... | collective-permute-start | bytes 2654216 | tf_op jit(solution)/shard_map/ppermute | solution.py:44
  97.7 19.9 %collective-permute-start.21 = (bf16[2,3,2,48,768]{4,3,2,1,0:T(8,128)(2,1)S(1)}, bf16[2,3,2,48,768]{4,3,2,1,0:T(8,128)(2,1)S(1)}, u32[]{:S(2)}, u32[]{:S(2)}) collective-permute-start(bf16[2,3,2,48,768]{4,3,2,1,0:T(8,128)(2,1)S(1)} %pad_maximum_fusion.3), channel_id=1, source_target_pairs={{0,8},{4,12},{8,0},{12,4},{16,24},{20,28},{24,16},{28,20},{1,9},{5... | collective-permute-start | bytes 2654216 | tf_op jit(solution)/shard_map/ppermute | solution.py:44
  118.2 48.9 %collective-permute-start.22 = (bf16[2,4,3,2,48,768]{5,4,3,2,1,0:T(8,128)(2,1)S(1)}, bf16[2,4,3,2,48,768]{5,4,3,2,1,0:T(8,128)(2,1)}, u32[]{:S(2)}, u32[]{:S(2)}) collective-permute-start(bf16[2,4,3,2,48,768]{5,4,3,2,1,0:T(8,128)(2,1)S(1)} %pad_maximum_fusion.fc_near.proj_near), channel_id=1, source_target_pairs={{0,4},{4,0},{8,12},{12,8},{16,20},{20,16},{24,28},{28,24},{1,5},{5... | collective-permute-start | bytes 10616840 | tf_op jit(solution)/shard_map/ppermute | solution.py:44
  139.3 12.4 %collective-permute-start.14 = (bf16[2,4,3,1,48,768]{5,4,3,2,1,0:T(8,128)(2,1)}, bf16[2,4,3,1,48,768]{5,4,3,2,1,0:T(8,128)(2,1)}, u32[]{:S(2)}, u32[]{:S(2)}) collective-permute-start(bf16[2,4,3,1,48,768]{5,4,3,2,1,0:T(8,128)(2,1)} %pad_maximum_fusion.1.near), channel_id=1, source_target_pairs={{0,4},{4,0},{8,12},{12,8},{16,20},{20,16},{24,28},{28,24},{1,5},{5... | collective-permute-start | bytes 5308424 | tf_op jit(solution)/shard_map/ppermute | solution.py:44
  192.9 16.7 %collective-permute-start.34 = (bf16[2,192,197]{2,1,0:T(8,128)(2,1)S(1)}, bf16[2,192,197]{2,1,0:T(8,128)(2,1)S(1)}, u32[]{:S(2)}, u32[]{:S(2)}) collective-permute-start(bf16[2,192,197]{2,1,0:T(8,128)(2,1)S(1)} %get-tuple-element.209), channel_id=1, source_target_pairs={{0,2},{1,3},{2,0},{3,1},{4,6},{5,7},{6,4},{7,5},{8,10},{9,11},{10,... | collective-permute-start | bytes 453896 | tf_op jit(solution)/shard_map/ppermute | solution.py:39
  235.6 19.8 %collective-permute-start.49 = (bf16[2,2,4,2,96,768]{5,4,3,2,1,0:T(8,128)(2,1)}, bf16[2,2,4,2,96,768]{5,4,3,2,1,0:T(8,128)(2,1)}, u32[]{:S(2)}, u32[]{:S(2)}) collective-permute-start(bf16[2,2,4,2,96,768]{5,4,3,2,1,0:T(8,128)(2,1)} %get-tuple-element.160), channel_id=1, source_target_pairs={{0,4},{4,0},{8,12},{12,8},{16,20},{20,16},{24,28},{28,24},{1,5},{5... | collective-permute-start | bytes 14155784 | tf_op jit(solution)/shard_map/ppermute | solution.py:44
  264.4 38.4 %collective-permute-start.59 = (bf16[2,2,4,1,112,768]{5,4,2,3,1,0:T(8,128)(2,1)}, bf16[2,2,4,1,112,768]{5,4,2,3,1,0:T(8,128)(2,1)S(1)}, u32[]{:S(2)}, u32[]{:S(2)}) collective-permute-start(bf16[2,2,4,1,112,768]{5,4,2,3,1,0:T(8,128)(2,1)} %bitcast.246), channel_id=1, source_target_pairs={{0,4},{4,0},{8,12},{12,8},{16,20},{20,16},{24,28},{28,24},{1,5},{5... | collective-permute-start | bytes 8257544 | tf_op jit(solution)/shard_map/ppermute | solution.py:44
  268.9 28.0 %collective-permute-start.52 = (bf16[2,4,2,48,768]{4,3,2,1,0:T(8,128)(2,1)S(1)}, bf16[2,4,2,48,768]{4,3,2,1,0:T(8,128)(2,1)S(1)}, u32[]{:S(2)}, u32[]{:S(2)}) collective-permute-start(bf16[2,4,2,48,768]{4,3,2,1,0:T(8,128)(2,1)S(1)} %fusion.1), channel_id=1, source_target_pairs={{0,16},{4,20},{8,24},{12,28},{16,0},{20,4},{24,8},{28,12},{1,17},{... | collective-permute-start | bytes 3538952 | tf_op jit(solution)/shard_map/ppermute | solution.py:44
  270.1 27.6 %collective-permute-start.50 = (bf16[2,4,2,48,768]{4,3,2,1,0:T(8,128)(2,1)S(1)}, bf16[2,4,2,48,768]{4,3,2,1,0:T(8,128)(2,1)S(1)}, u32[]{:S(2)}, u32[]{:S(2)}) collective-permute-start(bf16[2,4,2,48,768]{4,3,2,1,0:T(8,128)(2,1)S(1)} %fusion), channel_id=1, source_target_pairs={{0,8},{4,12},{8,0},{12,4},{16,24},{20,28},{24,16},{28,20},{1,9},{5... | collective-permute-start | bytes 3538952 | tf_op jit(solution)/shard_map/ppermute | solution.py:44
  300.3 16.3 %collective-permute-start.51 = (bf16[4,2,48,768]{3,2,1,0:T(8,128)(2,1)S(1)}, bf16[4,2,48,768]{3,2,1,0:T(8,128)(2,1)S(1)}, u32[]{:S(2)}, u32[]{:S(2)}) collective-permute-start(bf16[4,2,48,768]{3,2,1,0:T(8,128)(2,1)S(1)} %get-tuple-element.181), channel_id=1, source_target_pairs={{0,16},{4,20},{8,24},{12,28},{16,0},{20,4},{24,8},{28,12},{1,17},{... | collective-permute-start | bytes 1769480 | tf_op jit(solution)/shard_map/ppermute | solution.py:44
  301.3 16.2 %collective-permute-start.53 = (bf16[4,2,48,768]{3,2,1,0:T(8,128)(2,1)S(1)}, bf16[4,2,48,768]{3,2,1,0:T(8,128)(2,1)S(1)}, u32[]{:S(2)}, u32[]{:S(2)}) collective-permute-start(bf16[4,2,48,768]{3,2,1,0:T(8,128)(2,1)S(1)} %get-tuple-element.186), channel_id=1, source_target_pairs={{0,8},{4,12},{8,0},{12,4},{16,24},{20,28},{24,16},{28,20},{1,9},{5... | collective-permute-start | bytes 1769480 | tf_op jit(solution)/shard_map/ppermute | solution.py:44
  302.9 26.9 %collective-permute-start.60 = (bf16[2,4,1,56,768]{4,3,1,2,0:T(8,128)(2,1)S(1)}, bf16[2,4,1,56,768]{4,3,1,2,0:T(8,128)(2,1)S(1)}, u32[]{:S(2)}, u32[]{:S(2)}) collective-permute-start(bf16[2,4,1,56,768]{4,3,1,2,0:T(8,128)(2,1)S(1)} %fusion.4), channel_id=1, source_target_pairs={{0,8},{4,12},{8,0},{12,4},{16,24},{20,28},{24,16},{28,20},{1,9},{5... | collective-permute-start | bytes 2064392 | tf_op jit(solution)/shard_map/ppermute | solution.py:44
  303.7 26.2 %collective-permute-start.62 = (bf16[2,4,1,56,768]{4,3,1,2,0:T(8,128)(2,1)S(1)}, bf16[2,4,1,56,768]{4,3,1,2,0:T(8,128)(2,1)S(1)}, u32[]{:S(2)}, u32[]{:S(2)}) collective-permute-start(bf16[2,4,1,56,768]{4,3,1,2,0:T(8,128)(2,1)S(1)} %fusion.5), channel_id=1, source_target_pairs={{0,16},{4,20},{8,24},{12,28},{16,0},{20,4},{24,8},{28,12},{1,17},{... | collective-permute-start | bytes 2064392 | tf_op jit(solution)/shard_map/ppermute | solution.py:44
  317.6 25.0 %collective-permute-start.55 = (bf16[192,768]{1,0:T(8,128)(2,1)S(1)}, bf16[192,768]{1,0:T(8,128)(2,1)S(1)}, u32[]{:S(2)}, u32[]{:S(2)}) collective-permute-start(bf16[192,768]{1,0:T(8,128)(2,1)S(1)} %bitcast.244), channel_id=1, source_target_pairs={{0,2},{1,3},{2,0},{3,1},{4,6},{5,7},{6,4},{7,5},{8,10},{9,11},{10,... | collective-permute-start | bytes 884744 | tf_op jit(solution)/shard_map/ppermute | solution.py:39
  317.8 25.3 %collective-permute-start.56 = (bf16[192,768]{1,0:T(8,128)(2,1)S(1)}, bf16[192,768]{1,0:T(8,128)(2,1)S(1)}, u32[]{:S(2)}, u32[]{:S(2)}) collective-permute-start(bf16[192,768]{1,0:T(8,128)(2,1)S(1)} %bitcast.243), channel_id=1, source_target_pairs={{0,1},{1,2},{2,3},{3,0},{4,5},{5,6},{6,7},{7,4},{8,9},{9,10},{10,1... | collective-permute-start | bytes 884744 | tf_op jit(solution)/shard_map/ppermute | solution.py:39
  321.4 21.7 %collective-permute-start.54 = (bf16[192,768]{1,0:T(8,128)(2,1)S(1)}, bf16[192,768]{1,0:T(8,128)(2,1)S(1)}, u32[]{:S(2)}, u32[]{:S(2)}) collective-permute-start(bf16[192,768]{1,0:T(8,128)(2,1)S(1)} %bitcast.245), channel_id=1, source_target_pairs={{0,3},{1,0},{2,1},{3,2},{4,7},{5,4},{6,5},{7,6},{8,11},{9,8},{10,9... | collective-permute-start | bytes 884744 | tf_op jit(solution)/shard_map/ppermute | solution.py:39
  339.0 14.5 %collective-permute-start.65 = (bf16[112,768]{1,0:T(8,128)(2,1)S(1)}, bf16[112,768]{1,0:T(8,128)(2,1)S(1)}, u32[]{:S(2)}, u32[]{:S(2)}) collective-permute-start(bf16[112,768]{1,0:T(8,128)(2,1)S(1)} %maximum_bitcast_fusion.6), channel_id=1, source_target_pairs={{0,2},{1,3},{2,0},{3,1},{4,6},{5,7},{6,4},{7,5},{8,10},{9,11},{10,... | collective-permute-start | bytes 516104 | tf_op jit(solution)/shard_map/ppermute | solution.py:39
  339.1 14.4 %collective-permute-start.66 = (bf16[112,768]{1,0:T(8,128)(2,1)S(1)}, bf16[112,768]{1,0:T(8,128)(2,1)S(1)}, u32[]{:S(2)}, u32[]{:S(2)}) collective-permute-start(bf16[112,768]{1,0:T(8,128)(2,1)S(1)} %maximum_bitcast_fusion.7), channel_id=1, source_target_pairs={{0,1},{1,2},{2,3},{3,0},{4,5},{5,6},{6,7},{7,4},{8,9},{9,10},{10,1... | collective-permute-start | bytes 516104 | tf_op jit(solution)/shard_map/ppermute | solution.py:39
  373.1 63.1 %collective-permute-start.69 = (bf16[4,304,768]{2,1,0:T(8,128)(2,1)S(1)}, bf16[4,304,768]{2,1,0:T(8,128)(2,1)}, u32[]{:S(2)}, u32[]{:S(2)}) collective-permute-start(bf16[4,304,768]{2,1,0:T(8,128)(2,1)S(1)} %maximum_maximum_fusion.near), channel_id=1, source_target_pairs={{0,4},{4,0},{8,12},{12,8},{16,20},{20,16},{24,28},{28,24},{1,5},{5... | collective-permute-start | bytes 5603336 | tf_op jit(solution)/shard_map/ppermute | solution.py:44
  388.6 13.8 %collective-permute-start.23 = (bf16[2,192,197]{2,1,0:T(8,128)(2,1)S(1)}, bf16[2,192,197]{2,1,0:T(8,128)(2,1)S(1)}, u32[]{:S(2)}, u32[]{:S(2)}) collective-permute-start(bf16[2,192,197]{2,1,0:T(8,128)(2,1)S(1)} %copy-done.35), channel_id=1, source_target_pairs={{0,1},{1,2},{2,3},{3,0},{4,5},{5,6},{6,7},{7,4},{8,9},{9,10},{10,1... | collective-permute-start | bytes 453896 | tf_op jit(solution)/shard_map/ppermute | solution.py:39
  388.7 16.8 %collective-permute-start.24 = (bf16[2,192,197]{2,1,0:T(8,128)(2,1)S(1)}, bf16[2,192,197]{2,1,0:T(8,128)(2,1)S(1)}, u32[]{:S(2)}, u32[]{:S(2)}) collective-permute-start(bf16[2,192,197]{2,1,0:T(8,128)(2,1)S(1)} %copy-done.34), channel_id=1, source_target_pairs={{0,2},{1,3},{2,0},{3,1},{4,6},{5,7},{6,4},{7,5},{8,10},{9,11},{10,... | collective-permute-start | bytes 453896 | tf_op jit(solution)/shard_map/ppermute | solution.py:39
  391.6 18.9 %collective-permute-start.25 = (bf16[2,192,197]{2,1,0:T(8,128)(2,1)S(1)}, bf16[2,192,197]{2,1,0:T(8,128)(2,1)S(1)}, u32[]{:S(2)}, u32[]{:S(2)}) collective-permute-start(bf16[2,192,197]{2,1,0:T(8,128)(2,1)S(1)} %copy-done.33), channel_id=1, source_target_pairs={{0,3},{1,0},{2,1},{3,2},{4,7},{5,4},{6,5},{7,6},{8,11},{9,8},{10,9... | collective-permute-start | bytes 453896 | tf_op jit(solution)/shard_map/ppermute | solution.py:39
  402.5 19.9 %collective-permute-start.47 = (bf16[64,768]{1,0:T(8,128)(2,1)}, bf16[64,768]{1,0:T(8,128)(2,1)S(1)}, u32[]{:S(2)}, u32[]{:S(2)}) collective-permute-start(bf16[64,768]{1,0:T(8,128)(2,1)} %get-tuple-element.146), channel_id=1, source_target_pairs={{0,2},{1,3},{2,0},{3,1},{4,6},{5,7},{6,4},{7,5},{8,10},{9,11},{10,... | collective-permute-start | bytes 294920 | tf_op jit(solution)/shard_map/ppermute | solution.py:39
  405.4 27.2 %collective-permute-start.36 = (bf16[2,192,197]{2,1,0:T(8,128)(2,1)}, bf16[2,192,197]{2,1,0:T(8,128)(2,1)S(1)}, u32[]{:S(2)}, u32[]{:S(2)}) collective-permute-start(bf16[2,192,197]{2,1,0:T(8,128)(2,1)} %get-tuple-element.137), channel_id=1, source_target_pairs={{0,1},{1,2},{2,3},{3,0},{4,5},{5,6},{6,7},{7,4},{8,9},{9,10},{10,1... | collective-permute-start | bytes 453896 | tf_op jit(solution)/shard_map/ppermute | solution.py:39
  410.5 22.1 %collective-permute-start.37 = (bf16[2,192,197]{2,1,0:T(8,128)(2,1)}, bf16[2,192,197]{2,1,0:T(8,128)(2,1)S(1)}, u32[]{:S(2)}, u32[]{:S(2)}) collective-permute-start(bf16[2,192,197]{2,1,0:T(8,128)(2,1)} %get-tuple-element.138), channel_id=1, source_target_pairs={{0,2},{1,3},{2,0},{3,1},{4,6},{5,7},{6,4},{7,5},{8,10},{9,11},{10,... | collective-permute-start | bytes 453896 | tf_op jit(solution)/shard_map/ppermute | solution.py:39
  413.9 18.8 %collective-permute-start.38 = (bf16[2,192,197]{2,1,0:T(8,128)(2,1)S(1)}, bf16[2,192,197]{2,1,0:T(8,128)(2,1)S(1)}, u32[]{:S(2)}, u32[]{:S(2)}) collective-permute-start(bf16[2,192,197]{2,1,0:T(8,128)(2,1)S(1)} %copy-done.36), channel_id=1, source_target_pairs={{0,3},{1,0},{2,1},{3,2},{4,7},{5,4},{6,5},{7,6},{8,11},{9,8},{10,9... | collective-permute-start | bytes 453896 | tf_op jit(solution)/shard_map/ppermute | solution.py:39
  (79 other events, 714.2 us)
